TPU v7x, 32 devices: a whole 2x2x4 slice. The times are simulated.
32 devices in a mesh: fsdp: 16 (over z, y, core), tp: 2 (over x).
Axes of the slice: x: 2, y: 2, z: 4, core: 2. Of those that a mesh axis runs over, the one named last changes fastest.
Arguments:
- layer_input: bfloat16 [16, 512, 2048], P('fsdp', 'tp'), may hold values from -6 to 6
- attention_gain: float32 [2048], replicated, may hold values from 0.1 to 1.9
- query_gain: float32 [128], replicated, may hold values from 0.5 to 2
- key_gain: float32 [128], replicated, may hold values from 0.5 to 2
- query_weight: bfloat16 [2048, 4096], P('fsdp', 'tp'), may hold values from -0.125 to 0.125
- key_weight: bfloat16 [2048, 512], P('fsdp', 'tp'), may hold values from -0.125 to 0.125
- value_weight: bfloat16 [2048, 512], P('fsdp', 'tp'), may hold values from -0.125 to 0.125
- output_weight: bfloat16 [2048, 4096], P('fsdp', 'tp'), may hold values from -0.5 to 0.5
- router_weight: bfloat16 [2048, 32], P('fsdp'), may hold values from -0.125 to 0.125
- expert_gain: float32 [2048], replicated, may hold values from 0.1 to 1.9
- gate_weight: bfloat16 [32, 2048, 768], P('fsdp', None, 'tp'), may hold values from -0.125 to 0.125
- up_weight: bfloat16 [32, 2048, 768], P('fsdp', None, 'tp'), may hold values from -0.125 to 0.125
- down_weight: bfloat16 [32, 768, 2048], P('fsdp', 'tp'), may hold values from -0.625 to 0.625
- routes: int32 [16, 512, 8], P('fsdp'), may hold values from 0 to 31, all different within a row; in each aligned block of 512 rows (0 to 511, 512 to 1023, ..., all dimensions but the last counted through in order) at most 160 rows name the same one
- segments: int32 [16, 512], P('fsdp'), may hold values from 0 to 3, never falling along the last dimension, each value on 1 to 256 neighbouring positions
- cotangent: bfloat16 [16, 512, 2048], P('fsdp', 'tp'), may hold values from -6 to 6
Outputs:
- layer_output: bfloat16 [16, 512, 2048], P('fsdp', 'tp')
- input_grad: float32 [16, 512, 2048], P('fsdp', 'tp')
- attention_gain_grad: float32 [2048], P(('fsdp', 'tp'))
- query_gain_grad: float32 [128], P(('fsdp', 'tp'))
- key_gain_grad: float32 [128], P(('fsdp', 'tp'))
- query_grad: float32 [2048, 4096], P('fsdp', 'tp')
- key_grad: float32 [2048, 512], P('fsdp', 'tp')
- value_grad: float32 [2048, 512], P('fsdp', 'tp')
- output_grad: float32 [2048, 4096], P('fsdp', 'tp')
- router_grad: float32 [2048, 32], P(('fsdp', 'tp'))
- expert_gain_grad: float32 [2048], P(('fsdp', 'tp'))
- gate_grad: float32 [32, 2048, 768], P('fsdp', None, 'tp')
- up_grad: float32 [32, 2048, 768], P('fsdp', None, 'tp')
- down_grad: float32 [32, 768, 2048], P('fsdp', 'tp')
Inputs may be any that keep to these rules, and one draw needn't show every extreme that they name: `routes`: each token names 8 different experts. Among the tokens of one group of 1 row no expert is named more than 160 times, and in some group one expert is named exactly 160 times. `segments`: within a row the numbers never fall; each segment spans 1 to 256 positions and some segment spans exactly that many.
All inputs are finite; a program needn't handle non-finite values.
Results may differ from a plain program's by a relative error of at most 0.022.
Values may be sent and summed in bfloat16 or wider, within the bound.
No kernel may reach another device: no remote copies, remote signals or barrier semaphores. Data moves between devices by JAX's collectives and lax.ppermute only.
A program may use at most 448 MiB of HBM per device.

v0:
```python
import math

import jax
import jax.numpy as jnp
from jax import lax
from jax.sharding import PartitionSpec as P

EPSILON = 1e-06
ROPE_BASE = 1000000.0
NEGATIVE = -1e30


def inverse_rms(values):
    return lax.rsqrt(jnp.mean(values * values, axis=-1, keepdims=True) + EPSILON)


def norm_backward(grad_scaled, gain, normed, inverse):
    grad_normed = grad_scaled * gain
    return inverse * (grad_normed - normed * jnp.mean(grad_normed * normed, axis=-1, keepdims=True))


def rotary_tables(segment_ids, head_size):
    length = segment_ids.shape[1]
    starts = jnp.sum((segment_ids[:, None, :] < segment_ids[:, :, None]).astype(jnp.int32), axis=2)
    places = jnp.arange(length, dtype=jnp.int32)[None, :] - starts
    half_size = head_size // 2
    frequency = jnp.exp(
        jnp.arange(half_size, dtype=jnp.float32) * (-2.0 * math.log(ROPE_BASE) / head_size)
    )
    angles = places.astype(jnp.float32)[:, :, None] * frequency
    return (jnp.cos(angles), jnp.sin(angles))


def rotate(values, cosine_table, sine_table):
    half_size = values.shape[-1] // 2
    front_half = values[..., :half_size]
    back_half = values[..., half_size:]
    cosine = cosine_table[:, :, None, :]
    sine_part = sine_table[:, :, None, :]
    return jnp.concatenate(
        [front_half * cosine - back_half * sine_part, back_half * cosine + front_half * sine_part],
        axis=-1,
    )


def unrotate(grads, cosine_table, sine_table):
    half_size = grads.shape[-1] // 2
    front_half = grads[..., :half_size]
    back_half = grads[..., half_size:]
    cosine = cosine_table[:, :, None, :]
    sine_part = sine_table[:, :, None, :]
    return jnp.concatenate(
        [front_half * cosine + back_half * sine_part, back_half * cosine - front_half * sine_part],
        axis=-1,
    )


def segment_mask(segment_ids):
    length = segment_ids.shape[1]
    places = jnp.arange(length, dtype=jnp.int32)
    causal = places[None, :] <= places[:, None]
    return (segment_ids[:, :, None] == segment_ids[:, None, :]) & causal[None]


def project(activations, weight):
    row_count, length, model_width = activations.shape
    flat = activations.reshape(row_count * length, model_width)
    return jnp.dot(flat, weight, preferred_element_type=jnp.float32).reshape(
        row_count, length, weight.shape[1]
    )


def attend_row(operands):
    query_rot, key_rot, value_rows, allowed = operands
    factor = 1.0 / math.sqrt(query_rot.shape[-1])
    scores = (
        jnp.einsum("ingc,jnc->ngij", query_rot, key_rot, preferred_element_type=jnp.float32)
        * factor
    )
    scores = jnp.where(allowed[None, None], scores, NEGATIVE)
    row_max = jnp.max(scores, axis=-1, keepdims=True)
    log_total = row_max + jnp.log(jnp.sum(jnp.exp(scores - row_max), axis=-1, keepdims=True))
    attention_weights = jnp.exp(scores - log_total).astype(jnp.bfloat16)
    attended = jnp.einsum(
        "ngij,jnc->ingc", attention_weights, value_rows, preferred_element_type=jnp.float32
    ).astype(jnp.bfloat16)
    return (attended, log_total[..., 0])


def attend_back(operands):
    query_rot, key_rot, value_rows, allowed, log_total, attended, grad_out = operands
    factor = 1.0 / math.sqrt(query_rot.shape[-1])
    scores = (
        jnp.einsum("ingc,jnc->ngij", query_rot, key_rot, preferred_element_type=jnp.float32)
        * factor
    )
    scores = jnp.where(allowed[None, None], scores, NEGATIVE)
    attention_weights = jnp.exp(scores - log_total[..., None])
    grad_value = jnp.einsum(
        "ngij,ingc->jnc",
        attention_weights.astype(jnp.bfloat16),
        grad_out,
        preferred_element_type=jnp.float32,
    )
    grad_weights = jnp.einsum(
        "ingc,jnc->ngij", grad_out, value_rows, preferred_element_type=jnp.float32
    )
    row_delta = jnp.einsum("ingc,ingc->ngi", attended, grad_out, preferred_element_type=jnp.float32)
    grad_scores = (attention_weights * (grad_weights - row_delta[..., None]) * factor).astype(
        jnp.bfloat16
    )
    grad_query = jnp.einsum(
        "ngij,jnc->ingc", grad_scores, key_rot, preferred_element_type=jnp.float32
    )
    grad_key = jnp.einsum(
        "ngij,ingc->jnc", grad_scores, query_rot, preferred_element_type=jnp.float32
    )
    return (grad_query, grad_key, grad_value)


def local(
    layer_input,
    attention_gain,
    query_gain,
    key_gain,
    query_weight,
    key_weight,
    value_weight,
    output_weight,
    router_weight,
    expert_gain,
    gate_weight,
    up_weight,
    down_weight,
    routes,
    segments,
    cotangent,
):
    row_count, local_length, model_width = layer_input.shape
    length = segments.shape[1]
    head_size = query_gain.shape[0]
    expert_count = router_weight.shape[1]
    local_experts = gate_weight.shape[0]
    top_count = routes.shape[2]
    node_count = lax.axis_size("fsdp")
    capacity = max(2, row_count * length * top_count * 5 // (4 * expert_count))
    tokens = row_count * length
    assigned = tokens * top_count
    input_wide = layer_input.astype(jnp.float32)
    inverse_one = inverse_rms(input_wide)
    normed_one = input_wide * inverse_one
    normed_low = (normed_one * attention_gain).astype(jnp.bfloat16)
    query_full, key_full, value_full, output_full, router_full = (
        lax.all_gather(query_weight, "fsdp", axis=0, tiled=True),
        lax.all_gather(key_weight, "fsdp", axis=0, tiled=True),
        lax.all_gather(value_weight, "fsdp", axis=0, tiled=True),
        lax.all_gather(output_weight, "fsdp", axis=0, tiled=True),
        lax.all_gather(router_weight, "fsdp", axis=0, tiled=True),
    )
    normed_rows, cot_rows = (
        lax.all_gather(normed_low, "tp", axis=1, tiled=True),
        lax.all_gather(cotangent, "tp", axis=1, tiled=True),
    )
    kv_local = key_full.shape[1] // head_size
    group_size = query_full.shape[1] // key_full.shape[1]
    cosine_table, sine_table = rotary_tables(segments, head_size)
    allowed = segment_mask(segments)
    query_pre = project(normed_rows, query_full).reshape(
        row_count, length, kv_local * group_size, head_size
    )
    key_pre = project(normed_rows, key_full).reshape(row_count, length, kv_local, head_size)
    value_rows = (
        project(normed_rows, value_full)
        .astype(jnp.bfloat16)
        .reshape(row_count, length, kv_local, head_size)
    )
    inverse_query = inverse_rms(query_pre)
    normed_query = query_pre * inverse_query
    inverse_key = inverse_rms(key_pre)
    normed_key = key_pre * inverse_key
    query_rot = (
        rotate(normed_query * query_gain, cosine_table, sine_table)
        .astype(jnp.bfloat16)
        .reshape(row_count, length, kv_local, group_size, head_size)
    )
    key_rot = rotate(normed_key * key_gain, cosine_table, sine_table).astype(jnp.bfloat16)
    attended, log_total = lax.map(attend_row, (query_rot, key_rot, value_rows, allowed))
    attended_flat = attended.reshape(tokens, kv_local * group_size * head_size)
    projected = lax.dot_general(
        attended_flat, output_full, (((1,), (1,)), ((), ())), preferred_element_type=jnp.float32
    ).reshape(row_count, length, model_width)
    attention_local = lax.psum_scatter(projected, "tp", scatter_dimension=1, tiled=True)
    middle = input_wide + attention_local
    inverse_two = inverse_rms(middle)
    normed_two = middle * inverse_two
    expert_low = (normed_two * expert_gain).astype(jnp.bfloat16)
    expert_rows = lax.all_gather(expert_low, "tp", axis=1, tiled=True).reshape(tokens, model_width)
    logits = jnp.dot(expert_rows, router_full, preferred_element_type=jnp.float32)
    route_flat = routes.reshape(tokens, top_count)
    chosen_mask = route_flat[:, :, None] == jnp.arange(expert_count, dtype=jnp.int32)
    chosen = jnp.sum(jnp.where(chosen_mask, logits[:, None, :], 0.0), axis=-1)
    gate_probs = jax.nn.softmax(chosen, axis=-1)
    route_list = route_flat.reshape(assigned)
    member = (route_list[:, None] == jnp.arange(expert_count, dtype=jnp.int32)).astype(jnp.int32)
    slot_index = jnp.sum((jnp.cumsum(member, axis=0) - member) * member, axis=1)
    destination = route_list * capacity + slot_index
    owner_index = (
        jnp.full((expert_count * capacity,), assigned, jnp.int32)
        .at[destination]
        .set(jnp.arange(assigned, dtype=jnp.int32))
    )
    padded_rows = jnp.concatenate([expert_rows, jnp.zeros((1, model_width), jnp.bfloat16)], axis=0)
    outgoing = padded_rows[owner_index // top_count].reshape(
        node_count, local_experts, capacity, model_width
    )
    arrived = lax.all_to_all(outgoing, "fsdp", split_axis=0, concat_axis=0, tiled=True)
    gate_pre = jnp.einsum(
        "secd,edf->secf", arrived, gate_weight, preferred_element_type=jnp.float32
    )
    up_pre = jnp.einsum("secd,edf->secf", arrived, up_weight, preferred_element_type=jnp.float32)
    hidden = (jax.nn.silu(gate_pre) * up_pre).astype(jnp.bfloat16)
    produced = jnp.einsum(
        "secf,efd->secd", hidden, down_weight, preferred_element_type=jnp.float32
    ).astype(jnp.bfloat16)
    returned = lax.all_to_all(produced, "fsdp", split_axis=0, concat_axis=0, tiled=True)
    results = (returned, gate_pre, up_pre)
    returned = results[0]
    gate_pre = results[1]
    up_pre = results[2]
    picked = returned.reshape(expert_count * capacity, model_width)[destination].reshape(
        tokens, top_count, model_width
    )
    expert_part = jnp.sum(gate_probs[:, :, None] * picked, axis=1)
    expert_local = lax.psum_scatter(
        expert_part.reshape(row_count, length, model_width).astype(jnp.bfloat16),
        "tp",
        scatter_dimension=1,
        tiled=True,
    ).astype(jnp.float32)
    layer_output = (middle + expert_local).astype(jnp.bfloat16)
    cot_flat = cot_rows.reshape(tokens, model_width)
    grad_gate = jnp.einsum("tkd,td->tk", picked, cot_flat, preferred_element_type=jnp.float32)
    scaled = (
        (gate_probs[:, :, None] * cot_flat[:, None, :])
        .astype(jnp.bfloat16)
        .reshape(assigned, model_width)
    )
    padded_scaled = jnp.concatenate([scaled, jnp.zeros((1, model_width), jnp.bfloat16)], axis=0)
    grad_outgoing = padded_scaled[owner_index].reshape(
        node_count, local_experts, capacity, model_width
    )
    arrived_back = (
        lax.all_to_all(grad_outgoing, "fsdp", split_axis=0, concat_axis=0, tiled=True),
        lax.all_to_all(outgoing, "fsdp", split_axis=0, concat_axis=0, tiled=True),
    )
    grad_arrived = arrived_back[0]
    rows_arrived = arrived_back[1]
    activated = jax.nn.silu(gate_pre)
    hidden = (activated * up_pre).astype(jnp.bfloat16)
    grad_hidden = jnp.einsum(
        "secd,efd->secf", grad_arrived, down_weight, preferred_element_type=jnp.float32
    )
    sigmoid_gate = jax.nn.sigmoid(gate_pre)
    grad_gate_pre = (
        grad_hidden * up_pre * sigmoid_gate * (1.0 + gate_pre * (1.0 - sigmoid_gate))
    ).astype(jnp.bfloat16)
    grad_up_pre = (grad_hidden * activated).astype(jnp.bfloat16)
    down_grad = jnp.einsum(
        "secf,secd->efd", hidden, grad_arrived, preferred_element_type=jnp.float32
    )
    gate_grad = jnp.einsum(
        "secd,secf->edf", rows_arrived, grad_gate_pre, preferred_element_type=jnp.float32
    )
    up_grad = jnp.einsum(
        "secd,secf->edf", rows_arrived, grad_up_pre, preferred_element_type=jnp.float32
    )
    grad_places = (
        jnp.einsum("secf,edf->secd", grad_gate_pre, gate_weight, preferred_element_type=jnp.float32)
        + jnp.einsum("secf,edf->secd", grad_up_pre, up_weight, preferred_element_type=jnp.float32)
    ).astype(jnp.bfloat16)
    grad_back = lax.all_to_all(grad_places, "fsdp", split_axis=0, concat_axis=0, tiled=True)
    grad_picked = grad_back.reshape(expert_count * capacity, model_width)[destination].reshape(
        tokens, top_count, model_width
    )
    grad_expert = jnp.sum(grad_picked, axis=1, dtype=jnp.float32)
    grad_chosen = gate_probs * (grad_gate - jnp.sum(gate_probs * grad_gate, axis=-1, keepdims=True))
    grad_logits = jnp.sum(jnp.where(chosen_mask, grad_chosen[:, :, None], 0.0), axis=1).astype(
        jnp.bfloat16
    )
    router_part = jnp.dot(expert_rows.T, grad_logits, preferred_element_type=jnp.float32)
    grad_expert = grad_expert + jnp.dot(
        grad_logits, router_full.T, preferred_element_type=jnp.float32
    )
    grad_two = lax.psum_scatter(
        grad_expert.reshape(row_count, length, model_width), "tp", scatter_dimension=1, tiled=True
    )
    expert_gain_part = jnp.sum(grad_two * normed_two, axis=(0, 1))
    grad_middle = cotangent.astype(jnp.float32) + norm_backward(
        grad_two, expert_gain, normed_two, inverse_two
    )
    grad_low = lax.all_gather(grad_middle.astype(jnp.bfloat16), "tp", axis=1, tiled=True)
    grad_flat = grad_low.reshape(tokens, model_width)
    grad_attended = (
        jnp.dot(grad_flat, output_full, preferred_element_type=jnp.float32)
        .astype(jnp.bfloat16)
        .reshape(row_count, length, kv_local, group_size, head_size)
    )
    output_low = jnp.dot(grad_flat.T, attended_flat, preferred_element_type=jnp.float32).astype(
        jnp.bfloat16
    )
    grad_query_rot, grad_key_rot, grad_value = lax.map(
        attend_back, (query_rot, key_rot, value_rows, allowed, log_total, attended, grad_attended)
    )
    grad_query_norm = unrotate(
        grad_query_rot.reshape(row_count, length, kv_local * group_size, head_size),
        cosine_table,
        sine_table,
    )
    grad_key_norm = unrotate(grad_key_rot, cosine_table, sine_table)
    query_gain_part = jnp.sum(grad_query_norm * normed_query, axis=(0, 1, 2))
    key_gain_part = jnp.sum(grad_key_norm * normed_key, axis=(0, 1, 2))
    grad_query_pre = (
        norm_backward(grad_query_norm, query_gain, normed_query, inverse_query)
        .reshape(tokens, -1)
        .astype(jnp.bfloat16)
    )
    grad_key_pre = (
        norm_backward(grad_key_norm, key_gain, normed_key, inverse_key)
        .reshape(tokens, -1)
        .astype(jnp.bfloat16)
    )
    grad_value_low = grad_value.reshape(tokens, -1).astype(jnp.bfloat16)
    normed_flat = normed_rows.reshape(tokens, model_width)
    query_low = jnp.dot(normed_flat.T, grad_query_pre, preferred_element_type=jnp.float32).astype(
        jnp.bfloat16
    )
    key_low = jnp.dot(normed_flat.T, grad_key_pre, preferred_element_type=jnp.float32).astype(
        jnp.bfloat16
    )
    value_low = jnp.dot(normed_flat.T, grad_value_low, preferred_element_type=jnp.float32).astype(
        jnp.bfloat16
    )
    grad_normed = (
        jnp.dot(grad_query_pre, query_full.T, preferred_element_type=jnp.float32)
        + jnp.dot(grad_key_pre, key_full.T, preferred_element_type=jnp.float32)
        + jnp.dot(grad_value_low, value_full.T, preferred_element_type=jnp.float32)
    ).reshape(row_count, length, model_width)
    grad_one = lax.psum_scatter(
        grad_normed.astype(jnp.bfloat16), "tp", scatter_dimension=1, tiled=True
    ).astype(jnp.float32)
    attention_gain_part = jnp.sum(grad_one * normed_one, axis=(0, 1))
    input_grad = grad_middle + norm_backward(grad_one, attention_gain, normed_one, inverse_one)
    query_grad, key_grad, value_grad, output_grad = (
        lax.psum_scatter(query_low.astype(jnp.float32), "fsdp", scatter_dimension=0, tiled=True),
        lax.psum_scatter(key_low.astype(jnp.float32), "fsdp", scatter_dimension=0, tiled=True),
        lax.psum_scatter(value_low.astype(jnp.float32), "fsdp", scatter_dimension=0, tiled=True),
        lax.psum_scatter(output_low.astype(jnp.float32), "fsdp", scatter_dimension=0, tiled=True),
    )
    router_grad, attention_gain_grad, expert_gain_grad, query_gain_grad, key_gain_grad = (
        lax.psum_scatter(router_part, ("fsdp", "tp"), scatter_dimension=0, tiled=True),
        lax.psum_scatter(attention_gain_part, ("fsdp", "tp"), scatter_dimension=0, tiled=True),
        lax.psum_scatter(expert_gain_part, ("fsdp", "tp"), scatter_dimension=0, tiled=True),
        lax.psum_scatter(query_gain_part, ("fsdp", "tp"), scatter_dimension=0, tiled=True),
        lax.psum_scatter(key_gain_part, ("fsdp", "tp"), scatter_dimension=0, tiled=True),
    )
    return (
        layer_output,
        input_grad,
        attention_gain_grad,
        query_gain_grad,
        key_gain_grad,
        query_grad,
        key_grad,
        value_grad,
        output_grad,
        router_grad,
        expert_gain_grad,
        gate_grad,
        up_grad,
        down_grad,
    )


def solution(mesh):
    return jax.shard_map(
        local,
        mesh=mesh,
        in_specs=(
            P("fsdp", "tp", None),
            P(),
            P(),
            P(),
            P("fsdp", "tp"),
            P("fsdp", "tp"),
            P("fsdp", "tp"),
            P("fsdp", "tp"),
            P("fsdp", None),
            P(),
            P("fsdp", None, "tp"),
            P("fsdp", None, "tp"),
            P("fsdp", "tp", None),
            P("fsdp", None, None),
            P("fsdp", None),
            P("fsdp", "tp", None),
        ),
        out_specs=(
            P("fsdp", "tp", None),
            P("fsdp", "tp", None),
            P(("fsdp", "tp")),
            P(("fsdp", "tp")),
            P(("fsdp", "tp")),
            P("fsdp", "tp"),
            P("fsdp", "tp"),
            P("fsdp", "tp"),
            P("fsdp", "tp"),
            P(("fsdp", "tp"), None),
            P(("fsdp", "tp")),
            P("fsdp", None, "tp"),
            P("fsdp", None, "tp"),
            P("fsdp", "tp", None),
        ),
        check_vma=False,
    )
```

profile of v0, /device:TPU:0, one launch (start us, length us, event | category | flops | bytes accessed | tf_op | source)
XLA Modules:
  0.0 3400.6 jit_solution(7459134449120633202)
XLA Ops:
  17.1 33.7 all-gather.13.cloned.1.call-done
  50.8 34.2 %all-gather.9.cloned.1.call-done = bf16[1,512,2048]{2,1,0:T(8,128)(2,1)} async-done(((bf16[1,256,2048]{2,1,0:T(8,128)(2,1)}), bf16[1,512,2048]{2,1,0:T(8,128)(2,1)}) %all-gather.9.cloned.1.call-update) | async-done | bytes 2097168 | tf_op jit(solution)/shard_map/all_gather | solution.py:161
  95.5 29.6 all-gather.11.cloned.1.call-done
  128.4 72.0 %all-gather.15.cloned.1.call-done = bf16[2048,2048]{1,0:T(8,128)(2,1)} async-done(((bf16[128,2048]{1,0:T(8,128)(2,1)}), bf16[2048,2048]{1,0:T(8,128)(2,1)}) %all-gather.15.cloned.1.call-update) | async-done | bytes 8388624 | tf_op jit(solution)/shard_map/all_gather | solution.py:154
  250.0 25.3 all-gather.17.cloned.1.call-done
  287.0 52.0 %reduce-scatter.12.cloned.1.call-done = f32[1,256,2048]{2,1,0:T(8,128)} async-done(((f32[1,512,2048]{2,1,0:T(8,128)}), f32[1,256,2048]{2,1,0:T(8,128)}) %reduce-scatter.12.cloned.1.call-update) | async-done | bytes 2097168 | tf_op jit(solution)/shard_map/reduce_scatter | solution.py:192
  386.7 40.7 %gather_fusion = bf16[5120,2048]{1,0:T(8,128)(2,1)} fusion(bf16[513,2048]{1,0:T(8,128)(2,1)} %concatenate.66, s32[5120]{0:T(1024)S(1)} %get-tuple-element.103), kind=kCustom, calls=%fused_computation | custom fusion | bytes 41963520 | tf_op jit(solution)/shard_map/gather | solution.py:213
  427.4 458.4 %all_to_all.21 = bf16[16,2,160,2048]{3,2,1,0:T(8,128)(2,1)} all-to-all(bf16[16,2,160,2048]{3,2,1,0:T(8,128)(2,1)} %bitcast.334), channel_id=1, replica_groups=mesh['fsdp'=16,'tp'=2] {'fsdp'}, dimensions={0} | all-to-all | bytes 41943040 | tf_op jit(solution)/shard_map/all_to_all | solution.py:216
  903.0 20.3 fusion.21
  963.7 401.1 %all_gather.33 = bf16[2048,32]{0,1:T(8,128)(2,1)S(1)} all-gather(bf16[128,32]{0,1:T(8,128)(2,1)S(1)} %copy-done.78), channel_id=1, replica_groups=mesh['fsdp'=16,'tp'=2] {'fsdp'}, dimensions={0}, use_global_device_ids=true | all-gather | bytes 139264 | tf_op jit(solution)/shard_map/all_gather | solution.py:158
  1370.1 41.0 %gather_fusion.1 = bf16[4096,2048]{1,0:T(8,128)(2,1)} fusion(bf16[5120,2048]{1,0:T(8,128)(2,1)} %bitcast.33, s32[4096]{0:T(1024)S(1)} %broadcast_clamp_fusion), kind=kCustom, calls=%fused_computation.1 | custom fusion | bytes 33570816 | tf_op jit(solution)/shard_map/gather | solution.py:230
  1438.8 46.8 %gather_fusion.2 = bf16[5120,2048]{1,0:T(8,128)(2,1)} fusion(bf16[4097,2048]{1,0:T(8,128)(2,1)} %concatenate.67, s32[5120]{0:T(1024)S(1)} %copy-done.61), kind=kCustom, calls=%fused_computation.2 | custom fusion | bytes 41963520 | tf_op jit(solution)/shard_map/gather | solution.py:249
  1485.5 519.6 %all_to_all.22 = bf16[16,2,160,2048]{3,2,1,0:T(8,128)(2,1)} all-to-all(bf16[16,2,160,2048]{3,2,1,0:T(8,128)(2,1)} %bitcast.335), channel_id=1, replica_groups=mesh['fsdp'=16,'tp'=2] {'fsdp'}, dimensions={0} | all-to-all | bytes 41943040 | tf_op jit(solution)/shard_map/all_to_all | solution.py:253
  2005.1 20.7 fusion.20
  2025.8 21.6 fusion.48
  2047.4 24.3 fusion.1
  2095.5 369.4 %all-to-all-done.3 = bf16[16,2,160,2048]{3,2,1,0:T(8,128)(2,1)} async-done(((bf16[16,2,160,2048]{3,2,1,0:T(8,128)(2,1)}), bf16[16,2,160,2048]{3,2,1,0:T(8,128)(2,1)}, u32[]{:S(2)}, u32[]{:S(2)}) %all-to-all-start.3) | async-done | bytes 20971552 | tf_op jit(solution)/shard_map/all_to_all | solution.py:281
  2464.9 41.0 %gather_fusion.3 = bf16[4096,2048]{1,0:T(8,128)(2,1)} fusion(bf16[5120,2048]{1,0:T(8,128)(2,1)} %bitcast.44, s32[4096]{0:T(1024)S(1)} %copy-done.51), kind=kCustom, calls=%fused_computation.3 | custom fusion | bytes 33570816 | tf_op jit(solution)/shard_map/gather | solution.py:282
  2522.1 136.1 %reduce-scatter.16.cloned.1.call-done = f32[1,256,2048]{2,1,0:T(8,128)} async-done(((f32[1,512,2048]{2,1,0:T(8,128)}), f32[1,256,2048]{2,1,0:T(8,128)}) %reduce-scatter.16.cloned.1.call-update) | async-done | bytes 2097168 | tf_op jit(solution)/shard_map/reduce_scatter | solution.py:294
  2893.0 37.3 %all-reduce.6 = (f32[2048]{0:T(1024)S(1)}, f32[128]{0:T(128)S(1)}, f32[128]{0:T(128)S(1)}, f32[2048]{0:T(1024)S(1)}) all-reduce(f32[2048]{0:T(1024)S(1)} %get-tuple-element.59, f32[128]{0:T(128)S(1)} %bitcast_reduce_fusion, f32[128]{0:T(128)S(1)} %bitcast_reduce_fusion.1, ...), channel_id=6, replica_groups=mesh['fsdp'=16,'tp'=2] {'fsdp','tp'}, use_global_device_ids=true, to_apply=%region_27.28.clone | all-reduce | flops 4352 | bytes 34816
  2939.0 27.8 reduce-scatter.22.cloned.1.call-done
  2966.8 65.0 %reduce-scatter.24.cloned.1.call-done = f32[128,256]{1,0:T(8,128)} async-done(((f32[2048,256]{1,0:T(8,128)}), f32[128,256]{1,0:T(8,128)}) %reduce-scatter.24.cloned.1.call-update) | async-done | bytes 131088 | tf_op jit(solution)/shard_map/reduce_scatter | solution.py:356
  3031.8 180.8 %reduce-scatter.26.cloned.1.call-done = f32[128,2048]{1,0:T(8,128)} async-done(((f32[2048,2048]{1,0:T(8,128)}), f32[128,2048]{1,0:T(8,128)}) %reduce-scatter.26.cloned.1.call-update) | async-done | bytes 1048592 | tf_op jit(solution)/shard_map/reduce_scatter | solution.py:357
  3212.6 181.0 %reduce-scatter.20.cloned.1.call-done = f32[128,2048]{1,0:T(8,128)} async-done(((f32[2048,2048]{1,0:T(8,128)}), f32[128,2048]{1,0:T(8,128)}) %reduce-scatter.20.cloned.1.call-update) | async-done | bytes 1048592 | tf_op jit(solution)/shard_map/reduce_scatter | solution.py:354
  (342 shorter events, 505.4 us)
Async XLA Ops:
  7.2 916.1 %copy-start = (bf16[2,384,2048]{2,1,0:T(8,128)(2,1)S(1)}, bf16[2,384,2048]{2,1,0:T(8,128)(2,1)}, u32[]{:S(2)}) copy-start(bf16[2,384,2048]{2,1,0:T(8,128)(2,1)} %param.28) | copy-start | bytes 9437188
  7.2 43.6 %all-gather.13.cloned.1.call-start = ((), (), s32[]{:S(2)}) async-start(), calls=%async_computation.15 | async-start | bytes 1114112 | tf_op jit(solution)/shard_map/all_gather | solution.py:155
  7.9 77.1 %all-gather.9.cloned.1.call-start = ((), (), s32[]{:S(2)}) async-start(), calls=%async_computation.13 | async-start | bytes 3145728 | tf_op jit(solution)/shard_map/all_gather | solution.py:161
  12.8 112.3 %all-gather.11.cloned.1.call-start = ((), (), s32[]{:S(2)}) async-start(), calls=%async_computation.14 | async-start | bytes 1114112 | tf_op jit(solution)/shard_map/all_gather | solution.py:156
  13.5 186.9 %all-gather.15.cloned.1.call-start = ((), (), s32[]{:S(2)}) async-start(), calls=%async_computation.16 | async-start | bytes 8912896 | tf_op jit(solution)/shard_map/all_gather | solution.py:154
  14.1 261.2 %all-gather.17.cloned.1.call-start = ((), (), s32[]{:S(2)}) async-start(), calls=%async_computation.17 | async-start | bytes 8912896 | tf_op jit(solution)/shard_map/all_gather | solution.py:157
  14.7 324.3 %reduce-scatter.12.cloned.1.call-start = ((), (), s32[]{:S(2)}) async-start(), calls=%async_computation.18 | async-start | bytes 6291456 | tf_op jit(solution)/shard_map/reduce_scatter | solution.py:192
  285.9 97.6 %all-gather.19.cloned.1.call-start = ((), (), s32[]{:S(2)}) async-start(), calls=%async_computation.19 | async-start | bytes 3145728 | tf_op jit(solution)/shard_map/all_gather | solution.py:197
  427.4 458.4 %copy-start.30 = (bf16[2,2048,384]{2,1,0:T(8,128)(2,1)S(1)}, bf16[2,2048,384]{2,1,0:T(8,128)(2,1)}, u32[]{:S(2)}) copy-start(bf16[2,2048,384]{2,1,0:T(8,128)(2,1)} %param.26) | copy-start | bytes 9437188
  957.4 407.5 %copy-start.66 = (s32[4096,1]{0,1:T(1,128)S(1)}, s32[4096,1]{0,1:T(1,128)}, u32[]{:S(2)}) copy-start(s32[4096,1]{0,1:T(1,128)} %copy-done.65) | copy-start | bytes 49156
  957.4 412.7 %all-to-all-start.1 = ((bf16[16,2,160,2048]{3,2,1,0:T(8,128)(2,1)}), bf16[16,2,160,2048]{3,2,1,0:T(8,128)(2,1)}, u32[]{:S(2)}, u32[]{:S(2)}) async-start(bf16[16,2,160,2048]{3,2,1,0:T(8,128)(2,1)} %copy.111), calls=%async_computation.2 | async-start | bytes 41943040 | tf_op jit(solution)/shard_map/all_to_all | solution.py:225
  963.0 402.0 %all-gather.21.cloned.1.call-start = ((), (), s32[]{:S(2)}) async-start(), calls=%async_computation.21 | async-start | bytes 3145728 | tf_op jit(solution)/shard_map/all_gather | solution.py:162
  2089.4 375.6 %copy-start.51 = (s32[4096]{0:T(1024)S(1)}, s32[4096]{0:T(1024)}, u32[]{:S(2)}) copy-start(s32[4096]{0:T(1024)} %copy-done.50) | copy-start | bytes 49156
  2089.4 375.5 %all-to-all-start.3 = ((bf16[16,2,160,2048]{3,2,1,0:T(8,128)(2,1)}), bf16[16,2,160,2048]{3,2,1,0:T(8,128)(2,1)}, u32[]{:S(2)}, u32[]{:S(2)}) async-start(bf16[16,2,160,2048]{3,2,1,0:T(8,128)(2,1)} %copy.114), calls=%async_computation.5 | async-start | bytes 41943040 | tf_op jit(solution)/shard_map/all_to_all | solution.py:281
  2095.3 562.9 %reduce-scatter.16.cloned.1.call-start = ((), (), s32[]{:S(2)}) async-start(), calls=%async_computation.22 | async-start | bytes 6291456 | tf_op jit(solution)/shard_map/reduce_scatter | solution.py:294
  2522.0 174.6 %all-gather.23.cloned.1.call-start = ((), (), s32[]{:S(2)}) async-start(), calls=%async_computation.23 | async-start | bytes 3145728 | tf_op jit(solution)/shard_map/all_gather | solution.py:301
  2663.3 172.8 %reduce-scatter.28.cloned.1.call-start = ((), (), s32[]{:S(2)}) async-start(), calls=%async_computation.29 | async-start | bytes 1081344
  2686.0 204.9 %reduce-scatter.18.cloned.1.call-start = ((), (), s32[]{:S(2)}) async-start(), calls=%async_computation.24 | async-start | bytes 3145728 | tf_op jit(solution)/shard_map/reduce_scatter | solution.py:348
  2771.5 161.1 %reduce-scatter.14.cloned.1.call-start = ((), (), s32[]{:S(2)}) async-start(), calls=%async_computation.20 | async-start | bytes 3145728 | tf_op jit(solution)/shard_map/reduce_scatter | solution.py:234
  2788.1 178.8 %reduce-scatter.22.cloned.1.call-start = ((), (), s32[]{:S(2)}) async-start(), calls=%async_computation.26 | async-start | bytes 2228224 | tf_op jit(solution)/shard_map/reduce_scatter | solution.py:355
  2791.8 240.0 %reduce-scatter.24.cloned.1.call-start = ((), (), s32[]{:S(2)}) async-start(), calls=%async_computation.27 | async-start | bytes 2228224 | tf_op jit(solution)/shard_map/reduce_scatter | solution.py:356
  2793.9 418.7 %reduce-scatter.26.cloned.1.call-start = ((), (), s32[]{:S(2)}) async-start(), calls=%async_computation.28 | async-start | bytes 17825792 | tf_op jit(solution)/shard_map/reduce_scatter | solution.py:357
  2806.6 587.0 %reduce-scatter.20.cloned.1.call-start = ((), (), s32[]{:S(2)}) async-start(), calls=%async_computation.25 | async-start | bytes 17825792 | tf_op jit(solution)/shard_map/reduce_scatter | solution.py:354
  2932.6 461.1 %copy-start.1 = (bf16[2,384,2048]{2,1,0:T(8,128)(2,1)S(1)}, bf16[2,384,2048]{2,1,0:T(8,128)(2,1)}, u32[]{:S(2)}) copy-start(bf16[2,384,2048]{2,1,0:T(8,128)(2,1)} %param.28) | copy-start | bytes 9437188
  (83 other events, 1505.8 us)
Sparse Core Ops, SparseCore 0:
  10.2 40.5 all-gather.12
  52.9 32.0 all-gather.8
  87.2 37.8 all-gather.10
  127.1 73.2 all-gather.14
  202.4 72.8 all-gather.16
  286.0 52.9 reduce-scatter.11
  343.9 33.0 all-gather.18
  965.3 33.4 all-gather.20
  2522.2 135.9 reduce-scatter.15
  2663.5 33.0 all-gather.22
  2699.4 136.6 reduce-scatter.27
  2838.2 27.7 reduce-scatter.17
  2868.3 32.4 reduce-scatter.13
  2904.9 61.8 reduce-scatter.21
  2971.0 60.7 reduce-scatter.23
  3036.3 176.2 reduce-scatter.25
  3217.2 176.4 reduce-scatter.19
where the time goes:
time: 3410 us; the launch traced here: 3400 us
  blocking collectives  1420 us (42%)
  waiting for transfers between devices  1240 us (36%)
  local copies, waits for them, and re-layouts  292 us (9%)
  matrix products  291 us (9%)
  other arithmetic  133 us (4%)
    all_to_all x1, blocking collectives, local(): lax.all_to_all(grad_outgoing, 'fsdp', split_axis=0, concat_axis=0, tiled=...  520 us
    all_to_all x1, blocking collectives, local(): lax.all_to_all(outgoing, 'fsdp', split_axis=0, concat_axis=0, tiled=True)  458 us
    all_gather x1, blocking collectives, local(): lax.all_gather(router_weight, 'fsdp', axis=0, tiled=True)  401 us
    all_to_all x1, waiting for transfers between devices, local(): lax.all_to_all(grad_places, 'fsdp', split_axis=0, concat_axis=0, tiled=True)  369 us
    reduce_scatter x1, waiting for transfers between devices, local(): lax.psum_scatter(query_low.astype(jnp.float32), 'fsdp', scatter_dimension...  181 us
    reduce_scatter x1, waiting for transfers between devices, local(): lax.psum_scatter(output_low.astype(jnp.float32), 'fsdp', scatter_dimensio...  181 us
    reduce_scatter x1, waiting for transfers between devices, local(): lax.psum_scatter(grad_expert.reshape(row_count, length, model_width), 'tp...  136 us
    all_gather x1, waiting for transfers between devices, local(): lax.all_gather(query_weight, 'fsdp', axis=0, tiled=True)  72 us
  transfers between devices with their start and end apart: 19, of which 14 were waited for; matrix products, arithmetic and copies ran while one was open for 9% of the time, Pallas kernels for 0%

commit v1 on v0

v1 whole, which is shorter than its diff:
```python
import functools
import math

import jax
import jax.numpy as jnp
from jax import lax
from jax.experimental import pallas as pl
from jax.experimental.pallas import tpu as pltpu
from jax.sharding import PartitionSpec as P

EPSILON = 1e-06
ROPE_BASE = 1000000.0
NEGATIVE = -1e30
F32 = jnp.float32
BF16 = jnp.bfloat16


def inverse_rms(values):
    return lax.rsqrt(jnp.mean(values * values, axis=-1, keepdims=True) + EPSILON)


def norm_backward(grad_scaled, gain, normed, inverse):
    grad_normed = grad_scaled * gain
    return inverse * (grad_normed - normed * jnp.mean(grad_normed * normed, axis=-1, keepdims=True))


def mm(a, b, dims=((1,), (0,))):
    return lax.dot_general(a, b, (dims, ((), ())), preferred_element_type=F32)


def fetch_next(values, step):
    size = lax.axis_size("tp")
    return lax.ppermute(values, "tp", [(s, (s - step) % size) for s in range(size)])


def gather_tp(values, axis):
    size = lax.axis_size("tp")
    return jnp.concatenate([values] + [fetch_next(values, j) for j in range(1, size)], axis=axis)


def scatter_tp(pieces):
    size = lax.axis_size("tp")
    total = pieces[0].astype(F32)
    for j in range(1, size):
        moved = lax.ppermute(
            pieces[j].astype(BF16), "tp", [(s, (s + j) % size) for s in range(size)]
        )
        total = total + moved.astype(F32)
    return total


def turn(values, cosine, sine):
    return values * cosine + pltpu.roll(values, values.shape[-1] // 2, 1) * sine


def turn_back(values, cosine, sine):
    return values * cosine - pltpu.roll(values, values.shape[-1] // 2, 1) * sine


def normed_turned(pre, gain, cosine, sine):
    inverse = inverse_rms(pre)
    normed = pre * inverse
    return inverse, normed, turn(normed * gain, cosine, sine).astype(BF16)


def weights_of(query_rot, key_rot, bias):
    factor = 1.0 / math.sqrt(query_rot.shape[-1])
    scores = mm(query_rot, key_rot, ((1,), (1,))) * factor + bias
    powers = jnp.exp(scores - jnp.max(scores, axis=-1, keepdims=True))
    return powers * (1.0 / jnp.sum(powers, axis=-1, keepdims=True))


def attend_kernel(q_ref, k_ref, v_ref, cos_ref, sin_ref, bias_ref, qg_ref, kg_ref, out_ref, key_rot):
    cosine, sine = cos_ref[...], sin_ref[...]

    @pl.when(pl.program_id(2) == 0)
    def _():
        key_rot[...] = normed_turned(k_ref[...], kg_ref[...], cosine, sine)[2]

    query_rot = normed_turned(q_ref[...], qg_ref[...], cosine, sine)[2]
    weights = weights_of(query_rot, key_rot[...], bias_ref[...])
    out_ref[...] = mm(weights.astype(BF16), v_ref[...].astype(BF16)).astype(BF16)


def attend_back_kernel(
    q_ref, k_ref, v_ref, cos_ref, sin_ref, bias_ref, qg_ref, kg_ref, att_ref, go_ref,
    grad_ref, qgain_ref, kgain_ref, key_rot, key_normed, key_inverse, grad_key, grad_value,
):
    row, kv, step = pl.program_id(0), pl.program_id(1), pl.program_id(2)
    group_size = pl.num_programs(2) - 2
    cosine, sine = cos_ref[...], sin_ref[...]
    factor = 1.0 / math.sqrt(q_ref.shape[-1])

    @pl.when((row == 0) & (kv == 0) & (step == 0))
    def _():
        qgain_ref[...] = jnp.zeros_like(qgain_ref)
        kgain_ref[...] = jnp.zeros_like(kgain_ref)

    @pl.when(step == 0)
    def _():
        inverse, normed, rotated = normed_turned(k_ref[...], kg_ref[...], cosine, sine)
        key_rot[...] = rotated
        key_normed[...] = normed
        key_inverse[...] = jnp.broadcast_to(inverse, key_inverse.shape)
        grad_key[...] = jnp.zeros_like(grad_key)
        grad_value[...] = jnp.zeros_like(grad_value)

    @pl.when(step < group_size)
    def _():
        inverse, normed, query_rot = normed_turned(q_ref[...], qg_ref[...], cosine, sine)
        weights = weights_of(query_rot, key_rot[...], bias_ref[...])
        grad_out = go_ref[...]
        grad_value[...] += mm(weights.astype(BF16), grad_out, ((0,), (0,)))
        grad_weights = mm(grad_out, v_ref[...].astype(BF16), ((1,), (1,)))
        delta = jnp.sum(att_ref[...].astype(F32) * grad_out.astype(F32), axis=-1, keepdims=True)
        grad_scores = (weights * (grad_weights - delta) * factor).astype(BF16)
        grad_query = turn_back(mm(grad_scores, key_rot[...]), cosine, sine)
        grad_key[...] += mm(grad_scores, query_rot, ((0,), (0,)))
        qgain_ref[...] += jnp.sum(grad_query * normed, axis=0, keepdims=True)
        grad_ref[...] = norm_backward(grad_query, qg_ref[...], normed, inverse).astype(BF16)

    @pl.when(step == group_size)
    def _():
        grad = turn_back(grad_key[...], cosine, sine)
        normed = key_normed[...]
        kgain_ref[...] += jnp.sum(grad * normed, axis=0, keepdims=True)
        grad_ref[...] = norm_backward(
            grad, kg_ref[...], normed, key_inverse[...][:, :1]
        ).astype(BF16)

    @pl.when(step == group_size + 1)
    def _():
        grad_ref[...] = grad_value[...].astype(BF16)


def attention_specs(length, head_size, heads, kv_heads):
    group_size = heads // kv_heads

    def head(r, kv, g):
        return (r, kv * group_size + jnp.minimum(g, group_size - 1))

    block = (length, head_size)
    full = pl.BlockSpec((1, head_size), lambda r, kv, g: (0, 0))
    return head, [
        pl.BlockSpec(block, head),
        pl.BlockSpec(block, lambda r, kv, g: (r, heads + kv)),
        pl.BlockSpec(block, lambda r, kv, g: (r, heads + kv_heads + kv)),
        pl.BlockSpec(block, lambda r, kv, g: (r, 0)),
        pl.BlockSpec(block, lambda r, kv, g: (r, 0)),
        pl.BlockSpec((None, length, length), lambda r, kv, g: (r, 0, 0)),
        full,
        full,
    ]


def attend(pre, tables, gains, rows, heads, kv_heads):
    length, head_size = pre.shape[0] // rows, gains[0].shape[1]
    head, specs = attention_specs(length, head_size, heads, kv_heads)
    cost = rows * heads * length * length
    return pl.pallas_call(
        attend_kernel,
        grid=(rows, kv_heads, heads // kv_heads),
        in_specs=specs,
        out_specs=pl.BlockSpec((length, head_size), head),
        out_shape=jax.ShapeDtypeStruct((pre.shape[0], heads * head_size), BF16),
        scratch_shapes=[pltpu.VMEM((length, head_size), BF16)],
        cost_estimate=pl.CostEstimate(
            flops=4 * cost * head_size, bytes_accessed=6 * pre.size, transcendentals=cost
        ),
        name="attend",
    )(pre, pre, pre, *tables, *gains)


def attend_back(pre, tables, gains, attended, grad_attended, rows, heads, kv_heads):
    length, head_size = pre.shape[0] // rows, gains[0].shape[1]
    group_size = heads // kv_heads
    head, specs = attention_specs(length, head_size, heads, kv_heads)

    def target(r, kv, g):
        own = kv * group_size + g
        return (r, jnp.where(g < group_size, own, heads + kv + jnp.where(g > group_size, kv_heads, 0)))

    block = pl.BlockSpec((length, head_size), head)
    full = pl.BlockSpec((1, head_size), lambda r, kv, g: (0, 0))
    gain = jax.ShapeDtypeStruct((1, head_size), F32)
    cost = rows * heads * length * length
    wide = pltpu.VMEM((length, head_size), F32)
    return pl.pallas_call(
        attend_back_kernel,
        grid=(rows, kv_heads, group_size + 2),
        in_specs=specs + [block, block],
        out_specs=[pl.BlockSpec((length, head_size), target), full, full],
        out_shape=[jax.ShapeDtypeStruct(pre.shape, BF16), gain, gain],
        scratch_shapes=[pltpu.VMEM((length, head_size), BF16), wide, wide, wide, wide],
        cost_estimate=pl.CostEstimate(
            flops=10 * cost * head_size, bytes_accessed=10 * pre.size, transcendentals=cost
        ),
        name="attend_back",
    )(pre, pre, pre, *tables, *gains, attended, grad_attended)


def local(
    layer_input,
    attention_gain,
    query_gain,
    key_gain,
    query_weight,
    key_weight,
    value_weight,
    output_weight,
    router_weight,
    expert_gain,
    gate_weight,
    up_weight,
    down_weight,
    routes,
    segments,
    cotangent,
):
    rows, local_length, model_width = layer_input.shape
    length = segments.shape[1]
    head_size = query_gain.shape[0]
    expert_count = router_weight.shape[1]
    local_experts, _, half_hidden = gate_weight.shape
    top_count = routes.shape[2]
    nodes = lax.axis_size("fsdp")
    tp_size = lax.axis_size("tp")
    node = lax.axis_index("fsdp")
    part = lax.axis_index("tp")
    heads = query_weight.shape[1] // head_size
    kv_heads = key_weight.shape[1] // head_size
    hidden_size = half_hidden * tp_size
    capacity = max(2, rows * length * top_count * 5 // (4 * expert_count))
    tokens = rows * local_length
    places = min(capacity, tokens)
    every = tp_size * tokens

    qkv_full = lax.all_gather(
        jnp.concatenate([query_weight, key_weight, value_weight], axis=1), "fsdp", axis=0, tiled=True
    )
    input_wide = layer_input.astype(F32)
    inverse_one = inverse_rms(input_wide)
    normed_one = input_wide * inverse_one
    normed_low = (normed_one * attention_gain).astype(BF16)
    normed_rows = gather_tp(normed_low, 1).reshape(every, model_width)
    output_full = lax.all_gather(output_weight, "fsdp", axis=0, tiled=True)
    router_full = lax.all_gather(router_weight, "fsdp", axis=0, tiled=True)

    places_in = jnp.concatenate(
        [
            ((part + j) % tp_size) * local_length + jnp.arange(local_length, dtype=jnp.int32)
            for j in range(tp_size)
        ]
    )
    doubled = jnp.concatenate([segments, segments], axis=1)
    ids = lax.dynamic_slice_in_dim(doubled, part * local_length, length, axis=1)
    starts = jnp.sum((segments[:, None, :] < ids[:, :, None]).astype(jnp.int32), axis=2)
    half_size = head_size // 2
    frequency = jnp.exp(jnp.arange(half_size, dtype=F32) * (-2.0 * math.log(ROPE_BASE) / head_size))
    angles = (places_in[None, :] - starts).astype(F32)[:, :, None] * frequency
    cosine, sine = jnp.cos(angles), jnp.sin(angles)
    cosine_table = jnp.concatenate([cosine, cosine], axis=-1).reshape(every, head_size)
    sine_table = jnp.concatenate([-sine, sine], axis=-1).reshape(every, head_size)
    allowed = (ids[:, :, None] == ids[:, None, :]) & (places_in[None, :] <= places_in[:, None])[None]
    tables = (cosine_table, sine_table, jnp.where(allowed, 0.0, NEGATIVE).astype(F32))
    gains = (query_gain.reshape(1, head_size), key_gain.reshape(1, head_size))

    gate_weight, up_weight, down_weight, normed_rows = lax.optimization_barrier(
        (gate_weight, up_weight, down_weight, normed_rows)
    )
    gate_full = gather_tp(gate_weight, 2)
    up_full = gather_tp(up_weight, 2)
    down_full = gather_tp(down_weight, 1)

    own_routes = lax.dynamic_slice_in_dim(routes, part * local_length, local_length, axis=1)
    own_routes = own_routes.reshape(tokens, top_count)
    all_routes = lax.all_gather(own_routes, "fsdp", axis=0).reshape(nodes, tokens, top_count)
    own_experts = node * local_experts + jnp.arange(local_experts, dtype=jnp.int32)
    member = jnp.any(all_routes[:, None, :, :] == own_experts[None, :, None, None], axis=-1)
    before = jnp.arange(tokens)[:, None] < jnp.arange(tokens)[None, :]
    slot = jnp.einsum(
        "get,tu->geu", member.astype(BF16), before.astype(BF16), preferred_element_type=F32
    ).astype(jnp.int32)
    slot = jnp.where(member, slot, -1)
    placed = slot[:, :, None, :] == jnp.arange(places, dtype=jnp.int32)[None, None, :, None]

    pre = mm(normed_rows, qkv_full)
    attended = attend(pre, tables, gains, rows, heads, kv_heads)
    projected = mm(attended, output_full, ((1,), (1,))).reshape(rows, tp_size, local_length, model_width)
    middle = input_wide + scatter_tp([projected[:, j] for j in range(tp_size)])
    inverse_two = inverse_rms(middle)
    normed_two = middle * inverse_two
    expert_low = (normed_two * expert_gain).astype(BF16).reshape(tokens, model_width)

    rows_all = lax.all_gather(expert_low, "fsdp", axis=0)
    logits = mm(expert_low, router_full)
    chosen = jnp.any(
        own_routes[:, :, None] == jnp.arange(expert_count, dtype=jnp.int32), axis=1
    )
    top = jnp.max(jnp.where(chosen, logits, NEGATIVE), axis=-1, keepdims=True)
    powers = jnp.where(chosen, jnp.exp(jnp.minimum(logits - top, 0.0)), 0.0)
    gates = powers / jnp.sum(powers, axis=-1, keepdims=True)
    gates_all = lax.all_gather(gates, "fsdp", axis=0)
    cot_low = cotangent.reshape(tokens, model_width)
    cot_all = lax.all_gather(cot_low, "fsdp", axis=0)
    own_gates = lax.dynamic_slice_in_dim(gates_all, node * local_experts, local_experts, axis=2)
    gate_of = jnp.sum(
        jnp.where(placed, jnp.moveaxis(own_gates, 2, 1)[:, :, None, :], 0.0), axis=-1
    )

    out_total = None
    grad_total = None
    gate_columns = []
    own_grads = []
    far_grads = []
    for e in range(local_experts):
        spread = placed[:, e].astype(BF16)
        gate_here = gate_of[:, e].reshape(nodes * places, 1)
        arrived = jnp.einsum("gst,gtd->gsd", spread, rows_all, preferred_element_type=F32)
        arrived = arrived.astype(BF16).reshape(nodes * places, model_width)
        gate_pre = mm(arrived, gate_full[e])
        up_pre = mm(arrived, up_full[e])
        cots = jnp.einsum("gst,gtd->gsd", spread, cot_all, preferred_element_type=F32)
        cots = cots.astype(BF16).reshape(nodes * places, model_width)
        grad_plain = mm(cots, down_full[e], ((1,), (1,)))
        sigmoid_gate = jax.nn.sigmoid(gate_pre)
        activated = gate_pre * sigmoid_gate
        hidden = activated * up_pre
        gate_columns.append(jnp.sum(hidden * grad_plain, axis=-1).reshape(nodes, places))
        grad_hidden = grad_plain * gate_here
        grad_gate_pre = (
            grad_hidden * up_pre * sigmoid_gate * (1.0 + gate_pre * (1.0 - sigmoid_gate))
        ).astype(BF16)
        grad_up_pre = (grad_hidden * activated).astype(BF16)
        weighed = (hidden * gate_here).astype(BF16)
        grad_places = (
            mm(grad_gate_pre, gate_full[e], ((1,), (1,))) + mm(grad_up_pre, up_full[e], ((1,), (1,)))
        ).astype(BF16).reshape(nodes, places, model_width)
        produced = mm(weighed, down_full[e]).astype(BF16).reshape(nodes, places, model_width)
        out_here = jnp.einsum("gst,gsd->gtd", spread, produced, preferred_element_type=F32)
        grad_here = jnp.einsum("gst,gsd->gtd", spread, grad_places, preferred_element_type=F32)
        if out_total is not None:
            out_here = out_here + out_total.astype(F32)
            grad_here = grad_here + grad_total.astype(F32)
        out_total = out_here.astype(BF16)
        grad_total = grad_here.astype(BF16)
        grads = (
            mm(arrived, grad_gate_pre, ((0,), (0,))),
            mm(arrived, grad_up_pre, ((0,), (0,))),
            mm(weighed, cots, ((0,), (0,))),
        )
        own_grads.append(
            (grads[0][:, :half_hidden], grads[1][:, :half_hidden], grads[2][:half_hidden])
        )
        far_grads.append(
            [
                (
                    grads[0][:, j * half_hidden : (j + 1) * half_hidden].astype(BF16),
                    grads[1][:, j * half_hidden : (j + 1) * half_hidden].astype(BF16),
                    grads[2][j * half_hidden : (j + 1) * half_hidden].astype(BF16),
                )
                for j in range(1, tp_size)
            ]
        )

    column = jnp.sum(
        jnp.where(placed, jnp.stack(gate_columns, axis=1)[:, :, :, None], 0.0), axis=2
    )
    column = jnp.moveaxis(column, 1, 2)
    grad_gate = lax.all_to_all(column, "fsdp", split_axis=0, concat_axis=0, tiled=True)
    grad_gate = jnp.moveaxis(grad_gate, 0, 1).reshape(tokens, expert_count)

    grad_rows = lax.psum_scatter(grad_total, "fsdp", scatter_dimension=0, tiled=True)
    expert_part = lax.psum_scatter(out_total, "fsdp", scatter_dimension=0, tiled=True)
    layer_output = (middle + expert_part.reshape(middle.shape).astype(F32)).astype(BF16)

    grad_logits = (
        gates * (grad_gate - jnp.sum(gates * grad_gate, axis=-1, keepdims=True))
    ).astype(BF16)
    router_part = mm(expert_low, grad_logits, ((0,), (0,)))
    grad_two = grad_rows.reshape(tokens, model_width).astype(F32) + mm(
        grad_logits, router_full, ((1,), (1,))
    )
    grad_two = grad_two.reshape(middle.shape)
    expert_gain_part = jnp.sum(grad_two * normed_two, axis=(0, 1))
    grad_middle = cotangent.astype(F32) + norm_backward(grad_two, expert_gain, normed_two, inverse_two)

    grad_flat = gather_tp(grad_middle.astype(BF16), 1).reshape(every, model_width)
    grad_attended = mm(grad_flat, output_full).astype(BF16)
    output_low = mm(grad_flat, attended, ((0,), (0,))).astype(BF16)
    output_grad = lax.psum_scatter(output_low, "fsdp", scatter_dimension=0, tiled=True).astype(F32)
    grad_pre, query_gain_part, key_gain_part = attend_back(
        pre, tables, gains, attended, grad_attended, rows, heads, kv_heads
    )
    qkv_low = mm(normed_rows, grad_pre, ((0,), (0,))).astype(BF16)
    qkv_grad = lax.psum_scatter(qkv_low, "fsdp", scatter_dimension=0, tiled=True).astype(F32)
    query_width, key_width = query_weight.shape[1], key_weight.shape[1]
    query_grad = qkv_grad[:, :query_width]
    key_grad = qkv_grad[:, query_width : query_width + key_width]
    value_grad = qkv_grad[:, query_width + key_width :]
    grad_normed = mm(grad_pre, qkv_full, ((1,), (1,))).reshape(rows, tp_size, local_length, model_width)
    grad_one = scatter_tp([grad_normed[:, j] for j in range(tp_size)])
    attention_gain_part = jnp.sum(grad_one * normed_one, axis=(0, 1))
    input_grad = grad_middle + norm_backward(grad_one, attention_gain, normed_one, inverse_one)

    weight_grads = []
    for kind in range(3):
        mine = jnp.stack([own_grads[e][kind] for e in range(local_experts)])
        far = [
            jnp.stack([far_grads[e][j][kind] for e in range(local_experts)])
            for j in range(tp_size - 1)
        ]
        weight_grads.append(scatter_tp([mine] + far))
    gate_grad, up_grad, down_grad = weight_grads

    router_grad = lax.psum_scatter(router_part, ("fsdp", "tp"), scatter_dimension=0, tiled=True)
    small = [
        lax.psum_scatter(value.reshape(-1), ("fsdp", "tp"), scatter_dimension=0, tiled=True)
        for value in (attention_gain_part, expert_gain_part, query_gain_part, key_gain_part)
    ]
    attention_gain_grad, expert_gain_grad, query_gain_grad, key_gain_grad = small
    return (
        layer_output,
        input_grad,
        attention_gain_grad,
        query_gain_grad,
        key_gain_grad,
        query_grad,
        key_grad,
        value_grad,
        output_grad,
        router_grad,
        expert_gain_grad,
        gate_grad,
        up_grad,
        down_grad,
    )


def solution(mesh):
    return jax.shard_map(
        local,
        mesh=mesh,
        in_specs=(
            P("fsdp", "tp", None),
            P(),
            P(),
            P(),
            P("fsdp", "tp"),
            P("fsdp", "tp"),
            P("fsdp", "tp"),
            P("fsdp", "tp"),
            P("fsdp", None),
            P(),
            P("fsdp", None, "tp"),
            P("fsdp", None, "tp"),
            P("fsdp", "tp", None),
            P("fsdp", None, None),
            P("fsdp", None),
            P("fsdp", "tp", None),
        ),
        out_specs=(
            P("fsdp", "tp", None),
            P("fsdp", "tp", None),
            P(("fsdp", "tp")),
            P(("fsdp", "tp")),
            P(("fsdp", "tp")),
            P("fsdp", "tp"),
            P("fsdp", "tp"),
            P("fsdp", "tp"),
            P("fsdp", "tp"),
            P(("fsdp", "tp"), None),
            P(("fsdp", "tp")),
            P("fsdp", None, "tp"),
            P("fsdp", None, "tp"),
            P("fsdp", "tp", None),
        ),
        check_vma=False,
    )
```

time: 3410 us -> 1450 us (0.43)
  blocking collectives: 1420 us -> 103 us
  waiting for transfers between devices: 1240 us -> 679 us
  local copies, waits for them, and re-layouts: 292 us -> 53.7 us
  matrix products: 291 us -> 424 us
  Pallas kernels: 0 us -> 69.9 us
  other arithmetic: 133 us -> 73.9 us
    all_to_all x2 -> x0, blocking collectives: 978 us -> none  [the longest x1 520 us: local(): lax.all_to_all(grad_outgoing, 'fsdp', split_axis=0, concat_axis=0, tiled=...]
    all_to_all x2 -> x1, waiting for transfers between devices: 369 us -> 0.01 us  [local(): lax.all_to_all(column, 'fsdp', split_axis=0, concat_axis=0, tiled=True)]
    reduce_scatter x8 -> x4, waiting for transfers between devices: 643 us -> 281 us  [the longest x1 121 us: local(): lax.psum_scatter(qkv_low, 'fsdp', scatter_dimension=0, tiled=True)]
    all_gather x1 -> x3, blocking collectives: 401 us -> 60.6 us  [the longest x1 21.2 us: local(): gates_all = lax.all_gather(gates, 'fsdp', axis=0)]
    ppermute x0 -> x10, waiting for transfers between devices: none -> 301 us  [the longest x5 197 us: fetch_next(): lax.ppermute(values, 'tp', [(s, (s - step) % size) for s in range(size)])]
    gather x4 -> x0, local copies, waits for them, and re-layouts: 169 us -> none  [the longest x1 46.8 us: local(): padded_scaled[owner_index]]
    dot_general x30 -> x35, matrix products: 290 us -> 423 us  [the longest x26 313 us: mm(): return lax.dot_general(a, b, (dims, ((), ())), preferred_element_type=F32)]
    all_gather x8 -> x4, waiting for transfers between devices: 205 us -> 95.2 us  [the longest x1 59.5 us: local(): lax.all_gather(jnp.concatenate([query_weight, key_weight, value_weight],...]
  transfers between devices with their start and end apart: 19 -> 20, of which waited for: 14 -> 14; matrix products, arithmetic and copies ran while one was open for 9% -> 21% of each run, Pallas kernels for 0% -> 5%
where the time goes in v1:
time: 1450 us; the launch traced here: 1440 us
  waiting for transfers between devices  679 us (47%)
  matrix products  424 us (29%)
  blocking collectives  103 us (7%)
  other arithmetic  73.9 us (5%)
  Pallas kernels  69.9 us (5%)
  local copies, waits for them, and re-layouts  53.7 us (4%)
  starting transfers between devices  19.2 us (1%)
  between operations  15 us (1%)
    dot_general x26, matrix products, mm(): return lax.dot_general(a, b, (dims, ((), ())), preferred_element_type=F32)  313 us
    ppermute x5, waiting for transfers between devices, fetch_next(): lax.ppermute(values, 'tp', [(s, (s - step) % size) for s in range(size)])  197 us
    reduce_scatter x1, waiting for transfers between devices, local(): lax.psum_scatter(qkv_low, 'fsdp', scatter_dimension=0, tiled=True)  121 us
    reduce_scatter x1, waiting for transfers between devices, local(): lax.psum_scatter(grad_total, 'fsdp', scatter_dimension=0, tiled=True)  110 us
    ppermute x5, waiting for transfers between devices, scatter_tp(): lax.ppermute(pieces[j].astype(BF16), 'tp', [(s, (s + j) % size) for s in...  105 us
    all_gather x1, waiting for transfers between devices, local(): lax.all_gather(jnp.concatenate([query_weight, key_weight, value_weight],...  59.5 us
    reduce_scatter x1, waiting for transfers between devices, local(): lax.psum_scatter(output_low, 'fsdp', scatter_dimension=0, tiled=True)  50 us
    unnamed x1, blocking collectives  42 us
  transfers between devices with their start and end apart: 20, of which 14 were waited for; matrix products, arithmetic and copies ran while one was open for 21% of the time, Pallas kernels for 5%

profile of v1, /device:TPU:0, one launch (start us, length us, event | category | flops | bytes accessed | tf_op | source)
XLA Modules:
  0.0 1438.1 jit_solution(15343486989197333194)
XLA Ops:
  21.2 19.0 %collective-permute-done = bf16[1,256,2048]{2,1,0:T(8,128)(2,1)S(1)} collective-permute-done((bf16[1,256,2048]{2,1,0:T(8,128)(2,1)S(1)}, bf16[1,256,2048]{2,1,0:T(8,128)(2,1)S(1)}, u32[]{:S(2)}, u32[]{:S(2)}) %collective-permute-start) | collective-permute-done | bytes 1048608 | tf_op jit(solution)/shard_map/ppermute | solution.py:33
  41.7 59.5 %all-gather.6.cloned.1.call-done = bf16[2048,2560]{1,0:T(8,128)(2,1)} async-done(((bf16[128,2560]{1,0:T(8,128)(2,1)}), bf16[2048,2560]{1,0:T(8,128)(2,1)}) %all-gather.6.cloned.1.call-update) | async-done | bytes 10485776 | tf_op jit(solution)/shard_map/all_gather | solution.py:238
  111.6 28.7 %attend.1.att_ref = bf16[512,2048]{1,0:T(8,128)(2,1)} custom-call(f32[512,2560]{1,0:T(8,128)} %fusion.55.q_ref.k_ref.v_ref, f32[512,2560]{1,0:T(8,128)} %fusion.55.q_ref.k_ref.v_ref, f32[512,2560]{1,0:T(8,128)} %fusion.55.q_ref.k_ref.v_ref, f32[512,128]{1,0:T(8,128)} %maximum_bitcast_fusion.4.cos_ref, f32[512,128]{1,0:T(8,128)} %maximum_bitcast_fusion.5.sin_ref, ...), custom_call_target="tpu_custom_call" | custom-call | flops 2147483648 | bytes 7864320 | tf_op jit(solution)/shard_map/attend/pallas_call | solution.py:160
  140.2 35.7 %all-gather.8.cloned.1.call-done = bf16[2048,2048]{1,0:T(8,128)(2,1)} async-done(((bf16[128,2048]{1,0:T(8,128)(2,1)}), bf16[2048,2048]{1,0:T(8,128)(2,1)}) %all-gather.8.cloned.1.call-update) | async-done | bytes 8388624 | tf_op jit(solution)/shard_map/all_gather | solution.py:246
  185.3 23.8 %collective-permute-done.1 = bf16[1,256,2048]{2,1,0:T(8,128)(2,1)S(1)} collective-permute-done((bf16[1,256,2048]{2,1,0:T(8,128)(2,1)S(1)}, bf16[1,256,2048]{2,1,0:T(8,128)(2,1)S(1)}, u32[]{:S(2)}, u32[]{:S(2)}) %collective-permute-start.1) | collective-permute-done | bytes 1048608 | tf_op jit(solution)/shard_map/ppermute | solution.py:45
  216.0 20.0 %all_gather.26 = s32[16,256,8]{1,2,0:T(8,128)S(1)} all-gather(s32[1,256,8]{1,2,0:T(8,128)S(1)} %constant_dynamic-slice_fusion), channel_id=1, replica_groups=mesh['fsdp'=16,'tp'=2] {'fsdp'}, dimensions={0}, use_global_device_ids=true | all-gather | bytes 139264 | tf_op jit(solution)/shard_map/all_gather | solution.py:277
  235.9 19.4 %all_gather.28 = bf16[2048,32]{0,1:T(8,128)(2,1)S(1)} all-gather(bf16[128,32]{0,1:T(8,128)(2,1)S(1)} %copy-done.51), channel_id=1, replica_groups=mesh['fsdp'=16,'tp'=2] {'fsdp'}, dimensions={0}, use_global_device_ids=true | all-gather | bytes 139264 | tf_op jit(solution)/shard_map/all_gather | solution.py:247
  262.5 21.2 %collective-permute-done.4 = bf16[2,384,2048]{2,1,0:T(8,128)(2,1)} collective-permute-done((bf16[2,384,2048]{2,1,0:T(8,128)(2,1)}, bf16[2,384,2048]{2,1,0:T(8,128)(2,1)}, u32[]{:S(2)}, u32[]{:S(2)}) %collective-permute-start.4) | collective-permute-done | bytes 3145760 | tf_op jit(solution)/shard_map/ppermute | solution.py:33
  285.8 65.3 %collective-permute-done.2 = bf16[2,2048,384]{2,1,0:T(8,128)(2,1)} collective-permute-done((bf16[2,2048,384]{2,1,0:T(8,128)(2,1)}, bf16[2,2048,384]{2,1,0:T(8,128)(2,1)}, u32[]{:S(2)}, u32[]{:S(2)}) %collective-permute-start.2) | collective-permute-done | bytes 3145760 | tf_op jit(solution)/shard_map/ppermute | solution.py:33
  353.7 63.3 %collective-permute-done.3 = bf16[2,2048,384]{2,1,0:T(8,128)(2,1)} collective-permute-done((bf16[2,2048,384]{2,1,0:T(8,128)(2,1)}, bf16[2,2048,384]{2,1,0:T(8,128)(2,1)}, u32[]{:S(2)}, u32[]{:S(2)}) %collective-permute-start.3) | collective-permute-done | bytes 3145760 | tf_op jit(solution)/shard_map/ppermute | solution.py:33
  420.2 21.2 %all-gather = f32[4096,32]{0,1:T(8,128)S(1)} all-gather(f32[256,32]{0,1:T(8,128)S(1)} %fusion.47), channel_id=2, replica_groups=mesh['fsdp'=16,'tp'=2] {'fsdp'}, dimensions={0}, use_global_device_ids=true | all-gather | bytes 557056 | tf_op jit(solution)/shard_map/all_gather | solution.py:303
  549.3 17.1 %multiply_reduce_fusion = (f32[2560]{0:T(1024)S(1)}, f32[2560,768]{0,1:T(8,128)}) fusion(f32[2560,768]{0,1:T(8,128)} %fusion.8, f32[2560,768]{0,1:T(8,128)} %fusion.6, bf16[2560,2048]{1,0:T(8,128)(2,1)} %bitcast.220, bf16[2,768,2048]{2,1,0:T(8,128)(2,1)S(1)} %bitcast.253), kind=kOutput, calls=%fused_computation.7 | convolution fusion | flops 8066823680 | bytes 37234688 | tf_op jit(solution)/shard_map/dot_general | solution.py:28
  566.4 18.7 %multiply_reduce_fusion.1 = (f32[2560]{0:T(1024)S(1)}, f32[2560,768]{0,1:T(8,128)}) fusion(f32[2560,768]{0,1:T(8,128)} %fusion.12, f32[2560,768]{0,1:T(8,128)} %fusion.10, bf16[2560,2048]{1,0:T(8,128)(2,1)} %bitcast.222, bf16[2,768,2048]{2,1,0:T(8,128)(2,1)} %copy-done.27), kind=kOutput, calls=%fused_computation.8 | convolution fusion | flops 8066823680 | bytes 37234688 | tf_op jit(solution)/shard_map/dot_general | solution.py:28
  642.4 16.7 %add_convert_fusion.2 = bf16[2560,2048]{1,0:T(8,128)(2,1)} fusion(f32[2560,2048]{1,0:T(8,128)} %fusion.11, bf16[2560,768]{0,1:T(8,128)(2,1)} %get-tuple-element.43, bf16[2,2048,768]{2,1,0:T(8,128)(2,1)} %copy-done.29), kind=kOutput, calls=%fused_computation.2 | convolution fusion | flops 8063549440 | bytes 38535168 | tf_op jit(solution)/shard_map/dot_general | solution.py:28
  671.3 17.0 %add_convert_fusion.3 = bf16[2560,2048]{1,0:T(8,128)(2,1)} fusion(f32[2560,2048]{1,0:T(8,128)} %fusion.7, bf16[2560,768]{0,1:T(8,128)(2,1)} %get-tuple-element.40, bf16[2,2048,768]{2,1,0:T(8,128)(2,1)} %copy-done.29), kind=kOutput, calls=%fused_computation.3 | convolution fusion | flops 8063549440 | bytes 38535168 | tf_op jit(solution)/shard_map/dot_general | solution.py:28
  688.4 16.5 %add_convert_fusion = bf16[16,256,2048]{2,1,0:T(8,128)(2,1)} fusion(bf16[16,256,2048]{2,1,0:T(8,128)(2,1)} %fusion.40, bf16[16,160,2048]{2,1,0:T(8,128)(2,1)} %bitcast.227, pred[16,2,160,256]{3,2,0,1:T(32,128)(4,1)S(1)} %copy-done.3), kind=kOutput, calls=%fused_computation | convolution fusion | flops 2709520384 | bytes 44695552 | tf_op jit(solution)/shard_map/gst,gsd->gtd/dot_general | solution.py:341
  752.5 16.9 %add_convert_fusion.1 = bf16[16,256,2048]{2,1,0:T(8,128)(2,1)} fusion(bf16[16,256,2048]{2,1,0:T(8,128)(2,1)} %fusion.41, bf16[16,160,2048]{2,1,0:T(8,128)(2,1)} %bitcast.226, pred[16,2,160,256]{3,2,0,1:T(32,128)(4,1)S(1)} %copy-done.3), kind=kOutput, calls=%fused_computation.1 | convolution fusion | flops 2709520384 | bytes 44695552 | tf_op jit(solution)/shard_map/gst,gsd->gtd/dot_general | solution.py:340
  769.5 110.2 %reduce-scatter.10.cloned.1.call-done = bf16[1,256,2048]{2,1,0:T(8,128)(2,1)} async-done(((bf16[16,256,2048]{2,1,0:T(8,128)(2,1)}), bf16[1,256,2048]{2,1,0:T(8,128)(2,1)}) %reduce-scatter.10.cloned.1.call-update) | async-done | bytes 1048592 | tf_op jit(solution)/shard_map/reduce_scatter | solution.py:373
  885.3 27.7 %collective-permute-done.5 = bf16[1,256,2048]{2,1,0:T(8,128)(2,1)S(1)} collective-permute-done((bf16[1,256,2048]{2,1,0:T(8,128)(2,1)S(1)}, bf16[1,256,2048]{2,1,0:T(8,128)(2,1)S(1)}, u32[]{:S(2)}, u32[]{:S(2)}) %collective-permute-start.5) | collective-permute-done | bytes 1048608 | tf_op jit(solution)/shard_map/ppermute | solution.py:33
  985.2 41.3 %attend_back.1 = (bf16[512,2560]{1,0:T(8,128)(2,1)}, f32[1,128]{1,0:T(1,128)}, f32[1,128]{1,0:T(1,128)}) custom-call(f32[512,2560]{1,0:T(8,128)} %fusion.55.q_ref.k_ref.v_ref, f32[512,2560]{1,0:T(8,128)} %fusion.55.q_ref.k_ref.v_ref, f32[512,2560]{1,0:T(8,128)} %fusion.55.q_ref.k_ref.v_ref, f32[512,128]{1,0:T(8,128)} %maximum_bitcast_fusion.4.cos_ref, ...), custom_call_target="tpu_custom_call" | custom-call | flops 5368709120 | bytes 13107200 | tf_op jit(solution)/shard_map/attend_back/pallas_call | solution.py:188
  1121.4 62.2 %collective-permute-done.8 = bf16[2,2048,384]{2,1,0:T(8,128)(2,1)} collective-permute-done((bf16[2,2048,384]{2,1,0:T(8,128)(2,1)}, bf16[2,2048,384]{2,1,0:T(8,128)(2,1)}, u32[]{:S(2)}, u32[]{:S(2)}) %collective-permute-start.8) | collective-permute-done | bytes 3145760 | tf_op jit(solution)/shard_map/ppermute | solution.py:45
  1204.1 42.0 %all-reduce.4 = (f32[2048]{0:T(1024)S(1)}, f32[128]{0:T(128)S(1)}, f32[128]{0:T(128)S(1)}, f32[2048]{0:T(1024)S(1)}) all-reduce(f32[2048]{0:T(1024)S(1)} %get-tuple-element.28, f32[128]{0:T(128)S(1)} %bitcast.264, f32[128]{0:T(128)S(1)} %bitcast.265, f32[2048]{0:T(1024)S(1)} %copy-done.43), channel_id=5, replica_groups=mesh['fsdp'=16,'tp'=2] {'fsdp','tp'}, use_global_device_ids=true, to_apply=%region_17.18.clone | all-reduce | flops 4352 | bytes 34816
  1254.5 50.0 %reduce-scatter.14.cloned.1.call-done = bf16[128,2048]{1,0:T(8,128)(2,1)} async-done(((bf16[2048,2048]{1,0:T(8,128)(2,1)}), bf16[128,2048]{1,0:T(8,128)(2,1)}) %reduce-scatter.14.cloned.1.call-update) | async-done | bytes 524304 | tf_op jit(solution)/shard_map/reduce_scatter | solution.py:391
  1306.6 121.1 %reduce-scatter.12.cloned.1.call-done = bf16[128,2560]{1,0:T(8,128)(2,1)} async-done(((bf16[2048,2560]{1,0:T(8,128)(2,1)}), bf16[128,2560]{1,0:T(8,128)(2,1)}) %reduce-scatter.12.cloned.1.call-update) | async-done | bytes 655376 | tf_op jit(solution)/shard_map/reduce_scatter | solution.py:396
  (335 shorter events, 488.7 us)
Async XLA Ops:
  7.2 208.8 %copy-start = (s32[1,512,8]{1,2,0:T(8,128)S(1)}, s32[1,512,8]{1,2,0:T(8,128)}, u32[]{:S(2)}) copy-start(s32[1,512,8]{1,2,0:T(8,128)} %param.29) | copy-start | bytes 49156
  7.2 93.9 %all-gather.6.cloned.1.call-start = ((), (), s32[]{:S(2)}) async-start(), calls=%async_computation.6 | async-start | bytes 11141120 | tf_op jit(solution)/shard_map/all_gather | solution.py:238
  9.4 166.5 %all-gather.8.cloned.1.call-start = ((), (), s32[]{:S(2)}) async-start(), calls=%async_computation.7 | async-start | bytes 8912896 | tf_op jit(solution)/shard_map/all_gather | solution.py:246
  10.1 432.1 %all-gather.12.cloned.1.call-start = ((), (), s32[]{:S(2)}) async-start(), calls=%async_computation.10 | async-start | bytes 17825792 | tf_op jit(solution)/shard_map/all_gather | solution.py:305
  10.8 457.0 %all-gather.10.cloned.1.call-start = ((), (), s32[]{:S(2)}) async-start(), calls=%async_computation.8 | async-start | bytes 17825792 | tf_op jit(solution)/shard_map/all_gather | solution.py:295
  14.0 26.2 %collective-permute-start = (bf16[1,256,2048]{2,1,0:T(8,128)(2,1)S(1)}, bf16[1,256,2048]{2,1,0:T(8,128)(2,1)S(1)}, u32[]{:S(2)}, u32[]{:S(2)}) collective-permute-start(bf16[1,256,2048]{2,1,0:T(8,128)(2,1)S(1)} %fusion.14), channel_id=1, source_target_pairs={{0,1},{1,0},{2,3},{3,2},{4,5},{5,4},{6,7},{7,6},{8,9},{9,8},{10,11... | collective-permute-start | bytes 3145736 | tf_op jit(solution)/shard_map/ppermute | solution.py:33
  183.7 25.4 %collective-permute-start.1 = (bf16[1,256,2048]{2,1,0:T(8,128)(2,1)S(1)}, bf16[1,256,2048]{2,1,0:T(8,128)(2,1)S(1)}, u32[]{:S(2)}, u32[]{:S(2)}) collective-permute-start(bf16[1,256,2048]{2,1,0:T(8,128)(2,1)S(1)} %fusion.34), channel_id=1, source_target_pairs={{0,1},{1,0},{2,3},{3,2},{4,5},{5,4},{6,7},{7,6},{8,9},{9,8},{10,11... | collective-permute-start | bytes 3145736 | tf_op jit(solution)/shard_map/ppermute | solution.py:45
  212.3 667.4 %reduce-scatter.10.cloned.1.call-start = ((), (), s32[]{:S(2)}) async-start(), calls=%async_computation.11 | async-start | bytes 17825792 | tf_op jit(solution)/shard_map/reduce_scatter | solution.py:373
  212.4 71.4 %collective-permute-start.4 = (bf16[2,384,2048]{2,1,0:T(8,128)(2,1)}, bf16[2,384,2048]{2,1,0:T(8,128)(2,1)}, u32[]{:S(2)}, u32[]{:S(2)}) collective-permute-start(bf16[2,384,2048]{2,1,0:T(8,128)(2,1)} %param.28), channel_id=1, source_target_pairs={{0,1},{1,0},{2,3},{3,2},{4,5},{5,4},{6,7},{7,6},{8,9},{9,8},{10,11... | collective-permute-start | bytes 9437192 | tf_op jit(solution)/shard_map/ppermute | solution.py:33
  213.9 137.2 %collective-permute-start.2 = (bf16[2,2048,384]{2,1,0:T(8,128)(2,1)}, bf16[2,2048,384]{2,1,0:T(8,128)(2,1)}, u32[]{:S(2)}, u32[]{:S(2)}) collective-permute-start(bf16[2,2048,384]{2,1,0:T(8,128)(2,1)} %param.26), channel_id=1, source_target_pairs={{0,1},{1,0},{2,3},{3,2},{4,5},{5,4},{6,7},{7,6},{8,9},{9,8},{10,11... | collective-permute-start | bytes 9437192 | tf_op jit(solution)/shard_map/ppermute | solution.py:33
  214.5 202.6 %collective-permute-start.3 = (bf16[2,2048,384]{2,1,0:T(8,128)(2,1)}, bf16[2,2048,384]{2,1,0:T(8,128)(2,1)}, u32[]{:S(2)}, u32[]{:S(2)}) collective-permute-start(bf16[2,2048,384]{2,1,0:T(8,128)(2,1)} %param.27), channel_id=1, source_target_pairs={{0,1},{1,0},{2,3},{3,2},{4,5},{5,4},{6,7},{7,6},{8,9},{9,8},{10,11... | collective-permute-start | bytes 9437192 | tf_op jit(solution)/shard_map/ppermute | solution.py:33
  255.3 164.3 %copy-start.30 = (bf16[2048,32]{0,1:T(8,128)(2,1)}, bf16[2048,32]{0,1:T(8,128)(2,1)S(1)}, u32[]{:S(2)}) copy-start(bf16[2048,32]{0,1:T(8,128)(2,1)S(1)} %all_gather.28) | copy-start | bytes 393220
  256.4 238.7 %copy-start.2 = (pred[16,2,160,256]{3,2,0,1:T(32,128)(4,1)}, pred[16,2,160,256]{3,2,0,1:T(32,128)(4,1)S(1)}, u32[]{:S(2)}) copy-start(pred[16,2,160,256]{3,2,0,1:T(32,128)(4,1)S(1)} %iota_compare_fusion) | copy-start | bytes 3932164
  705.5 45.3 %all-to-all-start = ((f32[16,256,2]{1,2,0:T(2,128)}), f32[16,256,2]{1,2,0:T(2,128)S(1)}, u32[]{:S(2)}, u32[]{:S(2)}) async-start(f32[16,256,2]{1,2,0:T(2,128)} %copy.41), calls=%async_computation.2 | async-start | bytes 65536 | tf_op jit(solution)/shard_map/all_to_all | solution.py:370
  709.0 382.1 %reduce-scatter.16.cloned.1.call-start = ((), (), s32[]{:S(2)}) async-start(), calls=%async_computation.14 | async-start | bytes 1081344
  752.5 496.0 %reduce-scatter.8.cloned.1.call-start = ((), (), s32[]{:S(2)}) async-start(), calls=%async_computation.9 | async-start | bytes 17825792 | tf_op jit(solution)/shard_map/reduce_scatter | solution.py:374
  769.4 535.1 %reduce-scatter.14.cloned.1.call-start = ((), (), s32[]{:S(2)}) async-start(), calls=%async_computation.13 | async-start | bytes 8912896 | tf_op jit(solution)/shard_map/reduce_scatter | solution.py:391
  883.8 29.2 %collective-permute-start.5 = (bf16[1,256,2048]{2,1,0:T(8,128)(2,1)S(1)}, bf16[1,256,2048]{2,1,0:T(8,128)(2,1)S(1)}, u32[]{:S(2)}, u32[]{:S(2)}) collective-permute-start(bf16[1,256,2048]{2,1,0:T(8,128)(2,1)S(1)} %fusion.52), channel_id=1, source_target_pairs={{0,1},{1,0},{2,3},{3,2},{4,5},{5,4},{6,7},{7,6},{8,9},{9,8},{10,11... | collective-permute-start | bytes 3145736 | tf_op jit(solution)/shard_map/ppermute | solution.py:33
  919.8 507.9 %reduce-scatter.12.cloned.1.call-start = ((), (), s32[]{:S(2)}) async-start(), calls=%async_computation.12 | async-start | bytes 11141120 | tf_op jit(solution)/shard_map/reduce_scatter | solution.py:396
  950.8 141.7 %collective-permute-start.9 = (bf16[2,384,2048]{2,1,0:T(8,128)(2,1)}, bf16[2,384,2048]{2,1,0:T(8,128)(2,1)}, u32[]{:S(2)}, u32[]{:S(2)}) collective-permute-start(bf16[2,384,2048]{2,1,0:T(8,128)(2,1)} %pad_maximum_fusion.2), channel_id=1, source_target_pairs={{0,1},{1,0},{2,3},{3,2},{4,5},{5,4},{6,7},{7,6},{8,9},{9,8},{10,11... | collective-permute-start | bytes 9437192 | tf_op jit(solution)/shard_map/ppermute | solution.py:45
  1044.9 71.3 %collective-permute-start.7 = (bf16[2,2048,384]{2,1,0:T(8,128)(2,1)}, bf16[2,2048,384]{2,1,0:T(8,128)(2,1)}, u32[]{:S(2)}, u32[]{:S(2)}) collective-permute-start(bf16[2,2048,384]{2,1,0:T(8,128)(2,1)} %pad_maximum_fusion), channel_id=1, source_target_pairs={{0,1},{1,0},{2,3},{3,2},{4,5},{5,4},{6,7},{7,6},{8,9},{9,8},{10,11... | collective-permute-start | bytes 9437192 | tf_op jit(solution)/shard_map/ppermute | solution.py:45
  1078.6 105.1 %collective-permute-start.8 = (bf16[2,2048,384]{2,1,0:T(8,128)(2,1)}, bf16[2,2048,384]{2,1,0:T(8,128)(2,1)}, u32[]{:S(2)}, u32[]{:S(2)}) collective-permute-start(bf16[2,2048,384]{2,1,0:T(8,128)(2,1)} %pad_maximum_fusion.1), channel_id=1, source_target_pairs={{0,1},{1,0},{2,3},{3,2},{4,5},{5,4},{6,7},{7,6},{8,9},{9,8},{10,11... | collective-permute-start | bytes 9437192 | tf_op jit(solution)/shard_map/ppermute | solution.py:45
  1109.6 93.5 %collective-permute-start.6 = (bf16[1,256,2048]{2,1,0:T(8,128)(2,1)S(1)}, bf16[1,256,2048]{2,1,0:T(8,128)(2,1)S(1)}, u32[]{:S(2)}, u32[]{:S(2)}) collective-permute-start(bf16[1,256,2048]{2,1,0:T(8,128)(2,1)S(1)} %fusion.35), channel_id=1, source_target_pairs={{0,1},{1,0},{2,3},{3,2},{4,5},{5,4},{6,7},{7,6},{8,9},{9,8},{10,11... | collective-permute-start | bytes 3145736 | tf_op jit(solution)/shard_map/ppermute | solution.py:45
  1248.5 182.9 %copy-start.1 = (s32[1,512,8]{1,2,0:T(8,128)S(1)}, s32[1,512,8]{1,2,0:T(8,128)}, u32[]{:S(2)}) copy-start(s32[1,512,8]{1,2,0:T(8,128)} %param.29) | copy-start | bytes 49156
  (84 other events, 3035.5 us)
Sparse Core Ops, SparseCore 0:
  10.9 90.2 all-gather.5
  103.3 72.5 all-gather.7
  178.1 126.5 all-gather.11
  307.3 125.6 all-gather.9
  705.0 174.6 reduce-scatter.9
  882.3 137.9 reduce-scatter.15
  1024.4 173.3 reduce-scatter.7
  1201.9 102.5 reduce-scatter.13
  1308.6 119.0 reduce-scatter.11

commit v2 on v1

--- a/solution.py
+++ b/solution.py
@@ -1,4 +1,3 @@
-import functools
 import math
 
 import jax
@@ -7,6 +6,7 @@
 from jax.experimental import pallas as pl
 from jax.experimental.pallas import tpu as pltpu
 from jax.sharding import PartitionSpec as P
+
 
 EPSILON = 1e-06
 ROPE_BASE = 1000000.0
@@ -47,6 +47,80 @@
         )
         total = total + moved.astype(F32)
     return total
+
+
+def chip_ring(nodes):
+    chips = nodes // 2
+    order = list(range(0, chips, 2)) + list(range(1, chips, 2))[::-1]
+    links = [(order[i] * 2 + c, order[(i + 1) % chips] * 2 + c) for i in range(chips) for c in (0, 1)]
+    swap = [(i, i ^ 1) for i in range(nodes)]
+    return order, links, [(b, a) for a, b in links], swap
+
+
+def ring_fits(nodes):
+    return nodes % 4 == 0 and 8 <= nodes <= 16
+
+
+def node_at(order, shift, core):
+    place = jnp.asarray([order.index(i) for i in range(len(order))], jnp.int32)
+    mine = place[lax.axis_index("fsdp") // 2]
+    return jnp.asarray(order, jnp.int32)[(mine + shift) % len(order)] * 2 + core
+
+
+def ring_gather(block, between):
+    nodes = lax.axis_size("fsdp")
+    if not ring_fits(nodes):
+        for work in between:
+            work(())
+        return lax.all_gather(block, "fsdp", axis=0)
+    order, up, down, swap = chip_ring(nodes)
+    core = lax.axis_index("fsdp") % 2
+    whole = jnp.zeros((nodes,) + block.shape, block.dtype)
+
+    def keep(whole, piece, shift):
+        other = lax.ppermute(piece, "fsdp", swap)
+        for values, at in ((piece, core), (other, 1 - core)):
+            whole = lax.dynamic_update_index_in_dim(whole, values, node_at(order, shift, at), 0)
+        return whole
+
+    whole = keep(whole, block, 0)
+    ahead = behind = block
+    for step in range(1, len(order) // 2 + 1):
+        behind = lax.ppermute(behind, "fsdp", up)
+        if step < (len(order) + 1) // 2:
+            ahead = lax.ppermute(ahead, "fsdp", down)
+        if step <= len(between):
+            behind, ahead = between[step - 1]((behind, ahead))
+        whole = keep(whole, behind, -step)
+        if step < (len(order) + 1) // 2:
+            whole = keep(whole, ahead, step)
+    return whole
+
+
+def ring_scatter(blocks):
+    nodes = lax.axis_size("fsdp")
+    if not ring_fits(nodes):
+        return lax.psum_scatter(blocks, "fsdp", scatter_dimension=0, tiled=False).astype(F32)
+    order, up, down, swap = chip_ring(nodes)
+    core = lax.axis_index("fsdp") % 2
+
+    def chip_sum(shift):
+        mine = lax.dynamic_index_in_dim(blocks, node_at(order, shift, core), 0, keepdims=False)
+        away = lax.dynamic_index_in_dim(blocks, node_at(order, shift, 1 - core), 0, keepdims=False)
+        return mine.astype(F32) + lax.ppermute(away, "fsdp", swap).astype(F32)
+
+    far = len(order) // 2
+    rising = chip_sum(far).astype(BF16)
+    falling = chip_sum(far + 1).astype(BF16)
+    for step in range(far - 1, -1, -1):
+        rising = lax.ppermute(rising, "fsdp", up).astype(F32)
+        if step > 0:
+            rising = (rising + chip_sum(step)).astype(BF16)
+        if step < far - 1:
+            falling = lax.ppermute(falling, "fsdp", down).astype(F32)
+            if step > 0:
+                falling = (falling + chip_sum(-step)).astype(BF16)
+    return rising + falling + chip_sum(0)
 
 
 def turn(values, cosine, sine):
@@ -199,7 +273,7 @@
     )(pre, pre, pre, *tables, *gains, attended, grad_attended)
 
 
-def local(
+def layer(
     layer_input,
     attention_gain,
     query_gain,
@@ -229,7 +303,6 @@
     part = lax.axis_index("tp")
     heads = query_weight.shape[1] // head_size
     kv_heads = key_weight.shape[1] // head_size
-    hidden_size = half_hidden * tp_size
     capacity = max(2, rows * length * top_count * 5 // (4 * expert_count))
     tokens = rows * local_length
     places = min(capacity, tokens)
@@ -284,10 +357,28 @@
     slot = jnp.where(member, slot, -1)
     placed = slot[:, :, None, :] == jnp.arange(places, dtype=jnp.int32)[None, None, :, None]
 
+    normed_rows, router_full, all_routes = lax.optimization_barrier(
+        (normed_rows, router_full, all_routes)
+    )
     pre = mm(normed_rows, qkv_full)
+    cot_low = cotangent.reshape(tokens, model_width)
+    cot_low, pre = lax.optimization_barrier((cot_low, pre))
     attended = attend(pre, tables, gains, rows, heads, kv_heads)
-    projected = mm(attended, output_full, ((1,), (1,))).reshape(rows, tp_size, local_length, model_width)
-    middle = input_wide + scatter_tp([projected[:, j] for j in range(tp_size)])
+    made = {}
+
+    def project(moving):
+        held, moving = lax.optimization_barrier((attended, moving))
+        projected = mm(held, output_full, ((1,), (1,)))
+        projected = projected.reshape(rows, tp_size, local_length, model_width)
+        made["middle"] = input_wide + scatter_tp([projected[:, j] for j in range(tp_size)])
+        return moving
+
+    def settle(moving):
+        made["middle"], moving = lax.optimization_barrier((made["middle"], moving))
+        return moving
+
+    cot_all = ring_gather(cot_low, (project, settle))
+    middle = made["middle"]
     inverse_two = inverse_rms(middle)
     normed_two = middle * inverse_two
     expert_low = (normed_two * expert_gain).astype(BF16).reshape(tokens, model_width)
@@ -300,10 +391,8 @@
     top = jnp.max(jnp.where(chosen, logits, NEGATIVE), axis=-1, keepdims=True)
     powers = jnp.where(chosen, jnp.exp(jnp.minimum(logits - top, 0.0)), 0.0)
     gates = powers / jnp.sum(powers, axis=-1, keepdims=True)
-    gates_all = lax.all_gather(gates, "fsdp", axis=0)
-    cot_low = cotangent.reshape(tokens, model_width)
-    cot_all = lax.all_gather(cot_low, "fsdp", axis=0)
-    own_gates = lax.dynamic_slice_in_dim(gates_all, node * local_experts, local_experts, axis=2)
+    gates_out = jnp.moveaxis(gates.reshape(tokens, nodes, local_experts), 1, 0)
+    own_gates = lax.all_to_all(gates_out, "fsdp", split_axis=0, concat_axis=0, tiled=True)
     gate_of = jnp.sum(
         jnp.where(placed, jnp.moveaxis(own_gates, 2, 1)[:, :, None, :], 0.0), axis=-1
     )
@@ -370,10 +459,9 @@
     grad_gate = lax.all_to_all(column, "fsdp", split_axis=0, concat_axis=0, tiled=True)
     grad_gate = jnp.moveaxis(grad_gate, 0, 1).reshape(tokens, expert_count)
 
-    grad_rows = lax.psum_scatter(grad_total, "fsdp", scatter_dimension=0, tiled=True)
+    grad_rows = ring_scatter(grad_total)
     expert_part = lax.psum_scatter(out_total, "fsdp", scatter_dimension=0, tiled=True)
-    layer_output = (middle + expert_part.reshape(middle.shape).astype(F32)).astype(BF16)
-
+    grad_rows, far_grads = lax.optimization_barrier((grad_rows, far_grads))
     grad_logits = (
         gates * (grad_gate - jnp.sum(gates * grad_gate, axis=-1, keepdims=True))
     ).astype(BF16)
@@ -388,12 +476,14 @@
     grad_flat = gather_tp(grad_middle.astype(BF16), 1).reshape(every, model_width)
     grad_attended = mm(grad_flat, output_full).astype(BF16)
     output_low = mm(grad_flat, attended, ((0,), (0,))).astype(BF16)
-    output_grad = lax.psum_scatter(output_low, "fsdp", scatter_dimension=0, tiled=True).astype(F32)
+    output_low, expert_part = lax.optimization_barrier((output_low, expert_part))
+    output_part = lax.psum_scatter(output_low, "fsdp", scatter_dimension=0, tiled=True)
     grad_pre, query_gain_part, key_gain_part = attend_back(
         pre, tables, gains, attended, grad_attended, rows, heads, kv_heads
     )
     qkv_low = mm(normed_rows, grad_pre, ((0,), (0,))).astype(BF16)
-    qkv_grad = lax.psum_scatter(qkv_low, "fsdp", scatter_dimension=0, tiled=True).astype(F32)
+    qkv_grad = ring_scatter(qkv_low.reshape(nodes, -1, qkv_low.shape[1]))
+    qkv_grad = qkv_grad.reshape(query_weight.shape[0], -1)
     query_width, key_width = query_weight.shape[1], key_weight.shape[1]
     query_grad = qkv_grad[:, :query_width]
     key_grad = qkv_grad[:, query_width : query_width + key_width]
@@ -413,7 +503,10 @@
         weight_grads.append(scatter_tp([mine] + far))
     gate_grad, up_grad, down_grad = weight_grads
 
+    layer_output = (middle + expert_part.reshape(middle.shape).astype(F32)).astype(BF16)
+    router_part, output_part = lax.optimization_barrier((router_part, output_part))
     router_grad = lax.psum_scatter(router_part, ("fsdp", "tp"), scatter_dimension=0, tiled=True)
+    output_grad = output_part.astype(F32)
     small = [
         lax.psum_scatter(value.reshape(-1), ("fsdp", "tp"), scatter_dimension=0, tiled=True)
         for value in (attention_gain_part, expert_gain_part, query_gain_part, key_gain_part)
@@ -439,7 +532,7 @@
 
 def solution(mesh):
     return jax.shard_map(
-        local,
+        layer,
         mesh=mesh,
         in_specs=(
             P("fsdp", "tp", None),

time: 1450 us -> 1500 us (1.034)
  waiting for transfers between devices: 679 us -> 570 us
  local copies, waits for them, and re-layouts: 53.7 us -> 106 us
  starting transfers between devices: 19.2 us -> 61.1 us
  blocking collectives: 103 us -> 139 us
  other arithmetic: 73.9 us -> 93.5 us
  between operations: 15 us -> 30.3 us
    reduce_scatter x4 -> x2, waiting for transfers between devices: 281 us -> 0.01 us  [the longest x1 0.01 us: layer(): lax.psum_scatter(out_total, 'fsdp', scatter_dimension=0, tiled=True)]
    unnamed x10 -> x7, waiting for transfers between devices: 1.49 us -> 130 us
    ppermute x0 -> x45, waiting for transfers between devices: none -> 105 us  [the longest x8 71.6 us: ring_scatter(): rising = lax.ppermute(rising, 'fsdp', up).astype(F32)]
    unnamed x1, blocking collectives: 42 us -> 96.3 us
    ppermute x5, waiting for transfers between devices: 105 us -> 57.9 us  [scatter_tp(): lax.ppermute(pieces[j].astype(BF16), 'tp', [(s, (s + j) % size) for s in...]
    ppermute x0 -> x45, starting transfers between devices: none -> 36.4 us  [the longest x8 19.4 us: ring_scatter(): rising = lax.ppermute(rising, 'fsdp', up).astype(F32)]
    dynamic_update_slice x0 -> x16, local copies, waits for them, and re-layouts: none -> 27.2 us  [keep(): lax.dynamic_update_index_in_dim(whole, values, node_at(order, shift, at), 0)]
    all_gather x3 -> x2, blocking collectives: 60.6 us -> 42.6 us  [the longest x1 24.3 us: layer(): lax.all_gather(own_routes, 'fsdp', axis=0).reshape(nodes, tokens, top_count)]
  transfers between devices with their start and end apart: 20 -> 63, of which waited for: 14 -> 22; matrix products, arithmetic and copies ran while one was open for 21% -> 25% of each run, Pallas kernels for 5% -> 5%
where the time goes in v2:
time: 1500 us
  waiting for transfers between devices  570 us (38%)
  matrix products  424 us (28%)
  blocking collectives  139 us (9%)
  local copies, waits for them, and re-layouts  106 us (7%)
  other arithmetic  93.5 us (6%)
  Pallas kernels  70 us (5%)
  starting transfers between devices  61.1 us (4%)
  between operations  30.3 us (2%)
    dot_general x27, matrix products, mm(): return lax.dot_general(a, b, (dims, ((), ())), preferred_element_type=F32)  320 us
    ppermute x5, waiting for transfers between devices, fetch_next(): lax.ppermute(values, 'tp', [(s, (s - step) % size) for s in range(size)])  188 us
    unnamed x7, waiting for transfers between devices  130 us
    unnamed x1, blocking collectives  96.3 us
    ppermute x8, waiting for transfers between devices, ring_scatter(): rising = lax.ppermute(rising, 'fsdp', up).astype(F32)  71.6 us
    ppermute x5, waiting for transfers between devices, scatter_tp(): lax.ppermute(pieces[j].astype(BF16), 'tp', [(s, (s + j) % size) for s in...  57.9 us
    pallas_call x1, Pallas kernels, attend_back(): pl.pallas_call(attend_back_kernel, grid=(rows, kv_heads, group_size + 2),...  41.3 us
    all_gather x1, waiting for transfers between devices, layer(): output_full = lax.all_gather(output_weight, 'fsdp', axis=0, tiled=True)  40.7 us
  transfers between devices with their start and end apart: 63, of which 22 were waited for; matrix products, arithmetic and copies ran while one was open for 25% of the time, Pallas kernels for 5%

profile of v2, /device:TPU:0, one launch (start us, length us, event | category | flops | bytes accessed | tf_op | source)
XLA Modules:
  0.0 1495.1 jit_solution(16024246241986547306)
XLA Ops:
  16.3 24.3 %all_gather.16 = s32[16,256,8]{1,2,0:T(8,128)} all-gather(s32[1,256,8]{1,2,0:T(8,128)S(1)} %constant_dynamic-slice_fusion.2), channel_id=1, replica_groups=mesh['fsdp'=16,'tp'=2] {'fsdp'}, dimensions={0}, use_global_device_ids=true | all-gather | bytes 139264 | tf_op jit(solution)/shard_map/all_gather | solution.py:350
  40.6 18.3 %all_gather.15 = bf16[2048,32]{0,1:T(8,128)(2,1)S(1)} all-gather(bf16[128,32]{0,1:T(8,128)(2,1)S(1)} %copy-done.65), channel_id=1, replica_groups=mesh['fsdp'=16,'tp'=2] {'fsdp'}, dimensions={0}, use_global_device_ids=true | all-gather | bytes 139264 | tf_op jit(solution)/shard_map/all_gather | solution.py:320
  61.8 40.1 %all-gather.4.cloned.1.call-done = bf16[2048,2560]{1,0:T(8,128)(2,1)} async-done(((bf16[128,2560]{1,0:T(8,128)(2,1)}), bf16[2048,2560]{1,0:T(8,128)(2,1)}) %all-gather.4.cloned.1.call-update) | async-done | bytes 10485776 | tf_op jit(solution)/shard_map/all_gather | solution.py:311
  118.3 28.6 %attend.1.att_ref = bf16[512,2048]{1,0:T(8,128)(2,1)} custom-call(f32[512,2560]{1,0:T(8,128)} %fusion.76.q_ref.k_ref.v_ref, f32[512,2560]{1,0:T(8,128)} %fusion.76.q_ref.k_ref.v_ref, f32[512,2560]{1,0:T(8,128)} %fusion.76.q_ref.k_ref.v_ref, f32[512,128]{1,0:T(8,128)} %maximum_bitcast_fusion.4.cos_ref, f32[512,128]{1,0:T(8,128)} %maximum_bitcast_fusion.5.sin_ref, ...), custom_call_target="tpu_custom_call" | custom-call | flops 2147483648 | bytes 7864320 | tf_op jit(solution)/shard_map/attend/pallas_call | solution.py:234
  152.9 40.7 %all-gather.6.cloned.1.call-done = bf16[2048,2048]{1,0:T(8,128)(2,1)} async-done(((bf16[128,2048]{1,0:T(8,128)(2,1)}), bf16[2048,2048]{1,0:T(8,128)(2,1)}) %all-gather.6.cloned.1.call-update) | async-done | bytes 8388624 | tf_op jit(solution)/shard_map/all_gather | solution.py:319
  205.1 21.6 %collective-permute-done.3 = bf16[1,256,2048]{2,1,0:T(8,128)(2,1)S(1)} collective-permute-done((bf16[1,256,2048]{2,1,0:T(8,128)(2,1)S(1)}, bf16[1,256,2048]{2,1,0:T(8,128)(2,1)S(1)}, u32[]{:S(2)}, u32[]{:S(2)}) %collective-permute-start.3) | collective-permute-done | bytes 1048608 | tf_op jit(solution)/shard_map/ppermute | solution.py:45
  256.2 46.1 %collective-permute-done.18 = bf16[2,2048,384]{2,1,0:T(8,128)(2,1)} collective-permute-done((bf16[2,2048,384]{2,1,0:T(8,128)(2,1)}, bf16[2,2048,384]{2,1,0:T(8,128)(2,1)}, u32[]{:S(2)}, u32[]{:S(2)}) %collective-permute-start.18) | collective-permute-done | bytes 3145760 | tf_op jit(solution)/shard_map/ppermute | solution.py:33
  306.1 63.5 %collective-permute-done.19 = bf16[2,2048,384]{2,1,0:T(8,128)(2,1)} collective-permute-done((bf16[2,2048,384]{2,1,0:T(8,128)(2,1)}, bf16[2,2048,384]{2,1,0:T(8,128)(2,1)}, u32[]{:S(2)}, u32[]{:S(2)}) %collective-permute-start.19) | collective-permute-done | bytes 3145760 | tf_op jit(solution)/shard_map/ppermute | solution.py:33
  372.2 62.7 %collective-permute-done.17 = bf16[2,384,2048]{2,1,0:T(8,128)(2,1)} collective-permute-done((bf16[2,384,2048]{2,1,0:T(8,128)(2,1)}, bf16[2,384,2048]{2,1,0:T(8,128)(2,1)}, u32[]{:S(2)}, u32[]{:S(2)}) %collective-permute-start.17) | collective-permute-done | bytes 3145760 | tf_op jit(solution)/shard_map/ppermute | solution.py:33
  486.7 16.8 %collective-permute-done.15 = bf16[256,2048]{1,0:T(8,128)(2,1)S(1)} collective-permute-done((bf16[256,2048]{1,0:T(8,128)(2,1)S(1)}, bf16[256,2048]{1,0:T(8,128)(2,1)S(1)}, u32[]{:S(2)}, u32[]{:S(2)}) %collective-permute-start.15) | collective-permute-done | bytes 1048608 | tf_op jit(solution)/shard_map/ppermute | solution.py:89
  615.7 15.8 %multiply_reduce_fusion.1 = (f32[2560]{0:T(1024)S(1)}, f32[2560,768]{0,1:T(8,128)}) fusion(f32[2560,768]{0,1:T(8,128)} %fusion.12, f32[2560,768]{0,1:T(8,128)} %fusion.13, bf16[2560,2048]{1,0:T(8,128)(2,1)S(1)} %bitcast.332, bf16[2,768,2048]{2,1,0:T(8,128)(2,1)} %copy-done.38), kind=kOutput, calls=%fused_computation.8 | convolution fusion | flops 8066823680 | bytes 37234688 | tf_op jit(solution)/shard_map/dot_general | solution.py:28
  631.5 18.8 %multiply_reduce_fusion = (f32[2560]{0:T(1024)S(1)}, f32[2560,768]{0,1:T(8,128)}) fusion(f32[2560,768]{0,1:T(8,128)} %fusion.8, f32[2560,768]{0,1:T(8,128)} %fusion.9, bf16[2560,2048]{1,0:T(8,128)(2,1)} %bitcast.336, bf16[2,768,2048]{2,1,0:T(8,128)(2,1)} %copy-done.38), kind=kOutput, calls=%fused_computation.7 | convolution fusion | flops 8066823680 | bytes 37234688 | tf_op jit(solution)/shard_map/dot_general | solution.py:28
  653.8 15.6 %multiply_convert_fusion = (bf16[2560,768]{0,1:T(8,128)(2,1)}, bf16[2560,768]{0,1:T(8,128)(2,1)}, bf16[2560,768]{0,1:T(8,128)(2,1)}) fusion(f32[2560]{0:T(1024)S(1)} %mul.572, f32[2560,768]{0,1:T(8,128)} %fusion.8, f32[2560,768]{0,1:T(8,128)} %fusion.9, f32[2560,768]{0,1:T(8,128)} %get-tuple-element.136), kind=kLoop, calls=%fused_computation.9 | loop fusion | flops 33423360 | bytes 35399680 | tf_op jit(solution)/shard_map/convert_element_type | solution.py:424
  693.5 15.6 %fusion.11 = f32[2560,2048]{1,0:T(8,128)} fusion(bf16[2560,768]{0,1:T(8,128)(2,1)} %get-tuple-element.99, bf16[2,2048,768]{2,1,0:T(8,128)(2,1)} %constant_dynamic-update-slice_fusion.2), kind=kOutput, calls=%fused_computation.64 | convolution fusion | flops 8053063680 | bytes 28049408 | tf_op jit(solution)/shard_map/dot_general | solution.py:28
  745.5 16.5 %add_convert_fusion = bf16[16,256,2048]{2,1,0:T(8,128)(2,1)} fusion(bf16[16,256,2048]{2,1,0:T(8,128)(2,1)} %fusion.60, bf16[16,160,2048]{2,1,0:T(8,128)(2,1)} %bitcast.345, pred[16,2,160,256]{3,2,0,1:T(32,128)(4,1)S(1)} %copy-done.6), kind=kOutput, calls=%fused_computation | convolution fusion | flops 2709520384 | bytes 44695552 | tf_op jit(solution)/shard_map/gst,gsd->gtd/dot_general | solution.py:429
  762.0 19.2 %add_convert_fusion.3 = bf16[2560,2048]{1,0:T(8,128)(2,1)} fusion(f32[2560,2048]{1,0:T(8,128)} %fusion.7, bf16[2560,768]{0,1:T(8,128)(2,1)} %get-tuple-element.95, bf16[2,2048,768]{2,1,0:T(8,128)(2,1)} %copy-done.39), kind=kOutput, calls=%fused_computation.3 | convolution fusion | flops 8063549440 | bytes 38535168 | tf_op jit(solution)/shard_map/dot_general | solution.py:28
  781.2 19.1 %add_convert_fusion.2 = bf16[2560,2048]{1,0:T(8,128)(2,1)} fusion(f32[2560,2048]{1,0:T(8,128)} %fusion.11, bf16[2560,768]{0,1:T(8,128)(2,1)} %get-tuple-element.98, bf16[2,2048,768]{2,1,0:T(8,128)(2,1)} %copy-done.39), kind=kOutput, calls=%fused_computation.2 | convolution fusion | flops 8063549440 | bytes 38535168 | tf_op jit(solution)/shard_map/dot_general | solution.py:28
  829.9 18.4 %fusion.82 = f32[2048,768]{1,0:T(8,128)} fusion(bf16[2560,2048]{1,0:T(8,128)(2,1)} %bitcast.340, bf16[2560,768]{0,1:T(8,128)(2,1)} %get-tuple-element.96), kind=kOutput, calls=%fused_computation.232 | convolution fusion | flops 8053063680 | bytes 20709376 | tf_op jit(solution)/shard_map/dot_general | solution.py:28
  901.1 22.2 %collective-permute-done.21 = bf16[256,2048]{1,0:T(8,128)(2,1)S(1)} collective-permute-done((bf16[256,2048]{1,0:T(8,128)(2,1)S(1)}, bf16[256,2048]{1,0:T(8,128)(2,1)S(1)}, u32[]{:S(2)}, u32[]{:S(2)}) %collective-permute-start.21) | collective-permute-done | bytes 1048608 | tf_op jit(solution)/shard_map/ppermute | solution.py:116
  946.7 20.3 %collective-permute-done.23 = bf16[256,2048]{1,0:T(8,128)(2,1)} collective-permute-done((bf16[256,2048]{1,0:T(8,128)(2,1)}, bf16[256,2048]{1,0:T(8,128)(2,1)}, u32[]{:S(2)}, u32[]{:S(2)}) %collective-permute-start.23) | collective-permute-done | bytes 1048608 | tf_op jit(solution)/shard_map/ppermute | solution.py:116
  1079.7 41.3 %attend_back.1 = (bf16[512,2560]{1,0:T(8,128)(2,1)}, f32[1,128]{1,0:T(1,128)}, f32[1,128]{1,0:T(1,128)}) custom-call(f32[512,2560]{1,0:T(8,128)} %fusion.76.q_ref.k_ref.v_ref, f32[512,2560]{1,0:T(8,128)} %fusion.76.q_ref.k_ref.v_ref, f32[512,2560]{1,0:T(8,128)} %fusion.76.q_ref.k_ref.v_ref, f32[512,128]{1,0:T(8,128)} %maximum_bitcast_fusion.4.cos_ref, ...), custom_call_target="tpu_custom_call" | custom-call | flops 5368709120 | bytes 13107200 | tf_op jit(solution)/shard_map/attend_back/pallas_call | solution.py:262
  1174.6 96.3 %all-reduce.4 = (f32[2048]{0:T(1024)S(1)}, f32[128]{0:T(128)S(1)}, f32[128]{0:T(128)S(1)}, f32[2048]{0:T(1024)S(1)}) all-reduce(f32[2048]{0:T(1024)S(1)} %get-tuple-element.70, f32[128]{0:T(128)S(1)} %bitcast.391, f32[128]{0:T(128)S(1)} %bitcast.392, ...), channel_id=3, replica_groups=mesh['fsdp'=16,'tp'=2] {'fsdp','tp'}, use_global_device_ids=true, to_apply=%region_16.17.clone | all-reduce | flops 4352 | bytes 34816
  1306.4 36.2 %collective-permute-done.52 = bf16[2,2048,384]{2,1,0:T(8,128)(2,1)S(1)} collective-permute-done((bf16[2,2048,384]{2,1,0:T(8,128)(2,1)}, bf16[2,2048,384]{2,1,0:T(8,128)(2,1)S(1)}, u32[]{:S(2)}, u32[]{:S(2)}) %collective-permute-start.52) | collective-permute-done | bytes 3145760 | tf_op jit(solution)/shard_map/ppermute | solution.py:45
  1357.5 128.9 %reduce-scatter.10.cloned.1.call-done = f32[64,32]{1,0:T(8,128)} async-done(((f32[2048,32]{1,0:T(8,128)}), f32[64,32]{1,0:T(8,128)}) %reduce-scatter.10.cloned.1.call-update) | async-done | bytes 8208
  (459 shorter events, 617.7 us)
Async XLA Ops:
  7.2 94.7 %all-gather.4.cloned.1.call-start = ((), (), s32[]{:S(2)}) async-start(), calls=%async_computation.5 | async-start | bytes 11141120 | tf_op jit(solution)/shard_map/all_gather | solution.py:311
  9.4 184.2 %all-gather.6.cloned.1.call-start = ((), (), s32[]{:S(2)}) async-start(), calls=%async_computation.6 | async-start | bytes 8912896 | tf_op jit(solution)/shard_map/all_gather | solution.py:319
  10.1 524.3 %all-gather.8.cloned.1.call-start = ((), (), s32[]{:S(2)}) async-start(), calls=%async_computation.7 | async-start | bytes 17825792 | tf_op jit(solution)/shard_map/all_gather | solution.py:386
  230.9 71.4 %collective-permute-start.18 = (bf16[2,2048,384]{2,1,0:T(8,128)(2,1)}, bf16[2,2048,384]{2,1,0:T(8,128)(2,1)}, u32[]{:S(2)}, u32[]{:S(2)}) collective-permute-start(bf16[2,2048,384]{2,1,0:T(8,128)(2,1)} %param.123), channel_id=1, source_target_pairs={{0,1},{1,0},{2,3},{3,2},{4,5},{5,4},{6,7},{7,6},{8,9},{9,8},{10,11... | collective-permute-start | bytes 9437192 | tf_op jit(solution)/shard_map/ppermute | solution.py:33
  231.5 138.1 %collective-permute-start.19 = (bf16[2,2048,384]{2,1,0:T(8,128)(2,1)}, bf16[2,2048,384]{2,1,0:T(8,128)(2,1)}, u32[]{:S(2)}, u32[]{:S(2)}) collective-permute-start(bf16[2,2048,384]{2,1,0:T(8,128)(2,1)} %param.122), channel_id=1, source_target_pairs={{0,1},{1,0},{2,3},{3,2},{4,5},{5,4},{6,7},{7,6},{8,9},{9,8},{10,11... | collective-permute-start | bytes 9437192 | tf_op jit(solution)/shard_map/ppermute | solution.py:33
  233.0 202.0 %collective-permute-start.17 = (bf16[2,384,2048]{2,1,0:T(8,128)(2,1)}, bf16[2,384,2048]{2,1,0:T(8,128)(2,1)}, u32[]{:S(2)}, u32[]{:S(2)}) collective-permute-start(bf16[2,384,2048]{2,1,0:T(8,128)(2,1)} %param.124), channel_id=1, source_target_pairs={{0,1},{1,0},{2,3},{3,2},{4,5},{5,4},{6,7},{7,6},{8,9},{9,8},{10,11... | collective-permute-start | bytes 9437192 | tf_op jit(solution)/shard_map/ppermute | solution.py:33
  306.1 140.3 %collective-permute-start.6 = (bf16[256,2048]{1,0:T(8,128)(2,1)S(1)}, bf16[256,2048]{1,0:T(8,128)(2,1)S(1)}, u32[]{:S(2)}, u32[]{:S(2)}) collective-permute-start(bf16[256,2048]{1,0:T(8,128)(2,1)S(1)} %bitcast.354), channel_id=1, source_target_pairs={{0,2},{2,0},{4,6},{6,4},{8,10},{10,8},{12,14},{14,12},{16,18},{18,... | collective-permute-start | bytes 3145736 | tf_op jit(solution)/shard_map/ppermute | solution.py:81
  455.9 613.9 %reduce-scatter.6.cloned.1.call-start = ((), (), s32[]{:S(2)}) async-start(), calls=%async_computation.8 | async-start | bytes 17825792 | tf_op jit(solution)/shard_map/reduce_scatter | solution.py:463
  828.0 58.1 %collective-permute-start.20 = (bf16[256,2048]{1,0:T(8,128)(2,1)}, bf16[256,2048]{1,0:T(8,128)(2,1)}, u32[]{:S(2)}, u32[]{:S(2)}) collective-permute-start(bf16[256,2048]{1,0:T(8,128)(2,1)} %get-tuple-element.86), channel_id=1, source_target_pairs={{0,2},{2,0},{4,6},{6,4},{8,10},{10,8},{12,14},{14,12},{16,18},{18,... | collective-permute-start | bytes 3145736 | tf_op jit(solution)/shard_map/ppermute | solution.py:110
  828.8 72.1 %collective-permute-start.22 = (bf16[256,2048]{1,0:T(8,128)(2,1)}, bf16[256,2048]{1,0:T(8,128)(2,1)}, u32[]{:S(2)}, u32[]{:S(2)}) collective-permute-start(bf16[256,2048]{1,0:T(8,128)(2,1)} %get-tuple-element.93), channel_id=1, source_target_pairs={{0,2},{2,0},{4,6},{6,4},{8,10},{10,8},{12,14},{14,12},{16,18},{18,... | collective-permute-start | bytes 3145736 | tf_op jit(solution)/shard_map/ppermute | solution.py:110
  828.8 72.3 %collective-permute-start.28 = (bf16[256,2048]{1,0:T(8,128)(2,1)}, bf16[256,2048]{1,0:T(8,128)(2,1)}, u32[]{:S(2)}, u32[]{:S(2)}) collective-permute-start(bf16[256,2048]{1,0:T(8,128)(2,1)} %get-tuple-element.90), channel_id=1, source_target_pairs={{0,2},{2,0},{4,6},{6,4},{8,10},{10,8},{12,14},{14,12},{16,18},{18,... | collective-permute-start | bytes 3145736 | tf_op jit(solution)/shard_map/ppermute | solution.py:110
  829.3 116.8 %collective-permute-start.24 = (bf16[256,2048]{1,0:T(8,128)(2,1)}, bf16[256,2048]{1,0:T(8,128)(2,1)}, u32[]{:S(2)}, u32[]{:S(2)}) collective-permute-start(bf16[256,2048]{1,0:T(8,128)(2,1)} %get-tuple-element.92), channel_id=1, source_target_pairs={{0,2},{2,0},{4,6},{6,4},{8,10},{10,8},{12,14},{14,12},{16,18},{18,... | collective-permute-start | bytes 3145736 | tf_op jit(solution)/shard_map/ppermute | solution.py:110
  829.3 116.9 %collective-permute-start.30 = (bf16[256,2048]{1,0:T(8,128)(2,1)}, bf16[256,2048]{1,0:T(8,128)(2,1)}, u32[]{:S(2)}, u32[]{:S(2)}) collective-permute-start(bf16[256,2048]{1,0:T(8,128)(2,1)} %get-tuple-element.89), channel_id=1, source_target_pairs={{0,2},{2,0},{4,6},{6,4},{8,10},{10,8},{12,14},{14,12},{16,18},{18,... | collective-permute-start | bytes 3145736 | tf_op jit(solution)/shard_map/ppermute | solution.py:110
  901.0 80.1 %collective-permute-start.26 = (bf16[256,2048]{1,0:T(8,128)(2,1)S(1)}, bf16[256,2048]{1,0:T(8,128)(2,1)S(1)}, u32[]{:S(2)}, u32[]{:S(2)}) collective-permute-start(bf16[256,2048]{1,0:T(8,128)(2,1)S(1)} %copy-done.44), channel_id=1, source_target_pairs={{0,2},{2,0},{4,6},{6,4},{8,10},{10,8},{12,14},{14,12},{16,18},{18,... | collective-permute-start | bytes 3145736 | tf_op jit(solution)/shard_map/ppermute | solution.py:110
  946.2 84.3 %collective-permute-start.34 = (bf16[256,2048]{1,0:T(8,128)(2,1)S(1)}, bf16[256,2048]{1,0:T(8,128)(2,1)}, u32[]{:S(2)}, u32[]{:S(2)}) collective-permute-start(bf16[256,2048]{1,0:T(8,128)(2,1)S(1)} %copy-done.42), channel_id=1, source_target_pairs={{0,2},{2,0},{4,6},{6,4},{8,10},{10,8},{12,14},{14,12},{16,18},{18,... | collective-permute-start | bytes 3145736 | tf_op jit(solution)/shard_map/ppermute | solution.py:110
  1006.9 342.1 %reduce-scatter.8.cloned.1.call-start = ((), (), s32[]{:S(2)}) async-start(), calls=%async_computation.9 | async-start | bytes 8912896 | tf_op jit(solution)/shard_map/reduce_scatter | solution.py:480
  1044.8 233.8 %collective-permute-start.54 = (bf16[2,384,2048]{2,1,0:T(8,128)(2,1)}, bf16[2,384,2048]{2,1,0:T(8,128)(2,1)}, u32[]{:S(2)}, u32[]{:S(2)}) collective-permute-start(bf16[2,384,2048]{2,1,0:T(8,128)(2,1)} %pad_maximum_fusion.2), channel_id=1, source_target_pairs={{0,1},{1,0},{2,3},{3,2},{4,5},{5,4},{6,7},{7,6},{8,9},{9,8},{10,11... | collective-permute-start | bytes 9437192 | tf_op jit(solution)/shard_map/ppermute | solution.py:45
  1069.8 416.6 %reduce-scatter.10.cloned.1.call-start = ((), (), s32[]{:S(2)}) async-start(), calls=%async_computation.10 | async-start | bytes 1081344
  1149.5 136.6 %collective-permute-start.53 = (bf16[2,2048,384]{2,1,0:T(8,128)(2,1)}, bf16[2,2048,384]{2,1,0:T(8,128)(2,1)}, u32[]{:S(2)}, u32[]{:S(2)}) collective-permute-start(bf16[2,2048,384]{2,1,0:T(8,128)(2,1)} %pad_maximum_fusion.1), channel_id=1, source_target_pairs={{0,1},{1,0},{2,3},{3,2},{4,5},{5,4},{6,7},{7,6},{8,9},{9,8},{10,11... | collective-permute-start | bytes 9437192 | tf_op jit(solution)/shard_map/ppermute | solution.py:45
  1163.9 109.4 %collective-permute-start.47 = (bf16[128,2560]{1,0:T(8,128)(2,1)}, bf16[128,2560]{1,0:T(8,128)(2,1)}, u32[]{:S(2)}, u32[]{:S(2)}) collective-permute-start(bf16[128,2560]{1,0:T(8,128)(2,1)} %get-tuple-element.109), channel_id=1, source_target_pairs={{0,2},{2,0},{4,6},{6,4},{8,10},{10,8},{12,14},{14,12},{16,18},{18,... | collective-permute-start | bytes 1966088 | tf_op jit(solution)/shard_map/ppermute | solution.py:110
  1165.4 110.2 %collective-permute-start.40 = (bf16[128,2560]{1,0:T(8,128)(2,1)}, bf16[128,2560]{1,0:T(8,128)(2,1)}, u32[]{:S(2)}, u32[]{:S(2)}) collective-permute-start(bf16[128,2560]{1,0:T(8,128)(2,1)} %get-tuple-element.104), channel_id=1, source_target_pairs={{0,8},{2,10},{8,16},{10,18},{16,24},{18,26},{24,28},{26,30},{28,20... | collective-permute-start | bytes 1966088 | tf_op jit(solution)/shard_map/ppermute | solution.py:116
  1171.5 104.1 %collective-permute-start.46 = (bf16[128,2560]{1,0:T(8,128)(2,1)}, bf16[128,2560]{1,0:T(8,128)(2,1)}, u32[]{:S(2)}, u32[]{:S(2)}) collective-permute-start(bf16[128,2560]{1,0:T(8,128)(2,1)} %get-tuple-element.105), channel_id=1, source_target_pairs={{8,0},{10,2},{16,8},{18,10},{24,16},{26,18},{28,24},{30,26},{20,28... | collective-permute-start | bytes 1966088 | tf_op jit(solution)/shard_map/ppermute | solution.py:120
  1273.3 69.3 %collective-permute-start.52 = (bf16[2,2048,384]{2,1,0:T(8,128)(2,1)}, bf16[2,2048,384]{2,1,0:T(8,128)(2,1)S(1)}, u32[]{:S(2)}, u32[]{:S(2)}) collective-permute-start(bf16[2,2048,384]{2,1,0:T(8,128)(2,1)} %pad_maximum_fusion), channel_id=1, source_target_pairs={{0,1},{1,0},{2,3},{3,2},{4,5},{5,4},{6,7},{7,6},{8,9},{9,8},{10,11... | collective-permute-start | bytes 9437192 | tf_op jit(solution)/shard_map/ppermute | solution.py:45
  1293.1 52.8 %collective-permute-start.51 = (bf16[128,2560]{1,0:T(8,128)(2,1)S(1)}, bf16[128,2560]{1,0:T(8,128)(2,1)S(1)}, u32[]{:S(2)}, u32[]{:S(2)}) collective-permute-start(bf16[128,2560]{1,0:T(8,128)(2,1)S(1)} %copy-done.45), channel_id=1, source_target_pairs={{0,2},{2,0},{4,6},{6,4},{8,10},{10,8},{12,14},{14,12},{16,18},{18,... | collective-permute-start | bytes 1966088 | tf_op jit(solution)/shard_map/ppermute | solution.py:110
  (134 other events, 3604.5 us)
Sparse Core Ops, SparseCore 0:
  10.9 91.0 all-gather.3
  104.1 89.4 all-gather.5
  231.0 124.2 all-gather.7
  762.1 198.0 reduce-scatter.5
  1070.0 109.1 reduce-scatter.7
  1350.5 135.8 reduce-scatter.9

commit v3 on v2

--- a/solution.py
+++ b/solution.py
@@ -1,3 +1,4 @@
+import functools
 import math
 
 import jax
@@ -271,6 +272,226 @@
         ),
         name="attend_back",
     )(pre, pre, pre, *tables, *gains, attended, grad_attended)
+
+
+TILE = 256
+PACK = 16
+GRANT = 60 * 1024 * 1024
+HELD = 20 * 1024 * 1024
+
+
+def pick_kernel(tiles, first, last, places_ref, rows_ref, out_ref, total):
+    e, j = pl.program_id(1), pl.program_id(2)
+
+    @pl.when(j < tiles[e])
+    def _():
+        total[...] = jnp.zeros_like(total)
+        at = e * pl.num_programs(2) + j
+        wanted = j * TILE + lax.broadcasted_iota(jnp.int32, (TILE, places_ref.shape[2]), 0)
+
+        def add(g, carry):
+            hits = jnp.where(places_ref[g] == wanted, 1.0, 0.0).astype(BF16)
+            total[...] += mm(hits, rows_ref[g])
+            return carry
+
+        lax.fori_loop(first[at], last[at] + 1, add, 0)
+        out_ref[...] = total[...].astype(BF16)
+
+    @pl.when(j >= tiles[e])
+    def _():
+        out_ref[...] = jnp.zeros_like(out_ref)
+
+
+def pick(plan, source, start, width):
+    experts, nodes, _, tokens = plan["places"].shape
+    count = plan["tile_count"]
+    cuts = 1
+    while 2 * nodes * tokens * (width // cuts) > HELD and width % (256 * cuts) == 0:
+        cuts *= 2
+    part = width // cuts
+    return pl.pallas_call(
+        pick_kernel,
+        grid_spec=pltpu.PrefetchScalarGridSpec(
+            num_scalar_prefetch=3,
+            grid=(cuts, experts, count),
+            in_specs=[
+                pl.BlockSpec((None, nodes, 1, tokens), lambda c, e, j, *_: (e, 0, 0, 0)),
+                pl.BlockSpec(
+                    (nodes, tokens, part),
+                    lambda c, e, j, *_: (0, 0, start // part + c),
+                    pipeline_mode=pl.Buffered(1),
+                ),
+            ],
+            out_specs=pl.BlockSpec((None, TILE, part), lambda c, e, j, *_: (e, j, c)),
+            scratch_shapes=[pltpu.VMEM((TILE, part), F32)],
+        ),
+        out_shape=jax.ShapeDtypeStruct((experts, count * TILE, width), BF16),
+        compiler_params=pltpu.CompilerParams(vmem_limit_bytes=GRANT),
+        cost_estimate=pl.CostEstimate(
+            flops=6 * experts * count * TILE * tokens * width,
+            bytes_accessed=2 * nodes * tokens * width + 2 * experts * count * TILE * width,
+            transcendentals=0,
+        ),
+        name="pick",
+    )(plan["tiles"], plan["first"], plan["last"], plan["places"], source)
+
+
+def expert_kernel(
+    tiles, base, arrived_ref, extra_ref, cots_ref, gate_ref, up_ref, down_ref,
+    weighed_ref, grad_gate_ref, grad_up_ref, produced_ref, back_ref, column_ref, *, expert_count,
+):
+    e, j = pl.program_id(0), pl.program_id(1)
+
+    @pl.when(j < tiles[e])
+    def _():
+        lane = lax.broadcasted_iota(jnp.int32, extra_ref.shape, 1)
+        own = base[0] + e
+        gates = jnp.where(
+            (lane == own) | (lane == own + expert_count), extra_ref[...].astype(F32), 0.0
+        )
+        gate_here = jnp.sum(gates, axis=-1, keepdims=True)
+        gate_pre = mm(arrived_ref[...], gate_ref[...])
+        up_pre = mm(arrived_ref[...], up_ref[...])
+        grad_plain = mm(cots_ref[...], down_ref[...], ((1,), (1,)))
+        sigmoid_gate = 1.0 / (1.0 + jnp.exp(-gate_pre))
+        activated = gate_pre * sigmoid_gate
+        hidden = activated * up_pre
+        column = jnp.sum(hidden * grad_plain, axis=-1, keepdims=True)
+        high = column.astype(BF16).astype(F32)
+        spot = lax.broadcasted_iota(jnp.int32, column_ref.shape, 1)
+        column_ref[...] = jnp.where(
+            spot == 2 * e, high, jnp.where(spot == 2 * e + 1, column - high, 0.0)
+        ).astype(BF16)
+        weighed = (hidden * gate_here).astype(BF16)
+        weighed_ref[...] = weighed
+        grad_hidden = grad_plain * gate_here
+        grad_gate = (
+            grad_hidden * up_pre * sigmoid_gate * (1.0 + gate_pre * (1.0 - sigmoid_gate))
+        ).astype(BF16)
+        grad_up = (grad_hidden * activated).astype(BF16)
+        grad_gate_ref[...] = grad_gate
+        grad_up_ref[...] = grad_up
+        produced_ref[...] = mm(weighed, down_ref[...]).astype(BF16)
+        back_ref[...] = (
+            mm(grad_gate, gate_ref[...], ((1,), (1,))) + mm(grad_up, up_ref[...], ((1,), (1,)))
+        ).astype(BF16)
+
+    @pl.when(j >= tiles[e])
+    def _():
+        for ref in (weighed_ref, grad_gate_ref, grad_up_ref, produced_ref, back_ref, column_ref):
+            ref[...] = jnp.zeros_like(ref)
+
+
+def run_experts(plan, base, arrived, extra, cots, gate, up, down, expert_count):
+    experts, height, width = arrived.shape
+    hidden = gate.shape[2]
+    count = plan["tile_count"]
+
+    def tile(size):
+        return pl.BlockSpec((None, TILE, size), lambda e, j, *_: (e, j, 0))
+
+    def whole(shape):
+        return pl.BlockSpec((None,) + shape, lambda e, j, *_: (e, 0, 0))
+
+    def out(size):
+        return jax.ShapeDtypeStruct((experts, height, size), BF16)
+
+    return pl.pallas_call(
+        functools.partial(expert_kernel, expert_count=expert_count),
+        grid_spec=pltpu.PrefetchScalarGridSpec(
+            num_scalar_prefetch=2,
+            grid=(experts, count),
+            in_specs=[
+                tile(width), tile(extra.shape[2]), tile(width),
+                whole((width, hidden)), whole((width, hidden)), whole((hidden, width)),
+            ],
+            out_specs=[tile(hidden)] * 3 + [tile(width)] * 2 + [tile(128)],
+        ),
+        out_shape=[out(hidden)] * 3 + [out(width)] * 2 + [out(128)],
+        compiler_params=pltpu.CompilerParams(vmem_limit_bytes=GRANT),
+        cost_estimate=pl.CostEstimate(
+            flops=6 * experts * height * width * hidden,
+            bytes_accessed=2 * experts * (4 * height * width + 3 * height * hidden),
+            transcendentals=experts * height * hidden // 2,
+        ),
+        name="run_experts",
+    )(plan["tiles"], base, arrived, extra, cots, gate, up, down)
+
+
+def spread_kernel(starts, places_ref, *refs):
+    g = pl.program_id(0)
+    half = len(refs) // 2
+    experts, nodes = places_ref.shape[0], pl.num_programs(0)
+    window = refs[-1]
+    size = window.shape[0]
+    totals = [None] * half
+    for e in range(experts):
+        start = pl.multiple_of(starts[e * nodes + g], PACK)
+        wanted = start + lax.broadcasted_iota(jnp.int32, (size, places_ref.shape[2]), 0)
+        hits = jnp.where(places_ref[e] == wanted, 1.0, 0.0).astype(BF16)
+        for i in range(half):
+            part = mm(hits, refs[i][e, pl.ds(start, size), :], ((0,), (0,)))
+            totals[i] = part if totals[i] is None else totals[i] + part
+    for i in range(half):
+        refs[half + i][...] = totals[i].astype(BF16)
+
+
+def spread(plan, sources):
+    experts, nodes, _, tokens = plan["places"].shape
+    window = plan["window"]
+    return pl.pallas_call(
+        spread_kernel,
+        grid_spec=pltpu.PrefetchScalarGridSpec(
+            num_scalar_prefetch=1,
+            grid=(nodes,),
+            in_specs=[pl.BlockSpec((experts, None, 1, tokens), lambda g, *_: (0, g, 0, 0))]
+            + [
+                pl.BlockSpec(source.shape, lambda g, *_: (0, 0, 0), pipeline_mode=pl.Buffered(1))
+                for source in sources
+            ],
+            out_specs=[
+                pl.BlockSpec((None, tokens, source.shape[2]), lambda g, *_: (g, 0, 0))
+                for source in sources
+            ],
+            scratch_shapes=[pltpu.VMEM((window, 128), BF16)],
+        ),
+        out_shape=[
+            jax.ShapeDtypeStruct((nodes, tokens, source.shape[2]), BF16) for source in sources
+        ],
+        compiler_params=pltpu.CompilerParams(vmem_limit_bytes=GRANT),
+        cost_estimate=pl.CostEstimate(
+            flops=2 * experts * nodes * tokens * window * sum(s.shape[2] for s in sources),
+            bytes_accessed=sum(4 * s.size for s in sources),
+            transcendentals=0,
+        ),
+        name="spread",
+    )(plan["starts"], plan["places"], *sources)
+
+
+def plan_places(member, slot, places):
+    nodes, _, _ = member.shape
+    counts = jnp.sum(member.astype(jnp.int32), axis=2)
+    earlier = jnp.arange(nodes)[:, None] > jnp.arange(nodes)[None, :]
+    offset = jnp.sum(jnp.where(earlier[:, :, None], counts[None], 0), axis=1)
+    totals = jnp.sum(counts, axis=0)
+    count = -(-(nodes * places) // TILE)
+    edges = jnp.arange(count, dtype=jnp.int32) * TILE
+    ends = offset + counts
+    first = jnp.sum((ends[:, :, None] <= edges).astype(jnp.int32), axis=0)
+    last = jnp.sum((offset[:, :, None] < edges + TILE).astype(jnp.int32), axis=0) - 1
+    window = -(-places // PACK) * PACK + PACK
+    window = min(window, count * TILE)
+    starts = jnp.minimum(offset // PACK * PACK, count * TILE - window)
+    packed = jnp.where(member, offset[:, :, None] + slot, -1)
+    return {
+        "places": jnp.moveaxis(packed, 1, 0)[:, :, None, :],
+        "tiles": (totals + TILE - 1) // TILE,
+        "first": jnp.minimum(first, nodes - 1).reshape(-1),
+        "last": jnp.minimum(last, nodes - 1).reshape(-1),
+        "starts": starts.T.reshape(-1),
+        "tile_count": count,
+        "window": window,
+    }
 
 
 def layer(
@@ -343,7 +564,6 @@
     )
     gate_full = gather_tp(gate_weight, 2)
     up_full = gather_tp(up_weight, 2)
-    down_full = gather_tp(down_weight, 1)
 
     own_routes = lax.dynamic_slice_in_dim(routes, part * local_length, local_length, axis=1)
     own_routes = own_routes.reshape(tokens, top_count)
@@ -354,8 +574,8 @@
     slot = jnp.einsum(
         "get,tu->geu", member.astype(BF16), before.astype(BF16), preferred_element_type=F32
     ).astype(jnp.int32)
-    slot = jnp.where(member, slot, -1)
-    placed = slot[:, :, None, :] == jnp.arange(places, dtype=jnp.int32)[None, None, :, None]
+    plan = plan_places(member, slot, places)
+    base = (node * local_experts).reshape(1).astype(jnp.int32)
 
     normed_rows, router_full, all_routes = lax.optimization_barrier(
         (normed_rows, router_full, all_routes)
@@ -373,17 +593,13 @@
         made["middle"] = input_wide + scatter_tp([projected[:, j] for j in range(tp_size)])
         return moving
 
-    def settle(moving):
-        made["middle"], moving = lax.optimization_barrier((made["middle"], moving))
-        return moving
-
-    cot_all = ring_gather(cot_low, (project, settle))
-    middle = made["middle"]
+    cot_all = ring_gather(cot_low, (project,))
+    middle, down_weight = lax.optimization_barrier((made["middle"], down_weight))
+    down_full = gather_tp(down_weight, 1)
     inverse_two = inverse_rms(middle)
     normed_two = middle * inverse_two
     expert_low = (normed_two * expert_gain).astype(BF16).reshape(tokens, model_width)
 
-    rows_all = lax.all_gather(expert_low, "fsdp", axis=0)
     logits = mm(expert_low, router_full)
     chosen = jnp.any(
         own_routes[:, :, None] == jnp.arange(expert_count, dtype=jnp.int32), axis=1
@@ -391,52 +607,29 @@
     top = jnp.max(jnp.where(chosen, logits, NEGATIVE), axis=-1, keepdims=True)
     powers = jnp.where(chosen, jnp.exp(jnp.minimum(logits - top, 0.0)), 0.0)
     gates = powers / jnp.sum(powers, axis=-1, keepdims=True)
-    gates_out = jnp.moveaxis(gates.reshape(tokens, nodes, local_experts), 1, 0)
-    own_gates = lax.all_to_all(gates_out, "fsdp", split_axis=0, concat_axis=0, tiled=True)
-    gate_of = jnp.sum(
-        jnp.where(placed, jnp.moveaxis(own_gates, 2, 1)[:, :, None, :], 0.0), axis=-1
-    )
-
-    out_total = None
-    grad_total = None
-    gate_columns = []
+    high = lax.reduce_precision(gates, 8, 7)
+    filler = jnp.zeros((tokens, -2 * expert_count % 128), BF16)
+    sent = jnp.concatenate(
+        [expert_low, high.astype(BF16), (gates - high).astype(BF16), filler], axis=1
+    )
+    rows_all = lax.all_gather(sent, "fsdp", axis=0)
+
+    arrived = pick(plan, rows_all, 0, model_width)
+    extra = pick(plan, rows_all, model_width, sent.shape[1] - model_width)
+    cots = pick(plan, cot_all, 0, model_width)
+    weighed, grad_gate_pre, grad_up_pre, produced, back, columns = run_experts(
+        plan, base, arrived, extra, cots, gate_full, up_full, down_full, expert_count
+    )
+    out_total = spread(plan, [produced])[0]
+    out_total, back = lax.optimization_barrier((out_total, back))
+    grad_total, columns = spread(plan, [back, columns])
     own_grads = []
     far_grads = []
     for e in range(local_experts):
-        spread = placed[:, e].astype(BF16)
-        gate_here = gate_of[:, e].reshape(nodes * places, 1)
-        arrived = jnp.einsum("gst,gtd->gsd", spread, rows_all, preferred_element_type=F32)
-        arrived = arrived.astype(BF16).reshape(nodes * places, model_width)
-        gate_pre = mm(arrived, gate_full[e])
-        up_pre = mm(arrived, up_full[e])
-        cots = jnp.einsum("gst,gtd->gsd", spread, cot_all, preferred_element_type=F32)
-        cots = cots.astype(BF16).reshape(nodes * places, model_width)
-        grad_plain = mm(cots, down_full[e], ((1,), (1,)))
-        sigmoid_gate = jax.nn.sigmoid(gate_pre)
-        activated = gate_pre * sigmoid_gate
-        hidden = activated * up_pre
-        gate_columns.append(jnp.sum(hidden * grad_plain, axis=-1).reshape(nodes, places))
-        grad_hidden = grad_plain * gate_here
-        grad_gate_pre = (
-            grad_hidden * up_pre * sigmoid_gate * (1.0 + gate_pre * (1.0 - sigmoid_gate))
-        ).astype(BF16)
-        grad_up_pre = (grad_hidden * activated).astype(BF16)
-        weighed = (hidden * gate_here).astype(BF16)
-        grad_places = (
-            mm(grad_gate_pre, gate_full[e], ((1,), (1,))) + mm(grad_up_pre, up_full[e], ((1,), (1,)))
-        ).astype(BF16).reshape(nodes, places, model_width)
-        produced = mm(weighed, down_full[e]).astype(BF16).reshape(nodes, places, model_width)
-        out_here = jnp.einsum("gst,gsd->gtd", spread, produced, preferred_element_type=F32)
-        grad_here = jnp.einsum("gst,gsd->gtd", spread, grad_places, preferred_element_type=F32)
-        if out_total is not None:
-            out_here = out_here + out_total.astype(F32)
-            grad_here = grad_here + grad_total.astype(F32)
-        out_total = out_here.astype(BF16)
-        grad_total = grad_here.astype(BF16)
         grads = (
-            mm(arrived, grad_gate_pre, ((0,), (0,))),
-            mm(arrived, grad_up_pre, ((0,), (0,))),
-            mm(weighed, cots, ((0,), (0,))),
+            mm(arrived[e], grad_gate_pre[e], ((0,), (0,))),
+            mm(arrived[e], grad_up_pre[e], ((0,), (0,))),
+            mm(weighed[e], cots[e], ((0,), (0,))),
         )
         own_grads.append(
             (grads[0][:, :half_hidden], grads[1][:, :half_hidden], grads[2][:half_hidden])
@@ -452,10 +645,8 @@
             ]
         )
 
-    column = jnp.sum(
-        jnp.where(placed, jnp.stack(gate_columns, axis=1)[:, :, :, None], 0.0), axis=2
-    )
-    column = jnp.moveaxis(column, 1, 2)
+    pairs = columns[:, :, : 2 * local_experts].astype(F32).reshape(nodes, tokens, local_experts, 2)
+    column = jnp.sum(pairs, axis=-1)
     grad_gate = lax.all_to_all(column, "fsdp", split_axis=0, concat_axis=0, tiled=True)
     grad_gate = jnp.moveaxis(grad_gate, 0, 1).reshape(tokens, expert_count)
 
@@ -476,7 +667,7 @@
     grad_flat = gather_tp(grad_middle.astype(BF16), 1).reshape(every, model_width)
     grad_attended = mm(grad_flat, output_full).astype(BF16)
     output_low = mm(grad_flat, attended, ((0,), (0,))).astype(BF16)
-    output_low, expert_part = lax.optimization_barrier((output_low, expert_part))
+    output_low, grad_attended = lax.optimization_barrier((output_low, grad_attended))
     output_part = lax.psum_scatter(output_low, "fsdp", scatter_dimension=0, tiled=True)
     grad_pre, query_gain_part, key_gain_part = attend_back(
         pre, tables, gains, attended, grad_attended, rows, heads, kv_heads
@@ -484,34 +675,63 @@
     qkv_low = mm(normed_rows, grad_pre, ((0,), (0,))).astype(BF16)
     qkv_grad = ring_scatter(qkv_low.reshape(nodes, -1, qkv_low.shape[1]))
     qkv_grad = qkv_grad.reshape(query_weight.shape[0], -1)
+    grad_normed = mm(grad_pre, qkv_full, ((1,), (1,))).reshape(rows, tp_size, local_length, model_width)
+    grad_one = scatter_tp([grad_normed[:, j] for j in range(tp_size)])
+    attention_gain_part = jnp.sum(grad_one * normed_one, axis=(0, 1))
+    input_grad = grad_middle + norm_backward(grad_one, attention_gain, normed_one, inverse_one)
+
+    moved = []
+    for kind in range(3):
+        for j in range(1, tp_size):
+            far = jnp.stack([far_grads[e][j - 1][kind] for e in range(local_experts)])
+            moved.append(lax.ppermute(far, "tp", [(s, (s + j) % tp_size) for s in range(tp_size)]))
+    moved, qkv_grad = lax.optimization_barrier((moved, qkv_grad))
+    weight_grads = []
+    for kind in range(3):
+        total = jnp.stack([own_grads[e][kind] for e in range(local_experts)])
+        for j in range(tp_size - 1):
+            total = total + moved[kind * (tp_size - 1) + j].astype(F32)
+        weight_grads.append(total)
+    gate_grad, up_grad, down_grad = weight_grads
     query_width, key_width = query_weight.shape[1], key_weight.shape[1]
     query_grad = qkv_grad[:, :query_width]
     key_grad = qkv_grad[:, query_width : query_width + key_width]
     value_grad = qkv_grad[:, query_width + key_width :]
-    grad_normed = mm(grad_pre, qkv_full, ((1,), (1,))).reshape(rows, tp_size, local_length, model_width)
-    grad_one = scatter_tp([grad_normed[:, j] for j in range(tp_size)])
-    attention_gain_part = jnp.sum(grad_one * normed_one, axis=(0, 1))
-    input_grad = grad_middle + norm_backward(grad_one, attention_gain, normed_one, inverse_one)
-
-    weight_grads = []
-    for kind in range(3):
-        mine = jnp.stack([own_grads[e][kind] for e in range(local_experts)])
-        far = [
-            jnp.stack([far_grads[e][j][kind] for e in range(local_experts)])
-            for j in range(tp_size - 1)
-        ]
-        weight_grads.append(scatter_tp([mine] + far))
-    gate_grad, up_grad, down_grad = weight_grads
 
     layer_output = (middle + expert_part.reshape(middle.shape).astype(F32)).astype(BF16)
-    router_part, output_part = lax.optimization_barrier((router_part, output_part))
-    router_grad = lax.psum_scatter(router_part, ("fsdp", "tp"), scatter_dimension=0, tiled=True)
     output_grad = output_part.astype(F32)
-    small = [
-        lax.psum_scatter(value.reshape(-1), ("fsdp", "tp"), scatter_dimension=0, tiled=True)
-        for value in (attention_gain_part, expert_gain_part, query_gain_part, key_gain_part)
+
+    kept = [
+        value.reshape(nodes, tp_size, -1)
+        for value in (
+            router_part,
+            attention_gain_part,
+            expert_gain_part,
+            query_gain_part,
+            key_gain_part,
+        )
     ]
-    attention_gain_grad, expert_gain_grad, query_gain_grad, key_gain_grad = small
+    sizes = [value.shape[2] for value in kept]
+    shares = jnp.concatenate(kept, axis=2)
+    shares = jnp.pad(shares, ((0, 0), (0, 0), (0, -shares.shape[2] % 128)))
+    shares = lax.all_to_all(
+        shares.reshape(nodes, tp_size, -1, 128), "fsdp", split_axis=0, concat_axis=0, tiled=True
+    )
+    shares = jnp.sum(shares, axis=0)
+    mine = jnp.zeros(shares.shape[1:], F32)
+    for j in range(tp_size):
+        share = lax.dynamic_index_in_dim(shares, (part + j) % tp_size, 0, keepdims=False)
+        if j > 0:
+            share = lax.ppermute(share, "tp", [(s, (s + j) % tp_size) for s in range(tp_size)])
+        mine = mine + share
+    mine = mine.reshape(-1)
+    small = []
+    at = 0
+    for size in sizes:
+        small.append(mine[at : at + size])
+        at += size
+    router_grad = small[0].reshape(-1, expert_count)
+    attention_gain_grad, expert_gain_grad, query_gain_grad, key_gain_grad = small[1:]
     return (
         layer_output,
         input_grad,

time: 1500 us -> 1270 us (0.85)
  matrix products: 424 us -> 131 us
  Pallas kernels: 70 us -> 277 us
  blocking collectives: 139 us -> 41.3 us
  waiting for transfers between devices: 570 us -> 537 us
    pallas_call x0 -> x6, Pallas kernels: none -> 207 us  [the longest x3 81.7 us: pick(): pl.pallas_call(pick_kernel, grid_spec=pltpu.PrefetchScalarGridSpec(num_sc...]
    dot_general x27 -> x15, matrix products: 320 us -> 131 us  [mm(): return lax.dot_general(a, b, (dims, ((), ())), preferred_element_type=F32)]
    ppermute x0 -> x4, waiting for transfers between devices: none -> 158 us  [the longest x1 158 us: layer(): lax.ppermute(share, 'tp', [(s, (s + j) % tp_size) for s in range(tp_size)])]
    unnamed x7 -> x5, waiting for transfers between devices: 130 us -> 1.28 us
    dot_general x8 -> x0, matrix products: 104 us -> none  [the longest x2 28.6 us: layer(): jnp.einsum('gst,gsd->gtd', spread, produced, preferred_element_type=F32)]
    unnamed x1 -> x0, blocking collectives: 96.3 us -> none
    ppermute x5, waiting for transfers between devices: 188 us -> 131 us  [fetch_next(): lax.ppermute(values, 'tp', [(s, (s - step) % size) for s in range(size)])]
    ppermute x5 -> x2, waiting for transfers between devices: 57.9 us -> 24 us  [scatter_tp(): lax.ppermute(pieces[j].astype(BF16), 'tp', [(s, (s + j) % size) for s in...]
  transfers between devices with their start and end apart: 63 -> 63, of which waited for: 22 -> 22; matrix products, arithmetic and copies ran while one was open for 25% -> 21% of each run, Pallas kernels for 5% -> 8%
where the time goes in v3:
time: 1270 us; the launch traced here: 1260 us
  waiting for transfers between devices  537 us (42%)
  Pallas kernels  277 us (22%)
  matrix products  131 us (10%)
  other arithmetic  99.5 us (8%)
  local copies, waits for them, and re-layouts  93.8 us (7%)
  starting transfers between devices  52.6 us (4%)
  blocking collectives  41.3 us (3%)
  between operations  29.6 us (2%)
    ppermute x1, waiting for transfers between devices, layer(): lax.ppermute(share, 'tp', [(s, (s + j) % tp_size) for s in range(tp_size)])  158 us
    ppermute x5, waiting for transfers between devices, fetch_next(): lax.ppermute(values, 'tp', [(s, (s - step) % size) for s in range(size)])  131 us
    dot_general x15, matrix products, mm(): return lax.dot_general(a, b, (dims, ((), ())), preferred_element_type=F32)  131 us
    pallas_call x3, Pallas kernels, pick(): pl.pallas_call(pick_kernel, grid_spec=pltpu.PrefetchScalarGridSpec(num_sc...  81.7 us
    pallas_call x1, Pallas kernels, run_experts(): pl.pallas_call(functools.partial(expert_kernel, expert_count=expert_count...  79.3 us
    ppermute x8, waiting for transfers between devices, ring_scatter(): rising = lax.ppermute(rising, 'fsdp', up).astype(F32)  73.6 us
    ppermute x4, waiting for transfers between devices, ring_gather(): behind = lax.ppermute(behind, 'fsdp', up)  54.1 us
    pallas_call x2, Pallas kernels, spread(): pl.pallas_call(spread_kernel, grid_spec=pltpu.PrefetchScalarGridSpec(num_...  45.8 us
  transfers between devices with their start and end apart: 63, of which 22 were waited for; matrix products, arithmetic and copies ran while one was open for 21% of the time, Pallas kernels for 8%

profile of v3, /device:TPU:0, one launch (start us, length us, event | category | flops | bytes accessed | tf_op | source)
XLA Modules:
  0.0 1261.6 jit_solution(9109358933933428218)
XLA Ops:
  14.0 22.9 %all_gather.18 = bf16[2048,32]{0,1:T(8,128)(2,1)S(1)} all-gather(bf16[128,32]{0,1:T(8,128)(2,1)S(1)} %copy-done.50), channel_id=1, replica_groups=mesh['fsdp'=16,'tp'=2] {'fsdp'}, dimensions={0}, use_global_device_ids=true | all-gather | bytes 139264 | tf_op jit(solution)/shard_map/all_gather | solution.py:541
  36.9 18.4 %all_gather.19 = s32[16,256,8]{1,2,0:T(8,128)S(1)} all-gather(s32[1,256,8]{1,2,0:T(8,128)S(1)} %constant_dynamic-slice_fusion.4), channel_id=1, replica_groups=mesh['fsdp'=16,'tp'=2] {'fsdp'}, dimensions={0}, use_global_device_ids=true | all-gather | bytes 139264 | tf_op jit(solution)/shard_map/all_gather | solution.py:570
  57.0 44.9 %all-gather.5.cloned.1.call-done = bf16[2048,2560]{1,0:T(8,128)(2,1)} async-done(((bf16[128,2560]{1,0:T(8,128)(2,1)}), bf16[2048,2560]{1,0:T(8,128)(2,1)}) %all-gather.5.cloned.1.call-update) | async-done | bytes 10485776 | tf_op jit(solution)/shard_map/all_gather | solution.py:532
  118.4 28.6 %attend.1.att_ref = bf16[512,2048]{1,0:T(8,128)(2,1)} custom-call(f32[512,2560]{1,0:T(8,128)} %fusion.86.q_ref.k_ref.v_ref, f32[512,2560]{1,0:T(8,128)} %fusion.86.q_ref.k_ref.v_ref, f32[512,2560]{1,0:T(8,128)} %fusion.86.q_ref.k_ref.v_ref, f32[512,128]{1,0:T(8,128)} %maximum_bitcast_fusion.4.cos_ref, f32[512,128]{1,0:T(8,128)} %maximum_bitcast_fusion.5.sin_ref, ...), custom_call_target="tpu_custom_call" | custom-call | flops 2147483648 | bytes 7864320 | tf_op jit(solution)/shard_map/attend/pallas_call | solution.py:235
  152.7 40.9 %all-gather.7.cloned.1.call-done = bf16[2048,2048]{1,0:T(8,128)(2,1)} async-done(((bf16[128,2048]{1,0:T(8,128)(2,1)}), bf16[2048,2048]{1,0:T(8,128)(2,1)}) %all-gather.7.cloned.1.call-update) | async-done | bytes 8388624 | tf_op jit(solution)/shard_map/all_gather | solution.py:540
  206.0 24.0 %collective-permute-done.3 = bf16[1,256,2048]{2,1,0:T(8,128)(2,1)} collective-permute-done((bf16[1,256,2048]{2,1,0:T(8,128)(2,1)}, bf16[1,256,2048]{2,1,0:T(8,128)(2,1)}, u32[]{:S(2)}, u32[]{:S(2)}) %collective-permute-start.3) | collective-permute-done | bytes 1048608 | tf_op jit(solution)/shard_map/ppermute | solution.py:46
  259.3 48.7 %collective-permute-done.17 = bf16[2,2048,384]{2,1,0:T(8,128)(2,1)} collective-permute-done((bf16[2,2048,384]{2,1,0:T(8,128)(2,1)}, bf16[2,2048,384]{2,1,0:T(8,128)(2,1)}, u32[]{:S(2)}, u32[]{:S(2)}) %collective-permute-start.17) | collective-permute-done | bytes 3145760 | tf_op jit(solution)/shard_map/ppermute | solution.py:34
  314.1 59.8 %collective-permute-done.18 = bf16[2,2048,384]{2,1,0:T(8,128)(2,1)} collective-permute-done((bf16[2,2048,384]{2,1,0:T(8,128)(2,1)}, bf16[2,2048,384]{2,1,0:T(8,128)(2,1)}, u32[]{:S(2)}, u32[]{:S(2)}) %collective-permute-start.18) | collective-permute-done | bytes 3145760 | tf_op jit(solution)/shard_map/ppermute | solution.py:34
  411.1 19.2 %collective-permute-done.11 = bf16[256,2048]{1,0:T(8,128)(2,1)S(1)} collective-permute-done((bf16[256,2048]{1,0:T(8,128)(2,1)S(1)}, bf16[256,2048]{1,0:T(8,128)(2,1)S(1)}, u32[]{:S(2)}, u32[]{:S(2)}) %collective-permute-start.11) | collective-permute-done | bytes 1048608 | tf_op jit(solution)/shard_map/ppermute | solution.py:90
  436.4 19.7 %collective-permute-done.15 = bf16[256,2048]{1,0:T(8,128)(2,1)S(1)} collective-permute-done((bf16[256,2048]{1,0:T(8,128)(2,1)S(1)}, bf16[256,2048]{1,0:T(8,128)(2,1)S(1)}, u32[]{:S(2)}, u32[]{:S(2)}) %collective-permute-start.15) | collective-permute-done | bytes 1048608 | tf_op jit(solution)/shard_map/ppermute | solution.py:90
  467.1 33.9 %pick.5.cots_ref = bf16[2,2560,2048]{2,1,0:T(8,128)(2,1)} custom-call(s32[2]{0:T(128)} %and_select_fusion.1.tiles, s32[20]{0:T(128)} %min.30.first, s32[20]{0:T(128)} %min.32.last, s32[2,16,1,256]{3,2,1,0:T(1,128)} %broadcast_in_dim.136.places_ref, bf16[16,256,2048]{2,1,0:T(8,128)(2,1)} %bitcast_dynamic-update-slice_fusion.rows_ref), custom_call_target="tpu_custom_call" | custom-call | flops 16106127360 | bytes 37748736 | tf_op jit(solution)/shard_map/pick/pallas_call | solution.py:312
  501.0 33.8 %pick.3.arrived_ref = bf16[2,2560,2048]{2,1,0:T(8,128)(2,1)} custom-call(s32[2]{0:T(128)} %and_select_fusion.1.tiles, s32[20]{0:T(128)} %min.30.first, s32[20]{0:T(128)} %min.32.last, s32[2,16,1,256]{3,2,1,0:T(1,128)} %broadcast_in_dim.136.places_ref, bf16[16,256,2176]{2,1,0:T(8,128)(2,1)} %bitcast.285), custom_call_target="tpu_custom_call" | custom-call | flops 16106127360 | bytes 37748736 | tf_op jit(solution)/shard_map/pick/pallas_call | solution.py:312
  534.9 13.9 %pick.4.extra_ref = bf16[2,2560,128]{2,1,0:T(8,128)(2,1)} custom-call(s32[2]{0:T(128)} %and_select_fusion.1.tiles, s32[20]{0:T(128)} %min.30.first, s32[20]{0:T(128)} %min.32.last, s32[2,16,1,256]{3,2,1,0:T(1,128)} %broadcast_in_dim.136.places_ref, bf16[16,256,2176]{2,1,0:T(8,128)(2,1)} %bitcast.286), custom_call_target="tpu_custom_call" | custom-call | flops 1006632960 | bytes 2359296 | tf_op jit(solution)/shard_map/pick/pallas_call | solution.py:312
  548.7 79.3 %run_experts.1 = (bf16[2,2560,768]{2,1,0:T(8,128)(2,1)}, bf16[2,2560,768]{2,1,0:T(8,128)(2,1)}, bf16[2,2560,768]{2,1,0:T(8,128)(2,1)}, bf16[2,2560,2048]{2,1,0:T...) custom-call(s32[2]{0:T(128)} %and_select_fusion.1.tiles, s32[1]{0:T(128)} %bitcast.15.base, ...), custom_call_target="tpu_custom_call" | custom-call | flops 48318382080 | bytes 107479040 | tf_op jit(solution)/shard_map/run_experts/pallas_call | solution.py:399
  628.1 22.3 %spread.2 = bf16[16,256,2048]{2,1,0:T(8,128)(2,1)} custom-call(s32[32]{0:T(128)} %reshape.784.starts, s32[2,16,1,256]{3,2,1,0:T(1,128)} %broadcast_in_dim.136.places_ref, bf16[2,2560,2048]{2,1,0:T(8,128)(2,1)} %get-tuple-element.66.refs_0_), custom_call_target="tpu_custom_call" | custom-call | flops 5905580032 | bytes 41943040 | tf_op jit(solution)/shard_map/spread/pallas_call | solution.py:442
  650.4 23.5 %spread.3 = (bf16[16,256,2048]{2,1,0:T(8,128)(2,1)}, bf16[16,256,128]{2,1,0:T(8,128)(2,1)}) custom-call(s32[32]{0:T(128)} %reshape.784.starts, s32[2,16,1,256]{3,2,1,0:T(1,128)} %broadcast_in_dim.136.places_ref, bf16[2,2560,2048]{2,1,0:T(8,128)(2,1)} %get-tuple-element.69.refs_0_, bf16[2,2560,128]{2,1,0:T(8,128)(2,1)} %get-tuple-element.70.refs_1_), custom_call_target="tpu_custom_call" | custom-call | flops 6274678784 | bytes 44564480 | tf_op jit(solution)/shard_map/spread/pallas_call | solution.py:442
  682.5 13.6 %fusion.3 = f32[2048,768]{1,0:T(8,128)} fusion(bf16[2,2560,2048]{2,1,0:T(8,128)(2,1)} %pick.3.arrived_ref, bf16[2,2560,768]{2,1,0:T(8,128)(2,1)S(1)} %copy-done.57), kind=kOutput, calls=%fused_computation.8 | convolution fusion | flops 8053063680 | bytes 20709376 | tf_op jit(solution)/shard_map/dot_general | solution.py:29
  722.9 12.7 %fusion.2 = f32[2048,768]{1,0:T(8,128)S(1)} fusion(bf16[2,2560,2048]{2,1,0:T(8,128)(2,1)} %pick.3.arrived_ref, bf16[2,2560,768]{2,1,0:T(8,128)(2,1)} %get-tuple-element.73), kind=kOutput, calls=%fused_computation.7 | convolution fusion | flops 8053063680 | bytes 20709376 | tf_op jit(solution)/shard_map/dot_general | solution.py:29
  812.3 14.0 %fusion = f32[768,2048]{1,0:T(8,128)} fusion(bf16[2,2560,2048]{2,1,0:T(8,128)(2,1)} %pick.5.cots_ref, bf16[2,2560,768]{2,1,0:T(8,128)(2,1)} %get-tuple-element.74), kind=kOutput, calls=%fused_computation.2 | convolution fusion | flops 8053063680 | bytes 20709376 | tf_op jit(solution)/shard_map/dot_general | solution.py:29
  844.6 20.5 %collective-permute-done.35 = bf16[1,256,2048]{2,1,0:T(8,128)(2,1)S(1)} collective-permute-done((bf16[1,256,2048]{2,1,0:T(8,128)(2,1)S(1)}, bf16[1,256,2048]{2,1,0:T(8,128)(2,1)S(1)}, u32[]{:S(2)}, u32[]{:S(2)}) %collective-permute-start.35) | collective-permute-done | bytes 1048608 | tf_op jit(solution)/shard_map/ppermute | solution.py:34
  899.7 41.4 %attend_back.1 = (bf16[512,2560]{1,0:T(8,128)(2,1)}, f32[1,128]{1,0:T(1,128)}, f32[1,128]{1,0:T(1,128)}) custom-call(f32[512,2560]{1,0:T(8,128)} %fusion.86.q_ref.k_ref.v_ref, f32[512,2560]{1,0:T(8,128)} %fusion.86.q_ref.k_ref.v_ref, f32[512,2560]{1,0:T(8,128)} %fusion.86.q_ref.k_ref.v_ref, f32[512,128]{1,0:T(8,128)} %maximum_bitcast_fusion.4.cos_ref, ...), custom_call_target="tpu_custom_call" | custom-call | flops 5368709120 | bytes 13107200 | tf_op jit(solution)/shard_map/attend_back/pallas_call | solution.py:263
  976.8 18.2 %collective-permute-done.42 = bf16[128,2560]{1,0:T(8,128)(2,1)S(1)} collective-permute-done((bf16[128,2560]{1,0:T(8,128)(2,1)S(1)}, bf16[128,2560]{1,0:T(8,128)(2,1)S(1)}, u32[]{:S(2)}, u32[]{:S(2)}) %collective-permute-start.42) | collective-permute-done | bytes 655392 | tf_op jit(solution)/shard_map/ppermute | solution.py:117
  1052.7 158.2 %collective-permute-done.37 = f32[18,128]{1,0:T(8,128)S(1)} collective-permute-done((f32[18,128]{1,0:T(8,128)S(1)}, f32[18,128]{1,0:T(8,128)S(1)}, u32[]{:S(2)}, u32[]{:S(2)}) %collective-permute-start.37) | collective-permute-done | bytes 9248 | tf_op jit(solution)/shard_map/ppermute | solution.py:725
  1213.2 13.7 %collective-permute-done.48 = bf16[128,2560]{1,0:T(8,128)(2,1)} collective-permute-done((bf16[128,2560]{1,0:T(8,128)(2,1)}, bf16[128,2560]{1,0:T(8,128)(2,1)}, u32[]{:S(2)}, u32[]{:S(2)}) %collective-permute-start.48) | collective-permute-done | bytes 655392 | tf_op jit(solution)/shard_map/ppermute | solution.py:117
  (396 shorter events, 405.8 us)
Async XLA Ops:
  7.2 94.7 %all-gather.5.cloned.1.call-start = ((), (), s32[]{:S(2)}) async-start(), calls=%async_computation.4 | async-start | bytes 11141120 | tf_op jit(solution)/shard_map/all_gather | solution.py:532
  9.4 184.2 %all-gather.7.cloned.1.call-start = ((), (), s32[]{:S(2)}) async-start(), calls=%async_computation.5 | async-start | bytes 8912896 | tf_op jit(solution)/shard_map/all_gather | solution.py:540
  10.1 490.9 %all-gather.9.cloned.1.call-start = ((), (), s32[]{:S(2)}) async-start(), calls=%async_computation.8 | async-start | bytes 18939904 | tf_op jit(solution)/shard_map/all_gather | solution.py:615
  11.1 44.5 %collective-permute-start = (bf16[1,256,2048]{2,1,0:T(8,128)(2,1)S(1)}, bf16[1,256,2048]{2,1,0:T(8,128)(2,1)S(1)}, u32[]{:S(2)}, u32[]{:S(2)}) collective-permute-start(bf16[1,256,2048]{2,1,0:T(8,128)(2,1)S(1)} %fusion.22), channel_id=1, source_target_pairs={{0,1},{1,0},{2,3},{3,2},{4,5},{5,4},{6,7},{7,6},{8,9},{9,8},{10,11... | collective-permute-start | bytes 3145736 | tf_op jit(solution)/shard_map/ppermute | solution.py:34
  112.4 38.2 %collective-permute-start.1 = (bf16[256,2048]{1,0:T(8,128)(2,1)S(1)}, bf16[256,2048]{1,0:T(8,128)(2,1)}, u32[]{:S(2)}, u32[]{:S(2)}) collective-permute-start(bf16[256,2048]{1,0:T(8,128)(2,1)S(1)} %bitcast.293), channel_id=1, source_target_pairs={{0,8},{2,10},{8,16},{10,18},{16,24},{18,26},{24,28},{26,30},{28,20... | collective-permute-start | bytes 3145736 | tf_op jit(solution)/shard_map/ppermute | solution.py:90
  113.1 39.6 %collective-permute-start.2 = (bf16[256,2048]{1,0:T(8,128)(2,1)S(1)}, bf16[256,2048]{1,0:T(8,128)(2,1)S(1)}, u32[]{:S(2)}, u32[]{:S(2)}) collective-permute-start(bf16[256,2048]{1,0:T(8,128)(2,1)S(1)} %bitcast.294), channel_id=1, source_target_pairs={{8,0},{10,2},{16,8},{18,10},{24,16},{26,18},{28,24},{30,26},{20,28... | collective-permute-start | bytes 3145736 | tf_op jit(solution)/shard_map/ppermute | solution.py:92
  236.7 71.4 %collective-permute-start.17 = (bf16[2,2048,384]{2,1,0:T(8,128)(2,1)}, bf16[2,2048,384]{2,1,0:T(8,128)(2,1)}, u32[]{:S(2)}, u32[]{:S(2)}) collective-permute-start(bf16[2,2048,384]{2,1,0:T(8,128)(2,1)} %param.122), channel_id=1, source_target_pairs={{0,1},{1,0},{2,3},{3,2},{4,5},{5,4},{6,7},{7,6},{8,9},{9,8},{10,11... | collective-permute-start | bytes 9437192 | tf_op jit(solution)/shard_map/ppermute | solution.py:34
  238.2 135.7 %collective-permute-start.18 = (bf16[2,2048,384]{2,1,0:T(8,128)(2,1)}, bf16[2,2048,384]{2,1,0:T(8,128)(2,1)}, u32[]{:S(2)}, u32[]{:S(2)}) collective-permute-start(bf16[2,2048,384]{2,1,0:T(8,128)(2,1)} %param.123), channel_id=1, source_target_pairs={{0,1},{1,0},{2,3},{3,2},{4,5},{5,4},{6,7},{7,6},{8,9},{9,8},{10,11... | collective-permute-start | bytes 9437192 | tf_op jit(solution)/shard_map/ppermute | solution.py:34
  259.3 128.8 %collective-permute-start.4 = (bf16[256,2048]{1,0:T(8,128)(2,1)S(1)}, bf16[256,2048]{1,0:T(8,128)(2,1)S(1)}, u32[]{:S(2)}, u32[]{:S(2)}) collective-permute-start(bf16[256,2048]{1,0:T(8,128)(2,1)S(1)} %bitcast.295), channel_id=1, source_target_pairs={{0,2},{2,0},{4,6},{6,4},{8,10},{10,8},{12,14},{14,12},{16,18},{18,... | collective-permute-start | bytes 3145736 | tf_op jit(solution)/shard_map/ppermute | solution.py:82
  391.6 70.5 %collective-permute-start.19 = (bf16[2,384,2048]{2,1,0:T(8,128)(2,1)S(1)}, bf16[2,384,2048]{2,1,0:T(8,128)(2,1)S(1)}, u32[]{:S(2)}, u32[]{:S(2)}) collective-permute-start(bf16[2,384,2048]{2,1,0:T(8,128)(2,1)S(1)} %copy-done.29), channel_id=1, source_target_pairs={{0,1},{1,0},{2,3},{3,2},{4,5},{5,4},{6,7},{7,6},{8,9},{9,8},{10,11... | collective-permute-start | bytes 9437192 | tf_op jit(solution)/shard_map/ppermute | solution.py:34
  681.4 157.2 %collective-permute-start.34 = (bf16[256,2048]{1,0:T(8,128)(2,1)}, bf16[256,2048]{1,0:T(8,128)(2,1)S(1)}, u32[]{:S(2)}, u32[]{:S(2)}) collective-permute-start(bf16[256,2048]{1,0:T(8,128)(2,1)} %get-tuple-element.191), channel_id=1, source_target_pairs={{0,2},{2,0},{4,6},{6,4},{8,10},{10,8},{12,14},{14,12},{16,18},{18,... | collective-permute-start | bytes 3145736 | tf_op jit(solution)/shard_map/ppermute | solution.py:111
  681.4 83.0 %collective-permute-start.24 = (bf16[256,2048]{1,0:T(8,128)(2,1)}, bf16[256,2048]{1,0:T(8,128)(2,1)}, u32[]{:S(2)}, u32[]{:S(2)}) collective-permute-start(bf16[256,2048]{1,0:T(8,128)(2,1)} %get-tuple-element.196), channel_id=1, source_target_pairs={{0,2},{2,0},{4,6},{6,4},{8,10},{10,8},{12,14},{14,12},{16,18},{18,... | collective-permute-start | bytes 3145736 | tf_op jit(solution)/shard_map/ppermute | solution.py:111
  682.0 53.7 %collective-permute-start.22 = (bf16[256,2048]{1,0:T(8,128)(2,1)}, bf16[256,2048]{1,0:T(8,128)(2,1)}, u32[]{:S(2)}, u32[]{:S(2)}) collective-permute-start(bf16[256,2048]{1,0:T(8,128)(2,1)} %get-tuple-element.197), channel_id=1, source_target_pairs={{0,2},{2,0},{4,6},{6,4},{8,10},{10,8},{12,14},{14,12},{16,18},{18,... | collective-permute-start | bytes 3145736 | tf_op jit(solution)/shard_map/ppermute | solution.py:111
  682.5 53.3 %collective-permute-start.28 = (bf16[256,2048]{1,0:T(8,128)(2,1)}, bf16[256,2048]{1,0:T(8,128)(2,1)}, u32[]{:S(2)}, u32[]{:S(2)}) collective-permute-start(bf16[256,2048]{1,0:T(8,128)(2,1)} %get-tuple-element.194), channel_id=1, source_target_pairs={{0,2},{2,0},{4,6},{6,4},{8,10},{10,8},{12,14},{14,12},{16,18},{18,... | collective-permute-start | bytes 3145736 | tf_op jit(solution)/shard_map/ppermute | solution.py:111
  697.6 140.6 %all-to-all-start = ((f32[16,256,2]{1,2,0:T(2,128)}), f32[16,256,2]{1,2,0:T(2,128)S(1)}, u32[]{:S(2)}, u32[]{:S(2)}) async-start(f32[16,256,2]{1,2,0:T(2,128)} %copy.216), calls=%async_computation.1 | async-start | bytes 65536 | tf_op jit(solution)/shard_map/all_to_all | solution.py:650
  704.8 541.9 %reduce-scatter.5.cloned.1.call-start = ((), (), s32[]{:S(2)}) async-start(), calls=%async_computation.7 | async-start | bytes 8912896 | tf_op jit(solution)/shard_map/reduce_scatter | solution.py:671
  882.6 366.3 %reduce-scatter.3.cloned.1.call-start = ((), (), s32[]{:S(2)}) async-start(), calls=%async_computation.6 | async-start | bytes 17825792 | tf_op jit(solution)/shard_map/reduce_scatter | solution.py:654
  976.3 40.5 %collective-permute-start.45 = (bf16[128,2560]{1,0:T(8,128)(2,1)}, bf16[128,2560]{1,0:T(8,128)(2,1)}, u32[]{:S(2)}, u32[]{:S(2)}) collective-permute-start(bf16[128,2560]{1,0:T(8,128)(2,1)} %get-tuple-element.210), channel_id=1, source_target_pairs={{0,2},{2,0},{4,6},{6,4},{8,10},{10,8},{12,14},{14,12},{16,18},{18,... | collective-permute-start | bytes 1966088 | tf_op jit(solution)/shard_map/ppermute | solution.py:111
  976.3 41.6 %collective-permute-start.51 = (bf16[128,2560]{1,0:T(8,128)(2,1)}, bf16[128,2560]{1,0:T(8,128)(2,1)}, u32[]{:S(2)}, u32[]{:S(2)}) collective-permute-start(bf16[128,2560]{1,0:T(8,128)(2,1)} %get-tuple-element.207), channel_id=1, source_target_pairs={{0,2},{2,0},{4,6},{6,4},{8,10},{10,8},{12,14},{14,12},{16,18},{18,... | collective-permute-start | bytes 1966088 | tf_op jit(solution)/shard_map/ppermute | solution.py:111
  1005.8 223.1 %collective-permute-start.38 = (bf16[2,2048,384]{2,1,0:T(8,128)(2,1)}, bf16[2,2048,384]{2,1,0:T(8,128)(2,1)}, u32[]{:S(2)}, u32[]{:S(2)}) collective-permute-start(bf16[2,2048,384]{2,1,0:T(8,128)(2,1)} %pad_maximum_fusion.3), channel_id=1, source_target_pairs={{0,1},{1,0},{2,3},{3,2},{4,5},{5,4},{6,7},{7,6},{8,9},{9,8},{10,11... | collective-permute-start | bytes 9437192 | tf_op jit(solution)/shard_map/ppermute | solution.py:687
  1016.8 212.1 %collective-permute-start.39 = (bf16[2,2048,384]{2,1,0:T(8,128)(2,1)}, bf16[2,2048,384]{2,1,0:T(8,128)(2,1)}, u32[]{:S(2)}, u32[]{:S(2)}) collective-permute-start(bf16[2,2048,384]{2,1,0:T(8,128)(2,1)} %pad_maximum_fusion.4), channel_id=1, source_target_pairs={{0,1},{1,0},{2,3},{3,2},{4,5},{5,4},{6,7},{7,6},{8,9},{9,8},{10,11... | collective-permute-start | bytes 9437192 | tf_op jit(solution)/shard_map/ppermute | solution.py:687
  1017.9 211.0 %collective-permute-start.40 = (bf16[2,384,2048]{2,1,0:T(8,128)(2,1)}, bf16[2,384,2048]{2,1,0:T(8,128)(2,1)}, u32[]{:S(2)}, u32[]{:S(2)}) collective-permute-start(bf16[2,384,2048]{2,1,0:T(8,128)(2,1)} %pad_maximum_fusion.5), channel_id=1, source_target_pairs={{0,1},{1,0},{2,3},{3,2},{4,5},{5,4},{6,7},{7,6},{8,9},{9,8},{10,11... | collective-permute-start | bytes 9437192 | tf_op jit(solution)/shard_map/ppermute | solution.py:687
  1048.5 162.5 %collective-permute-start.37 = (f32[18,128]{1,0:T(8,128)S(1)}, f32[18,128]{1,0:T(8,128)S(1)}, u32[]{:S(2)}, u32[]{:S(2)}) collective-permute-start(f32[18,128]{1,0:T(8,128)S(1)} %bitcast.318), channel_id=1, source_target_pairs={{0,1},{1,0},{2,3},{3,2},{4,5},{5,4},{6,7},{7,6},{8,9},{9,8},{10,11... | collective-permute-start | bytes 27656 | tf_op jit(solution)/shard_map/ppermute | solution.py:725
  1052.7 160.5 %collective-permute-start.54 = (bf16[128,2560]{1,0:T(8,128)(2,1)}, bf16[128,2560]{1,0:T(8,128)(2,1)}, u32[]{:S(2)}, u32[]{:S(2)}) collective-permute-start(bf16[128,2560]{1,0:T(8,128)(2,1)} %get-tuple-element.199), channel_id=1, source_target_pairs={{8,0},{10,2},{16,8},{18,10},{24,16},{26,18},{28,24},{30,26},{20,28... | collective-permute-start | bytes 1966088 | tf_op jit(solution)/shard_map/ppermute | solution.py:121
  (101 other events, 2041.1 us)
Sparse Core Ops, SparseCore 0:
  10.9 90.9 all-gather.4
  104.1 89.4 all-gather.6
  236.8 92.5 all-gather.8
  882.7 113.6 reduce-scatter.4
  1000.4 193.9 reduce-scatter.2

commit v4 on v3

--- a/solution.py
+++ b/solution.py
@@ -280,52 +280,72 @@
 HELD = 20 * 1024 * 1024
 
 
-def pick_kernel(tiles, first, last, places_ref, rows_ref, out_ref, total):
+def pick_kernel(tiles, first, last, places_ref, *refs):
     e, j = pl.program_id(1), pl.program_id(2)
+    third = len(refs) // 3
+    sources, outs, totals = refs[:third], refs[third : 2 * third], refs[2 * third :]
 
     @pl.when(j < tiles[e])
     def _():
-        total[...] = jnp.zeros_like(total)
+        for total in totals:
+            total[...] = jnp.zeros_like(total)
         at = e * pl.num_programs(2) + j
         wanted = j * TILE + lax.broadcasted_iota(jnp.int32, (TILE, places_ref.shape[2]), 0)
 
         def add(g, carry):
             hits = jnp.where(places_ref[g] == wanted, 1.0, 0.0).astype(BF16)
-            total[...] += mm(hits, rows_ref[g])
+            for source, total in zip(sources, totals):
+                total[...] += mm(hits, source[g])
             return carry
 
         lax.fori_loop(first[at], last[at] + 1, add, 0)
-        out_ref[...] = total[...].astype(BF16)
+        for out, total in zip(outs, totals):
+            out[...] = total[...].astype(BF16)
 
     @pl.when(j >= tiles[e])
     def _():
-        out_ref[...] = jnp.zeros_like(out_ref)
-
-
-def pick(plan, source, start, width):
+        for out in outs:
+            out[...] = jnp.zeros_like(out)
+
+
+def pick(plan, source, width):
     experts, nodes, _, tokens = plan["places"].shape
     count = plan["tile_count"]
     cuts = 1
     while 2 * nodes * tokens * (width // cuts) > HELD and width % (256 * cuts) == 0:
         cuts *= 2
     part = width // cuts
+    more = source.shape[2] - width
+    out_specs = [pl.BlockSpec((None, TILE, part), lambda c, e, j, *_: (e, j, c))]
+    in_specs = [
+        pl.BlockSpec((None, nodes, 1, tokens), lambda c, e, j, *_: (e, 0, 0, 0)),
+        pl.BlockSpec(
+            (nodes, tokens, part), lambda c, e, j, *_: (0, 0, c), pipeline_mode=pl.Buffered(1)
+        ),
+    ]
+    widths = [width]
+    scratch = [pltpu.VMEM((TILE, part), F32)]
+    if more:
+        out_specs.append(pl.BlockSpec((None, TILE, more), lambda c, e, j, *_: (e, j, 0)))
+        in_specs.append(
+            pl.BlockSpec(
+                (nodes, tokens, more),
+                lambda c, e, j, *_: (0, 0, width // more),
+                pipeline_mode=pl.Buffered(1),
+            )
+        )
+        widths.append(more)
+        scratch.append(pltpu.VMEM((TILE, more), F32))
     return pl.pallas_call(
         pick_kernel,
         grid_spec=pltpu.PrefetchScalarGridSpec(
             num_scalar_prefetch=3,
             grid=(cuts, experts, count),
-            in_specs=[
-                pl.BlockSpec((None, nodes, 1, tokens), lambda c, e, j, *_: (e, 0, 0, 0)),
-                pl.BlockSpec(
-                    (nodes, tokens, part),
-                    lambda c, e, j, *_: (0, 0, start // part + c),
-                    pipeline_mode=pl.Buffered(1),
-                ),
-            ],
-            out_specs=pl.BlockSpec((None, TILE, part), lambda c, e, j, *_: (e, j, c)),
-            scratch_shapes=[pltpu.VMEM((TILE, part), F32)],
-        ),
-        out_shape=jax.ShapeDtypeStruct((experts, count * TILE, width), BF16),
+            in_specs=in_specs,
+            out_specs=out_specs,
+            scratch_shapes=scratch,
+        ),
+        out_shape=[jax.ShapeDtypeStruct((experts, count * TILE, w), BF16) for w in widths],
         compiler_params=pltpu.CompilerParams(vmem_limit_bytes=GRANT),
         cost_estimate=pl.CostEstimate(
             flops=6 * experts * count * TILE * tokens * width,
@@ -333,7 +353,72 @@
             transcendentals=0,
         ),
         name="pick",
-    )(plan["tiles"], plan["first"], plan["last"], plan["places"], source)
+    )(
+        plan["tiles"], plan["first"], plan["last"], plan["places"], *([source] * len(widths))
+    )
+
+
+def weight_kernel(tiles, left_ref, right_ref, own_ref, far_ref, total, *, axis, piece, group):
+    e, j = pl.program_id(0), pl.program_id(1)
+
+    @pl.when(j == 0)
+    def _():
+        total[...] = jnp.zeros_like(total)
+
+    @pl.when(j * group < tiles[e])
+    def _():
+        total[...] += mm(left_ref[...], right_ref[...], ((0,), (0,)))
+
+    @pl.when(j == pl.num_programs(1) - 1)
+    def _():
+        if axis == 0:
+            own_ref[...] = total[:piece, :]
+            far_ref[...] = total[piece:, :].astype(BF16)
+        else:
+            own_ref[...] = total[:, :piece]
+            far_ref[...] = total[:, piece:].astype(BF16)
+
+
+def weight_grad(plan, left, right, axis, piece):
+    experts, height, deep = left.shape
+    wide = right.shape[2]
+    group = 2 if plan["tile_count"] % 2 == 0 else 1
+    size = group * TILE
+
+    def block(rows, columns):
+        return pl.BlockSpec((None, rows, columns), lambda e, j, *_: (e, 0, 0))
+
+    own = (piece, wide) if axis == 0 else (deep, piece)
+    far = (deep - piece, wide) if axis == 0 else (deep, wide - piece)
+
+    def rows_at(e, j, tiles):
+        used = (tiles[e] + group - 1) // group
+        return (e, jnp.minimum(j, jnp.maximum(used - 1, 0)), 0)
+
+    return pl.pallas_call(
+        functools.partial(weight_kernel, axis=axis, piece=piece, group=group),
+        grid_spec=pltpu.PrefetchScalarGridSpec(
+            num_scalar_prefetch=1,
+            grid=(experts, height // size),
+            in_specs=[
+                pl.BlockSpec((None, size, deep), rows_at),
+                pl.BlockSpec((None, size, wide), rows_at),
+            ],
+            out_specs=[block(*own), block(*far)],
+            scratch_shapes=[pltpu.VMEM((deep, wide), F32)],
+        ),
+        out_shape=[
+            jax.ShapeDtypeStruct((experts,) + own, F32),
+            jax.ShapeDtypeStruct((experts,) + far, BF16),
+        ],
+        compiler_params=pltpu.CompilerParams(vmem_limit_bytes=GRANT),
+        cost_estimate=pl.CostEstimate(
+            flops=experts * height * deep * wide,
+            bytes_accessed=experts * (height * (deep + wide) + 6 * deep * wide),
+            transcendentals=0,
+        ),
+        name="weight_grad",
+    )(plan["tiles"], left, right)
 
 
 def expert_kernel(
@@ -593,7 +678,11 @@
         made["middle"] = input_wide + scatter_tp([projected[:, j] for j in range(tp_size)])
         return moving
 
-    cot_all = ring_gather(cot_low, (project,))
+    def settle(moving):
+        made["middle"], moving = lax.optimization_barrier((made["middle"], moving))
+        return moving
+
+    cot_all = ring_gather(cot_low, (project, settle))
     middle, down_weight = lax.optimization_barrier((made["middle"], down_weight))
     down_full = gather_tp(down_weight, 1)
     inverse_two = inverse_rms(middle)
@@ -614,45 +703,42 @@
     )
     rows_all = lax.all_gather(sent, "fsdp", axis=0)
 
-    arrived = pick(plan, rows_all, 0, model_width)
-    extra = pick(plan, rows_all, model_width, sent.shape[1] - model_width)
-    cots = pick(plan, cot_all, 0, model_width)
+    arrived, extra = pick(plan, rows_all, model_width)
+    cots = pick(plan, cot_all, model_width)[0]
     weighed, grad_gate_pre, grad_up_pre, produced, back, columns = run_experts(
         plan, base, arrived, extra, cots, gate_full, up_full, down_full, expert_count
     )
     out_total = spread(plan, [produced])[0]
     out_total, back = lax.optimization_barrier((out_total, back))
     grad_total, columns = spread(plan, [back, columns])
-    own_grads = []
-    far_grads = []
-    for e in range(local_experts):
-        grads = (
-            mm(arrived[e], grad_gate_pre[e], ((0,), (0,))),
-            mm(arrived[e], grad_up_pre[e], ((0,), (0,))),
-            mm(weighed[e], cots[e], ((0,), (0,))),
-        )
-        own_grads.append(
-            (grads[0][:, :half_hidden], grads[1][:, :half_hidden], grads[2][:half_hidden])
-        )
-        far_grads.append(
+    own_grads, far_grads = zip(
+        weight_grad(plan, arrived, grad_gate_pre, 1, half_hidden),
+        weight_grad(plan, arrived, grad_up_pre, 1, half_hidden),
+        weight_grad(plan, weighed, cots, 0, half_hidden),
+    )
+
+    pairs = columns[:, :, : 2 * local_experts].astype(F32).reshape(nodes, tokens, local_experts, 2)
+    column = jnp.sum(pairs, axis=-1)
+    grad_gate = lax.all_to_all(column, "fsdp", split_axis=0, concat_axis=0, tiled=True)
+    grad_gate = jnp.moveaxis(grad_gate, 0, 1).reshape(tokens, expert_count)
+
+    moved = []
+    for kind in range(3):
+        axis = 2 if kind < 2 else 1
+        moved.append(
             [
-                (
-                    grads[0][:, j * half_hidden : (j + 1) * half_hidden].astype(BF16),
-                    grads[1][:, j * half_hidden : (j + 1) * half_hidden].astype(BF16),
-                    grads[2][j * half_hidden : (j + 1) * half_hidden].astype(BF16),
+                lax.ppermute(
+                    lax.slice_in_dim(
+                        far_grads[kind], (j - 1) * half_hidden, j * half_hidden, axis=axis
+                    ),
+                    "tp",
+                    [(s, (s + j) % tp_size) for s in range(tp_size)],
                 )
                 for j in range(1, tp_size)
             ]
         )
-
-    pairs = columns[:, :, : 2 * local_experts].astype(F32).reshape(nodes, tokens, local_experts, 2)
-    column = jnp.sum(pairs, axis=-1)
-    grad_gate = lax.all_to_all(column, "fsdp", split_axis=0, concat_axis=0, tiled=True)
-    grad_gate = jnp.moveaxis(grad_gate, 0, 1).reshape(tokens, expert_count)
-
     grad_rows = ring_scatter(grad_total)
     expert_part = lax.psum_scatter(out_total, "fsdp", scatter_dimension=0, tiled=True)
-    grad_rows, far_grads = lax.optimization_barrier((grad_rows, far_grads))
     grad_logits = (
         gates * (grad_gate - jnp.sum(gates * grad_gate, axis=-1, keepdims=True))
     ).astype(BF16)
@@ -664,10 +750,13 @@
     expert_gain_part = jnp.sum(grad_two * normed_two, axis=(0, 1))
     grad_middle = cotangent.astype(F32) + norm_backward(grad_two, expert_gain, normed_two, inverse_two)
 
-    grad_flat = gather_tp(grad_middle.astype(BF16), 1).reshape(every, model_width)
+    grad_low = gather_tp(grad_middle.astype(BF16), 1)
+    grad_flat = grad_low.reshape(every, model_width)
     grad_attended = mm(grad_flat, output_full).astype(BF16)
     output_low = mm(grad_flat, attended, ((0,), (0,))).astype(BF16)
-    output_low, grad_attended = lax.optimization_barrier((output_low, grad_attended))
+    output_low, grad_attended, expert_part = lax.optimization_barrier(
+        (output_low, grad_attended, expert_part)
+    )
     output_part = lax.psum_scatter(output_low, "fsdp", scatter_dimension=0, tiled=True)
     grad_pre, query_gain_part, key_gain_part = attend_back(
         pre, tables, gains, attended, grad_attended, rows, heads, kv_heads
@@ -676,21 +765,24 @@
     qkv_grad = ring_scatter(qkv_low.reshape(nodes, -1, qkv_low.shape[1]))
     qkv_grad = qkv_grad.reshape(query_weight.shape[0], -1)
     grad_normed = mm(grad_pre, qkv_full, ((1,), (1,))).reshape(rows, tp_size, local_length, model_width)
-    grad_one = scatter_tp([grad_normed[:, j] for j in range(tp_size)])
+    received = [
+        lax.ppermute(
+            grad_normed[:, j].astype(BF16), "tp", [(s, (s + j) % tp_size) for s in range(tp_size)]
+        )
+        for j in range(1, tp_size)
+    ]
+
+    moved, received, qkv_grad = lax.optimization_barrier((moved, received, qkv_grad))
+    grad_one = grad_normed[:, 0]
+    for value in received:
+        grad_one = grad_one + value.astype(F32)
     attention_gain_part = jnp.sum(grad_one * normed_one, axis=(0, 1))
     input_grad = grad_middle + norm_backward(grad_one, attention_gain, normed_one, inverse_one)
-
-    moved = []
-    for kind in range(3):
-        for j in range(1, tp_size):
-            far = jnp.stack([far_grads[e][j - 1][kind] for e in range(local_experts)])
-            moved.append(lax.ppermute(far, "tp", [(s, (s + j) % tp_size) for s in range(tp_size)]))
-    moved, qkv_grad = lax.optimization_barrier((moved, qkv_grad))
     weight_grads = []
     for kind in range(3):
-        total = jnp.stack([own_grads[e][kind] for e in range(local_experts)])
-        for j in range(tp_size - 1):
-            total = total + moved[kind * (tp_size - 1) + j].astype(F32)
+        total = own_grads[kind]
+        for value in moved[kind]:
+            total = total + value.astype(F32)
         weight_grads.append(total)
     gate_grad, up_grad, down_grad = weight_grads
     query_width, key_width = query_weight.shape[1], key_weight.shape[1]

time: 1270 us -> 1330 us (1.047)
  matrix products: 131 us -> 54.2 us
  starting transfers between devices: 52.6 us -> 116 us
  Pallas kernels: 277 us -> 325 us
  waiting for transfers between devices: 537 us -> 567 us
  local copies, waits for them, and re-layouts: 93.8 us -> 74.4 us
  blocking collectives: 41.3 us -> 57.9 us
    ppermute x1, waiting for transfers between devices: 158 us -> 0.01 us  [layer(): lax.ppermute(share, 'tp', [(s, (s + j) % tp_size) for s in range(tp_size)])]
    ppermute x3 -> x4, waiting for transfers between devices: 0.01 us -> 120 us  [the longest x3 99.9 us: layer(): lax.ppermute(lax.slice_in_dim(far_grads[kind], (j - 1) * half_hidden, j *...]
    dot_general x15 -> x9, matrix products: 131 us -> 53.3 us  [mm(): return lax.dot_general(a, b, (dims, ((), ())), preferred_element_type=F32)]
    ppermute x8, starting transfers between devices: 12.7 us -> 72.6 us  [ring_scatter(): rising = lax.ppermute(rising, 'fsdp', up).astype(F32)]
    pallas_call x0 -> x3, Pallas kernels: none -> 58.9 us  [weight_grad(): pl.pallas_call(functools.partial(weight_kernel, axis=axis, piece=piece, g...]
    ppermute x8, waiting for transfers between devices: 73.6 us -> 128 us  [ring_scatter(): rising = lax.ppermute(rising, 'fsdp', up).astype(F32)]
    ppermute x5, waiting for transfers between devices: 131 us -> 155 us  [fetch_next(): lax.ppermute(values, 'tp', [(s, (s - step) % size) for s in range(size)])]
    ppermute x4, waiting for transfers between devices: 54.1 us -> 31.5 us  [ring_gather(): behind = lax.ppermute(behind, 'fsdp', up)]
  transfers between devices with their start and end apart: 63 -> 62, of which waited for: 22 -> 22; matrix products, arithmetic and copies ran while one was open for 21% -> 14% of each run, Pallas kernels for 8% -> 11%
where the time goes in v4:
time: 1330 us; the launch traced here: 1320 us
  waiting for transfers between devices  567 us (43%)
  Pallas kernels  325 us (24%)
  starting transfers between devices  116 us (9%)
  other arithmetic  98 us (7%)
  local copies, waits for them, and re-layouts  74.4 us (6%)
  blocking collectives  57.9 us (4%)
  matrix products  54.2 us (4%)
  between operations  29.3 us (2%)
    ppermute x5, waiting for transfers between devices, fetch_next(): lax.ppermute(values, 'tp', [(s, (s - step) % size) for s in range(size)])  155 us
    ppermute x8, waiting for transfers between devices, ring_scatter(): rising = lax.ppermute(rising, 'fsdp', up).astype(F32)  128 us
    ppermute x3, waiting for transfers between devices, layer(): lax.ppermute(lax.slice_in_dim(far_grads[kind], (j - 1) * half_hidden, j *...  99.9 us
    pallas_call x1, Pallas kernels, run_experts(): pl.pallas_call(functools.partial(expert_kernel, expert_count=expert_count...  79.3 us
    ppermute x8, starting transfers between devices, ring_scatter(): rising = lax.ppermute(rising, 'fsdp', up).astype(F32)  72.6 us
    pallas_call x2, Pallas kernels, pick(): pl.pallas_call(pick_kernel, grid_spec=pltpu.PrefetchScalarGridSpec(num_sc...  70.1 us
    pallas_call x3, Pallas kernels, weight_grad(): pl.pallas_call(functools.partial(weight_kernel, axis=axis, piece=piece, g...  58.9 us
    dot_general x9, matrix products, mm(): return lax.dot_general(a, b, (dims, ((), ())), preferred_element_type=F32)  53.3 us
  transfers between devices with their start and end apart: 62, of which 22 were waited for; matrix products, arithmetic and copies ran while one was open for 14% of the time, Pallas kernels for 11%

profile of v4, /device:TPU:0, one launch (start us, length us, event | category | flops | bytes accessed | tf_op | source)
XLA Modules:
  0.0 1322.1 jit_solution(1155279389921340100)
XLA Ops:
  13.9 24.3 %all_gather.19 = s32[16,256,8]{1,2,0:T(8,128)} all-gather(s32[1,256,8]{1,2,0:T(8,128)S(1)} %constant_dynamic-slice_fusion.4), channel_id=1, replica_groups=mesh['fsdp'=16,'tp'=2] {'fsdp'}, dimensions={0}, use_global_device_ids=true | all-gather | bytes 139264 | tf_op jit(solution)/shard_map/all_gather | solution.py:655
  59.7 42.1 %all-gather.5.cloned.1.call-done = bf16[2048,2560]{1,0:T(8,128)(2,1)} async-done(((bf16[128,2560]{1,0:T(8,128)(2,1)}), bf16[2048,2560]{1,0:T(8,128)(2,1)}) %all-gather.5.cloned.1.call-update) | async-done | bytes 10485776 | tf_op jit(solution)/shard_map/all_gather | solution.py:617
  118.2 28.7 %attend.1.att_ref = bf16[512,2048]{1,0:T(8,128)(2,1)} custom-call(f32[512,2560]{1,0:T(8,128)} %fusion.70.q_ref.k_ref.v_ref, f32[512,2560]{1,0:T(8,128)} %fusion.70.q_ref.k_ref.v_ref, f32[512,2560]{1,0:T(8,128)} %fusion.70.q_ref.k_ref.v_ref, f32[512,128]{1,0:T(8,128)} %maximum_bitcast_fusion.4.cos_ref, f32[512,128]{1,0:T(8,128)} %maximum_bitcast_fusion.5.sin_ref, ...), custom_call_target="tpu_custom_call" | custom-call | flops 2147483648 | bytes 7864320 | tf_op jit(solution)/shard_map/attend/pallas_call | solution.py:235
  152.7 40.3 %all-gather.7.cloned.1.call-done = bf16[2048,2048]{1,0:T(8,128)(2,1)} async-done(((bf16[128,2048]{1,0:T(8,128)(2,1)}), bf16[2048,2048]{1,0:T(8,128)(2,1)}) %all-gather.7.cloned.1.call-update) | async-done | bytes 8388624 | tf_op jit(solution)/shard_map/all_gather | solution.py:625
  206.5 21.7 %collective-permute-done.3 = bf16[1,256,2048]{2,1,0:T(8,128)(2,1)} collective-permute-done((bf16[1,256,2048]{2,1,0:T(8,128)(2,1)S(1)}, bf16[1,256,2048]{2,1,0:T(8,128)(2,1)}, u32[]{:S(2)}, u32[]{:S(2)}) %collective-permute-start.3) | collective-permute-done | bytes 1048608 | tf_op jit(solution)/shard_map/ppermute | solution.py:46
  261.5 48.1 %collective-permute-done.17 = bf16[2,2048,384]{2,1,0:T(8,128)(2,1)} collective-permute-done((bf16[2,2048,384]{2,1,0:T(8,128)(2,1)}, bf16[2,2048,384]{2,1,0:T(8,128)(2,1)}, u32[]{:S(2)}, u32[]{:S(2)}) %collective-permute-start.17) | collective-permute-done | bytes 3145760 | tf_op jit(solution)/shard_map/ppermute | solution.py:34
  315.9 59.5 %collective-permute-done.18 = bf16[2,2048,384]{2,1,0:T(8,128)(2,1)} collective-permute-done((bf16[2,2048,384]{2,1,0:T(8,128)(2,1)}, bf16[2,2048,384]{2,1,0:T(8,128)(2,1)}, u32[]{:S(2)}, u32[]{:S(2)}) %collective-permute-start.18) | collective-permute-done | bytes 3145760 | tf_op jit(solution)/shard_map/ppermute | solution.py:34
  445.5 22.2 %collective-permute-done.19 = bf16[2,384,2048]{2,1,0:T(8,128)(2,1)S(1)} collective-permute-done((bf16[2,384,2048]{2,1,0:T(8,128)(2,1)S(1)}, bf16[2,384,2048]{2,1,0:T(8,128)(2,1)S(1)}, u32[]{:S(2)}, u32[]{:S(2)}) %collective-permute-start.19) | collective-permute-done | bytes 3145760 | tf_op jit(solution)/shard_map/ppermute | solution.py:34
  473.8 34.0 %pick.3.cots_ref.right_ref = bf16[2,2560,2048]{2,1,0:T(8,128)(2,1)} custom-call(s32[2]{0:T(128)} %and_select_fusion.1.tiles, s32[20]{0:T(128)} %min.30.first, s32[20]{0:T(128)} %min.32.last, s32[2,16,1,256]{3,2,1,0:T(1,128)} %broadcast_in_dim.136.places_ref, bf16[16,256,2048]{2,1,0:T(8,128)(2,1)} %bitcast_dynamic-update-slice_fusion.refs_0_), custom_call_target="tpu_custom_call" | custom-call | flops 16106127360 | bytes 37748736 | tf_op jit(solution)/shard_map/pick/pallas_call | solution.py:339
  507.7 36.1 %pick.2 = (bf16[2,2560,2048]{2,1,0:T(8,128)(2,1)}, bf16[2,2560,128]{2,1,0:T(8,128)(2,1)}) custom-call(s32[2]{0:T(128)} %and_select_fusion.1.tiles, s32[20]{0:T(128)} %min.30.first, s32[20]{0:T(128)} %min.32.last, s32[2,16,1,256]{3,2,1,0:T(1,128)} %broadcast_in_dim.136.places_ref, bf16[16,256,2176]{2,1,0:T(8,128)(2,1)} %bitcast.265, ...), custom_call_target="tpu_custom_call" | custom-call | flops 16106127360 | bytes 37748736 | tf_op jit(solution)/shard_map/pick/pallas_call | solution.py:339
  543.8 79.3 %run_experts.1 = (bf16[2,2560,768]{2,1,0:T(8,128)(2,1)}, bf16[2,2560,768]{2,1,0:T(8,128)(2,1)}, bf16[2,2560,768]{2,1,0:T(8,128)(2,1)}, bf16[2,2560,2048]{2,1,0:T...) custom-call(s32[2]{0:T(128)} %and_select_fusion.1.tiles, s32[1]{0:T(128)} %bitcast.15.base, ...), custom_call_target="tpu_custom_call" | custom-call | flops 48318382080 | bytes 107479040 | tf_op jit(solution)/shard_map/run_experts/pallas_call | solution.py:484
  623.2 22.4 %spread.2 = bf16[16,256,2048]{2,1,0:T(8,128)(2,1)} custom-call(s32[32]{0:T(128)} %reshape.784.starts, s32[2,16,1,256]{3,2,1,0:T(1,128)} %broadcast_in_dim.136.places_ref, bf16[2,2560,2048]{2,1,0:T(8,128)(2,1)} %get-tuple-element.77.refs_0_), custom_call_target="tpu_custom_call" | custom-call | flops 5905580032 | bytes 41943040 | tf_op jit(solution)/shard_map/spread/pallas_call | solution.py:527
  646.9 24.3 %spread.3 = (bf16[16,256,2048]{2,1,0:T(8,128)(2,1)}, bf16[16,256,128]{2,1,0:T(8,128)(2,1)}) custom-call(s32[32]{0:T(128)} %reshape.784.starts, s32[2,16,1,256]{3,2,1,0:T(1,128)} %broadcast_in_dim.136.places_ref, bf16[2,2560,2048]{2,1,0:T(8,128)(2,1)} %get-tuple-element.79.refs_0_, bf16[2,2560,128]{2,1,0:T(8,128)(2,1)} %get-tuple-element.80.refs_1_), custom_call_target="tpu_custom_call" | custom-call | flops 6274678784 | bytes 44564480 | tf_op jit(solution)/shard_map/spread/pallas_call | solution.py:527
  697.7 45.6 %collective-permute-done.21 = bf16[256,2048]{1,0:T(8,128)(2,1)} collective-permute-done((bf16[256,2048]{1,0:T(8,128)(2,1)}, bf16[256,2048]{1,0:T(8,128)(2,1)}, u32[]{:S(2)}, u32[]{:S(2)}) %collective-permute-start.21) | collective-permute-done | bytes 1048608 | tf_op jit(solution)/shard_map/ppermute | solution.py:117
  769.7 38.1 %collective-permute-done.23 = bf16[256,2048]{1,0:T(8,128)(2,1)S(1)} collective-permute-done((bf16[256,2048]{1,0:T(8,128)(2,1)S(1)}, bf16[256,2048]{1,0:T(8,128)(2,1)S(1)}, u32[]{:S(2)}, u32[]{:S(2)}) %collective-permute-start.23) | collective-permute-done | bytes 1048608 | tf_op jit(solution)/shard_map/ppermute | solution.py:117
  813.2 28.2 %collective-permute-done.25 = bf16[256,2048]{1,0:T(8,128)(2,1)S(1)} collective-permute-done((bf16[256,2048]{1,0:T(8,128)(2,1)S(1)}, bf16[256,2048]{1,0:T(8,128)(2,1)S(1)}, u32[]{:S(2)}, u32[]{:S(2)}) %collective-permute-start.25) | collective-permute-done | bytes 1048608 | tf_op jit(solution)/shard_map/ppermute | solution.py:117
  846.6 40.7 %collective-permute-start.27 = (bf16[256,2048]{1,0:T(8,128)(2,1)}, bf16[256,2048]{1,0:T(8,128)(2,1)}, u32[]{:S(2)}, u32[]{:S(2)}) collective-permute-start(bf16[256,2048]{1,0:T(8,128)(2,1)} %get-tuple-element.197), channel_id=1, source_target_pairs={{0,8},{2,10},{8,16},{10,18},{16,24},{18,26},{24,28},{26,30},{28,20... | collective-permute-start | bytes 3145736 | tf_op jit(solution)/shard_map/ppermute | solution.py:117
  913.3 25.2 %collective-permute-done.35 = bf16[1,256,2048]{2,1,0:T(8,128)(2,1)S(1)} collective-permute-done((bf16[1,256,2048]{2,1,0:T(8,128)(2,1)S(1)}, bf16[1,256,2048]{2,1,0:T(8,128)(2,1)S(1)}, u32[]{:S(2)}, u32[]{:S(2)}) %collective-permute-start.35) | collective-permute-done | bytes 1048608 | tf_op jit(solution)/shard_map/ppermute | solution.py:34
  954.8 41.1 %attend_back.1 = (bf16[512,2560]{1,0:T(8,128)(2,1)}, f32[1,128]{1,0:T(1,128)}, f32[1,128]{1,0:T(1,128)}) custom-call(f32[512,2560]{1,0:T(8,128)} %fusion.70.q_ref.k_ref.v_ref, f32[512,2560]{1,0:T(8,128)} %fusion.70.q_ref.k_ref.v_ref, f32[512,2560]{1,0:T(8,128)} %fusion.70.q_ref.k_ref.v_ref, f32[512,128]{1,0:T(8,128)} %maximum_bitcast_fusion.4.cos_ref, ...), custom_call_target="tpu_custom_call" | custom-call | flops 5368709120 | bytes 13107200 | tf_op jit(solution)/shard_map/attend_back/pallas_call | solution.py:263
  1014.7 19.9 %weight_grad.5 = (f32[2,384,2048]{2,1,0:T(8,128)}, bf16[2,384,2048]{2,1,0:T(8,128)(2,1)}) custom-call(s32[2]{0:T(128)} %and_select_fusion.1.tiles, bf16[2,2560,768]{2,1,0:T(8,128)(2,1)} %get-tuple-element.91.left_ref, bf16[2,2560,2048]{2,1,0:T(8,128)(2,1)} %pick.3.cots_ref.right_ref), custom_call_target="tpu_custom_call" | custom-call | flops 8053063680 | bytes 33292288 | tf_op jit(solution)/shard_map/weight_grad/pallas_call | solution.py:398
  1090.7 19.7 %weight_grad.4 = (f32[2,2048,384]{2,1,0:T(8,128)}, bf16[2,2048,384]{2,1,0:T(8,128)(2,1)}) custom-call(s32[2]{0:T(128)} %and_select_fusion.1.tiles, bf16[2,2560,2048]{2,1,0:T(8,128)(2,1)} %get-tuple-element.70.arrived_ref.left_ref, bf16[2,2560,768]{2,1,0:T(8,128)(2,1)} %get-tuple-element.89.right_ref), custom_call_target="tpu_custom_call" | custom-call | flops 8053063680 | bytes 33292288 | tf_op jit(solution)/shard_map/weight_grad/pallas_call | solution.py:398
  1149.1 32.5 %collective-permute-done.36 = bf16[2,2048,384]{2,1,0:T(8,128)(2,1)} collective-permute-done((bf16[2,2048,384]{2,1,0:T(8,128)(2,1)}, bf16[2,2048,384]{2,1,0:T(8,128)(2,1)}, u32[]{:S(2)}, u32[]{:S(2)}) %collective-permute-start.36) | collective-permute-done | bytes 3145760 | tf_op jit(solution)/shard_map/ppermute | solution.py:730
  1181.6 67.4 %collective-permute-done.37 = bf16[2,2048,384]{2,1,0:T(8,128)(2,1)} collective-permute-done((bf16[2,2048,384]{2,1,0:T(8,128)(2,1)}, bf16[2,2048,384]{2,1,0:T(8,128)(2,1)}, u32[]{:S(2)}, u32[]{:S(2)}) %collective-permute-start.37) | collective-permute-done | bytes 3145760 | tf_op jit(solution)/shard_map/ppermute | solution.py:730
  1249.0 20.5 %collective-permute-done.39 = bf16[1,256,2048]{2,1,0:T(8,128)(2,1)} collective-permute-done((bf16[1,256,2048]{2,1,0:T(8,128)(2,1)}, bf16[1,256,2048]{2,1,0:T(8,128)(2,1)}, u32[]{:S(2)}, u32[]{:S(2)}) %collective-permute-start.39) | collective-permute-done | bytes 1048608 | tf_op jit(solution)/shard_map/ppermute | solution.py:769
  (339 shorter events, 431.1 us)
Async XLA Ops:
  7.2 94.6 %all-gather.5.cloned.1.call-start = ((), (), s32[]{:S(2)}) async-start(), calls=%async_computation.4 | async-start | bytes 11141120 | tf_op jit(solution)/shard_map/all_gather | solution.py:617
  9.4 183.6 %all-gather.7.cloned.1.call-start = ((), (), s32[]{:S(2)}) async-start(), calls=%async_computation.5 | async-start | bytes 8912896 | tf_op jit(solution)/shard_map/all_gather | solution.py:625
  10.1 497.6 %all-gather.9.cloned.1.call-start = ((), (), s32[]{:S(2)}) async-start(), calls=%async_computation.8 | async-start | bytes 18939904 | tf_op jit(solution)/shard_map/all_gather | solution.py:704
  10.8 46.1 %collective-permute-start = (bf16[1,256,2048]{2,1,0:T(8,128)(2,1)S(1)}, bf16[1,256,2048]{2,1,0:T(8,128)(2,1)}, u32[]{:S(2)}, u32[]{:S(2)}) collective-permute-start(bf16[1,256,2048]{2,1,0:T(8,128)(2,1)S(1)} %fusion.4), channel_id=1, source_target_pairs={{0,1},{1,0},{2,3},{3,2},{4,5},{5,4},{6,7},{7,6},{8,9},{9,8},{10,11... | collective-permute-start | bytes 3145736 | tf_op jit(solution)/shard_map/ppermute | solution.py:34
  237.8 717.0 %reduce-scatter.3.cloned.1.call-start = ((), (), s32[]{:S(2)}) async-start(), calls=%async_computation.6 | async-start | bytes 17825792 | tf_op jit(solution)/shard_map/reduce_scatter | solution.py:741
  238.2 71.4 %collective-permute-start.17 = (bf16[2,2048,384]{2,1,0:T(8,128)(2,1)}, bf16[2,2048,384]{2,1,0:T(8,128)(2,1)}, u32[]{:S(2)}, u32[]{:S(2)}) collective-permute-start(bf16[2,2048,384]{2,1,0:T(8,128)(2,1)} %param.122), channel_id=1, source_target_pairs={{0,1},{1,0},{2,3},{3,2},{4,5},{5,4},{6,7},{7,6},{8,9},{9,8},{10,11... | collective-permute-start | bytes 9437192 | tf_op jit(solution)/shard_map/ppermute | solution.py:34
  239.8 135.7 %collective-permute-start.18 = (bf16[2,2048,384]{2,1,0:T(8,128)(2,1)}, bf16[2,2048,384]{2,1,0:T(8,128)(2,1)}, u32[]{:S(2)}, u32[]{:S(2)}) collective-permute-start(bf16[2,2048,384]{2,1,0:T(8,128)(2,1)} %param.123), channel_id=1, source_target_pairs={{0,1},{1,0},{2,3},{3,2},{4,5},{5,4},{6,7},{7,6},{8,9},{9,8},{10,11... | collective-permute-start | bytes 9437192 | tf_op jit(solution)/shard_map/ppermute | solution.py:34
  261.5 126.7 %collective-permute-start.6 = (bf16[256,2048]{1,0:T(8,128)(2,1)S(1)}, bf16[256,2048]{1,0:T(8,128)(2,1)S(1)}, u32[]{:S(2)}, u32[]{:S(2)}) collective-permute-start(bf16[256,2048]{1,0:T(8,128)(2,1)S(1)} %bitcast.244), channel_id=1, source_target_pairs={{0,2},{2,0},{4,6},{6,4},{8,10},{10,8},{12,14},{14,12},{16,18},{18,... | collective-permute-start | bytes 3145736 | tf_op jit(solution)/shard_map/ppermute | solution.py:82
  397.3 70.3 %collective-permute-start.19 = (bf16[2,384,2048]{2,1,0:T(8,128)(2,1)S(1)}, bf16[2,384,2048]{2,1,0:T(8,128)(2,1)S(1)}, u32[]{:S(2)}, u32[]{:S(2)}) collective-permute-start(bf16[2,384,2048]{2,1,0:T(8,128)(2,1)S(1)} %copy-done.16), channel_id=1, source_target_pairs={{0,1},{1,0},{2,3},{3,2},{4,5},{5,4},{6,7},{7,6},{8,9},{9,8},{10,11... | collective-permute-start | bytes 9437192 | tf_op jit(solution)/shard_map/ppermute | solution.py:34
  645.6 667.7 %reduce-scatter.5.cloned.1.call-start = ((), (), s32[]{:S(2)}) async-start(), calls=%async_computation.7 | async-start | bytes 8912896 | tf_op jit(solution)/shard_map/reduce_scatter | solution.py:760
  685.1 58.2 %collective-permute-start.21 = (bf16[256,2048]{1,0:T(8,128)(2,1)}, bf16[256,2048]{1,0:T(8,128)(2,1)}, u32[]{:S(2)}, u32[]{:S(2)}) collective-permute-start(bf16[256,2048]{1,0:T(8,128)(2,1)} %fusion.26), channel_id=1, source_target_pairs={{0,8},{2,10},{8,16},{10,18},{16,24},{18,26},{24,28},{26,30},{28,20... | collective-permute-start | bytes 3145736 | tf_op jit(solution)/shard_map/ppermute | solution.py:117
  697.2 72.0 %collective-permute-start.30 = (bf16[256,2048]{1,0:T(8,128)(2,1)}, bf16[256,2048]{1,0:T(8,128)(2,1)S(1)}, u32[]{:S(2)}, u32[]{:S(2)}) collective-permute-start(bf16[256,2048]{1,0:T(8,128)(2,1)} %get-tuple-element.206), channel_id=1, source_target_pairs={{0,2},{2,0},{4,6},{6,4},{8,10},{10,8},{12,14},{14,12},{16,18},{18,... | collective-permute-start | bytes 3145736 | tf_op jit(solution)/shard_map/ppermute | solution.py:111
  697.2 72.5 %collective-permute-start.24 = (bf16[256,2048]{1,0:T(8,128)(2,1)}, bf16[256,2048]{1,0:T(8,128)(2,1)S(1)}, u32[]{:S(2)}, u32[]{:S(2)}) collective-permute-start(bf16[256,2048]{1,0:T(8,128)(2,1)} %get-tuple-element.209), channel_id=1, source_target_pairs={{0,2},{2,0},{4,6},{6,4},{8,10},{10,8},{12,14},{14,12},{16,18},{18,... | collective-permute-start | bytes 3145736 | tf_op jit(solution)/shard_map/ppermute | solution.py:111
  746.9 60.9 %collective-permute-start.23 = (bf16[256,2048]{1,0:T(8,128)(2,1)S(1)}, bf16[256,2048]{1,0:T(8,128)(2,1)S(1)}, u32[]{:S(2)}, u32[]{:S(2)}) collective-permute-start(bf16[256,2048]{1,0:T(8,128)(2,1)S(1)} %get-tuple-element.201), channel_id=1, source_target_pairs={{0,8},{2,10},{8,16},{10,18},{16,24},{18,26},{24,28},{26,30},{28,20... | collective-permute-start | bytes 3145736 | tf_op jit(solution)/shard_map/ppermute | solution.py:117
  763.5 44.3 %collective-permute-start.29 = (bf16[256,2048]{1,0:T(8,128)(2,1)S(1)}, bf16[256,2048]{1,0:T(8,128)(2,1)S(1)}, u32[]{:S(2)}, u32[]{:S(2)}) collective-permute-start(bf16[256,2048]{1,0:T(8,128)(2,1)S(1)} %get-tuple-element.202), channel_id=1, source_target_pairs={{8,0},{10,2},{16,8},{18,10},{24,16},{26,18},{28,24},{30,26},{20,28... | collective-permute-start | bytes 3145736 | tf_op jit(solution)/shard_map/ppermute | solution.py:121
  813.1 95.2 %collective-permute-start.34 = (bf16[256,2048]{1,0:T(8,128)(2,1)}, bf16[256,2048]{1,0:T(8,128)(2,1)}, u32[]{:S(2)}, u32[]{:S(2)}) collective-permute-start(bf16[256,2048]{1,0:T(8,128)(2,1)} %get-tuple-element.204), channel_id=1, source_target_pairs={{0,2},{2,0},{4,6},{6,4},{8,10},{10,8},{12,14},{14,12},{16,18},{18,... | collective-permute-start | bytes 3145736 | tf_op jit(solution)/shard_map/ppermute | solution.py:111
  846.6 61.8 %collective-permute-start.27 = (bf16[256,2048]{1,0:T(8,128)(2,1)}, bf16[256,2048]{1,0:T(8,128)(2,1)}, u32[]{:S(2)}, u32[]{:S(2)}) collective-permute-start(bf16[256,2048]{1,0:T(8,128)(2,1)} %get-tuple-element.197), channel_id=1, source_target_pairs={{0,8},{2,10},{8,16},{10,18},{16,24},{18,26},{24,28},{26,30},{28,20... | collective-permute-start | bytes 3145736 | tf_op jit(solution)/shard_map/ppermute | solution.py:117
  1034.6 114.5 %collective-permute-start.38 = (bf16[2,384,2048]{2,1,0:T(8,128)(2,1)}, bf16[2,384,2048]{2,1,0:T(8,128)(2,1)}, u32[]{:S(2)}, u32[]{:S(2)}) collective-permute-start(bf16[2,384,2048]{2,1,0:T(8,128)(2,1)} %get-tuple-element.92), channel_id=1, source_target_pairs={{0,1},{1,0},{2,3},{3,2},{4,5},{5,4},{6,7},{7,6},{8,9},{9,8},{10,11... | collective-permute-start | bytes 9437192 | tf_op jit(solution)/shard_map/ppermute | solution.py:730
  1039.2 45.8 %collective-permute-start.49 = (bf16[128,2560]{1,0:T(8,128)(2,1)}, bf16[128,2560]{1,0:T(8,128)(2,1)}, u32[]{:S(2)}, u32[]{:S(2)}) collective-permute-start(bf16[128,2560]{1,0:T(8,128)(2,1)} %get-tuple-element.216), channel_id=1, source_target_pairs={{8,0},{10,2},{16,8},{18,10},{24,16},{26,18},{28,24},{30,26},{20,28... | collective-permute-start | bytes 1966088 | tf_op jit(solution)/shard_map/ppermute | solution.py:121
  1060.1 50.2 %collective-permute-start.52 = (bf16[128,2560]{1,0:T(8,128)(2,1)S(1)}, bf16[128,2560]{1,0:T(8,128)(2,1)}, u32[]{:S(2)}, u32[]{:S(2)}) collective-permute-start(bf16[128,2560]{1,0:T(8,128)(2,1)S(1)} %copy-done.23), channel_id=1, source_target_pairs={{0,2},{2,0},{4,6},{6,4},{8,10},{10,8},{12,14},{14,12},{16,18},{18,... | collective-permute-start | bytes 1966088 | tf_op jit(solution)/shard_map/ppermute | solution.py:111
  1060.2 52.1 %collective-permute-start.46 = (bf16[128,2560]{1,0:T(8,128)(2,1)S(1)}, bf16[128,2560]{1,0:T(8,128)(2,1)}, u32[]{:S(2)}, u32[]{:S(2)}) collective-permute-start(bf16[128,2560]{1,0:T(8,128)(2,1)S(1)} %get-tuple-element.222), channel_id=1, source_target_pairs={{0,2},{2,0},{4,6},{6,4},{8,10},{10,8},{12,14},{14,12},{16,18},{18,... | collective-permute-start | bytes 1966088 | tf_op jit(solution)/shard_map/ppermute | solution.py:111
  1110.3 71.3 %collective-permute-start.36 = (bf16[2,2048,384]{2,1,0:T(8,128)(2,1)}, bf16[2,2048,384]{2,1,0:T(8,128)(2,1)}, u32[]{:S(2)}, u32[]{:S(2)}) collective-permute-start(bf16[2,2048,384]{2,1,0:T(8,128)(2,1)} %get-tuple-element.88), channel_id=1, source_target_pairs={{0,1},{1,0},{2,3},{3,2},{4,5},{5,4},{6,7},{7,6},{8,9},{9,8},{10,11... | collective-permute-start | bytes 9437192 | tf_op jit(solution)/shard_map/ppermute | solution.py:730
  1112.3 136.7 %collective-permute-start.37 = (bf16[2,2048,384]{2,1,0:T(8,128)(2,1)}, bf16[2,2048,384]{2,1,0:T(8,128)(2,1)}, u32[]{:S(2)}, u32[]{:S(2)}) collective-permute-start(bf16[2,2048,384]{2,1,0:T(8,128)(2,1)} %get-tuple-element.90), channel_id=1, source_target_pairs={{0,1},{1,0},{2,3},{3,2},{4,5},{5,4},{6,7},{7,6},{8,9},{9,8},{10,11... | collective-permute-start | bytes 9437192 | tf_op jit(solution)/shard_map/ppermute | solution.py:730
  1138.3 131.2 %collective-permute-start.39 = (bf16[1,256,2048]{2,1,0:T(8,128)(2,1)}, bf16[1,256,2048]{2,1,0:T(8,128)(2,1)}, u32[]{:S(2)}, u32[]{:S(2)}) collective-permute-start(bf16[1,256,2048]{2,1,0:T(8,128)(2,1)} %fusion.49), channel_id=1, source_target_pairs={{0,1},{1,0},{2,3},{3,2},{4,5},{5,4},{6,7},{7,6},{8,9},{9,8},{10,11... | collective-permute-start | bytes 3145736 | tf_op jit(solution)/shard_map/ppermute | solution.py:769
  (82 other events, 2074.1 us)
Sparse Core Ops, SparseCore 0:
  10.9 90.8 all-gather.4
  103.9 88.9 all-gather.6
  237.9 92.5 all-gather.8
  645.7 237.4 reduce-scatter.2
  1009.6 120.7 reduce-scatter.4

commit v5 on v4

--- a/solution.py
+++ b/solution.py
@@ -91,7 +91,10 @@
         if step < (len(order) + 1) // 2:
             ahead = lax.ppermute(ahead, "fsdp", down)
         if step <= len(between):
-            behind, ahead = between[step - 1]((behind, ahead))
+            behind, ahead, *rest = between[step - 1](
+                (behind, ahead, whole) if step == 1 else (behind, ahead)
+            )
+            whole = rest[0] if rest else whole
         whole = keep(whole, behind, -step)
         if step < (len(order) + 1) // 2:
             whole = keep(whole, ahead, step)
@@ -662,9 +665,9 @@
     plan = plan_places(member, slot, places)
     base = (node * local_experts).reshape(1).astype(jnp.int32)
 
-    normed_rows, router_full, all_routes = lax.optimization_barrier(
-        (normed_rows, router_full, all_routes)
-    )
+    steady = {key: plan[key] for key in ("places", "tiles", "first", "last", "starts")}
+    normed_rows, router_full, steady = lax.optimization_barrier((normed_rows, router_full, steady))
+    plan = {**plan, **steady}
     pre = mm(normed_rows, qkv_full)
     cot_low = cotangent.reshape(tokens, model_width)
     cot_low, pre = lax.optimization_barrier((cot_low, pre))
@@ -711,33 +714,34 @@
     out_total = spread(plan, [produced])[0]
     out_total, back = lax.optimization_barrier((out_total, back))
     grad_total, columns = spread(plan, [back, columns])
+    pairs = columns[:, :, : 2 * local_experts].astype(F32).reshape(nodes, tokens, local_experts, 2)
+    column = jnp.sum(pairs, axis=-1)
+    grad_gate = lax.all_to_all(column, "fsdp", split_axis=0, concat_axis=0, tiled=True)
+    grad_gate = jnp.moveaxis(grad_gate, 0, 1).reshape(tokens, expert_count)
+    weighed, grad_gate = lax.optimization_barrier((weighed, grad_gate))
     own_grads, far_grads = zip(
         weight_grad(plan, arrived, grad_gate_pre, 1, half_hidden),
         weight_grad(plan, arrived, grad_up_pre, 1, half_hidden),
         weight_grad(plan, weighed, cots, 0, half_hidden),
     )
 
-    pairs = columns[:, :, : 2 * local_experts].astype(F32).reshape(nodes, tokens, local_experts, 2)
-    column = jnp.sum(pairs, axis=-1)
-    grad_gate = lax.all_to_all(column, "fsdp", split_axis=0, concat_axis=0, tiled=True)
-    grad_gate = jnp.moveaxis(grad_gate, 0, 1).reshape(tokens, expert_count)
-
-    moved = []
-    for kind in range(3):
+    def send_far(kind):
         axis = 2 if kind < 2 else 1
-        moved.append(
-            [
-                lax.ppermute(
-                    lax.slice_in_dim(
-                        far_grads[kind], (j - 1) * half_hidden, j * half_hidden, axis=axis
-                    ),
-                    "tp",
-                    [(s, (s + j) % tp_size) for s in range(tp_size)],
-                )
-                for j in range(1, tp_size)
-            ]
-        )
+        return [
+            lax.ppermute(
+                lax.slice_in_dim(
+                    far_grads[kind], (j - 1) * half_hidden, j * half_hidden, axis=axis
+                ),
+                "tp",
+                [(s, (s + j) % tp_size) for s in range(tp_size)],
+            )
+            for j in range(1, tp_size)
+        ]
+
+    moved = [send_far(0)]
     grad_rows = ring_scatter(grad_total)
+    grad_rows, far_grads = lax.optimization_barrier((grad_rows, far_grads))
+    moved += [send_far(kind) for kind in (1, 2)]
     expert_part = lax.psum_scatter(out_total, "fsdp", scatter_dimension=0, tiled=True)
     grad_logits = (
         gates * (grad_gate - jnp.sum(gates * grad_gate, axis=-1, keepdims=True))

time: 1330 us -> 1320 us (level)
  waiting for transfers between devices: 567 us -> 623 us
  starting transfers between devices: 116 us -> 81.1 us
  blocking collectives: 57.9 us -> 42.5 us
    ppermute x8, starting transfers between devices: 72.6 us -> 26.5 us  [ring_scatter(): rising = lax.ppermute(rising, 'fsdp', up).astype(F32)]
    ppermute x8, waiting for transfers between devices: 128 us -> 159 us  [ring_scatter(): rising = lax.ppermute(rising, 'fsdp', up).astype(F32)]
    ppermute x3, waiting for transfers between devices: 99.9 us -> 129 us  [send_far(): lax.ppermute(lax.slice_in_dim(far_grads[kind], (j - 1) * half_hidden, j *...]
    all_gather x1, waiting for transfers between devices: 42.1 us -> 26.5 us  [layer(): lax.all_gather(jnp.concatenate([query_weight, key_weight, value_weight],...]
    all_to_all x1 -> x0, blocking collectives: 15.1 us -> none  [layer(): lax.all_to_all(column, 'fsdp', split_axis=0, concat_axis=0, tiled=True)]
    ppermute x6, waiting for transfers between devices: 17.7 us -> 31.3 us  [ring_scatter(): falling = lax.ppermute(falling, 'fsdp', down).astype(F32)]
  transfers between devices with their start and end apart: 62 -> 63, of which waited for: 22 -> 25; matrix products, arithmetic and copies ran while one was open for 14% -> 14% of each run, Pallas kernels for 11% -> 11%
where the time goes in v5:
time: 1320 us; the launch traced here: 1310 us
  waiting for transfers between devices  623 us (47%)
  Pallas kernels  324 us (25%)
  other arithmetic  94.3 us (7%)
  starting transfers between devices  81.1 us (6%)
  local copies, waits for them, and re-layouts  67.6 us (5%)
  matrix products  53 us (4%)
  blocking collectives  42.5 us (3%)
  between operations  29.3 us (2%)
    ppermute x5, waiting for transfers between devices, fetch_next(): lax.ppermute(values, 'tp', [(s, (s - step) % size) for s in range(size)])  167 us
    ppermute x8, waiting for transfers between devices, ring_scatter(): rising = lax.ppermute(rising, 'fsdp', up).astype(F32)  159 us
    ppermute x3, waiting for transfers between devices, send_far(): lax.ppermute(lax.slice_in_dim(far_grads[kind], (j - 1) * half_hidden, j *...  129 us
    pallas_call x1, Pallas kernels, run_experts(): pl.pallas_call(functools.partial(expert_kernel, expert_count=expert_count...  79.4 us
    pallas_call x2, Pallas kernels, pick(): pl.pallas_call(pick_kernel, grid_spec=pltpu.PrefetchScalarGridSpec(num_sc...  70.1 us
    pallas_call x3, Pallas kernels, weight_grad(): pl.pallas_call(functools.partial(weight_kernel, axis=axis, piece=piece, g...  57.8 us
    dot_general x9, matrix products, mm(): return lax.dot_general(a, b, (dims, ((), ())), preferred_element_type=F32)  52.9 us
    pallas_call x2, Pallas kernels, spread(): pl.pallas_call(spread_kernel, grid_spec=pltpu.PrefetchScalarGridSpec(num_...  46.6 us
  transfers between devices with their start and end apart: 63, of which 25 were waited for; matrix products, arithmetic and copies ran while one was open for 14% of the time, Pallas kernels for 11%

profile of v5, /device:TPU:0, one launch (start us, length us, event | category | flops | bytes accessed | tf_op | source)
XLA Modules:
  0.0 1314.6 jit_solution(15091870235889848704)
XLA Ops:
  24.0 23.3 %all_gather.19 = s32[16,256,8]{1,2,0:T(8,128)S(1)} all-gather(s32[1,256,8]{1,2,0:T(8,128)S(1)} %constant_dynamic-slice_fusion.4), channel_id=1, replica_groups=mesh['fsdp'=16,'tp'=2] {'fsdp'}, dimensions={0}, use_global_device_ids=true | all-gather | bytes 139264 | tf_op jit(solution)/shard_map/all_gather | solution.py:658
  76.1 26.5 %all-gather.5.cloned.1.call-done = bf16[2048,2560]{1,0:T(8,128)(2,1)} async-done(((bf16[128,2560]{1,0:T(8,128)(2,1)}), bf16[2048,2560]{1,0:T(8,128)(2,1)}) %all-gather.5.cloned.1.call-update) | async-done | bytes 10485776 | tf_op jit(solution)/shard_map/all_gather | solution.py:620
  117.3 28.7 %attend.1.att_ref = bf16[512,2048]{1,0:T(8,128)(2,1)} custom-call(f32[512,2560]{1,0:T(8,128)} %fusion.68.q_ref.k_ref.v_ref, f32[512,2560]{1,0:T(8,128)} %fusion.68.q_ref.k_ref.v_ref, f32[512,2560]{1,0:T(8,128)} %fusion.68.q_ref.k_ref.v_ref, f32[512,128]{1,0:T(8,128)} %maximum_bitcast_fusion.4.cos_ref, f32[512,128]{1,0:T(8,128)} %maximum_bitcast_fusion.5.sin_ref, ...), custom_call_target="tpu_custom_call" | custom-call | flops 2147483648 | bytes 7864320 | tf_op jit(solution)/shard_map/attend/pallas_call | solution.py:238
  155.7 36.4 %all-gather.7.cloned.1.call-done = bf16[2048,2048]{1,0:T(8,128)(2,1)} async-done(((bf16[128,2048]{1,0:T(8,128)(2,1)}), bf16[2048,2048]{1,0:T(8,128)(2,1)}) %all-gather.7.cloned.1.call-update) | async-done | bytes 8388624 | tf_op jit(solution)/shard_map/all_gather | solution.py:628
  206.9 21.5 %collective-permute-done.4 = bf16[1,256,2048]{2,1,0:T(8,128)(2,1)} collective-permute-done((bf16[1,256,2048]{2,1,0:T(8,128)(2,1)}, bf16[1,256,2048]{2,1,0:T(8,128)(2,1)}, u32[]{:S(2)}, u32[]{:S(2)}) %collective-permute-start.4) | collective-permute-done | bytes 1048608 | tf_op jit(solution)/shard_map/ppermute | solution.py:46
  242.8 64.6 %collective-permute-done.17 = bf16[2,2048,384]{2,1,0:T(8,128)(2,1)} collective-permute-done((bf16[2,2048,384]{2,1,0:T(8,128)(2,1)}, bf16[2,2048,384]{2,1,0:T(8,128)(2,1)}, u32[]{:S(2)}, u32[]{:S(2)}) %collective-permute-start.17) | collective-permute-done | bytes 3145760 | tf_op jit(solution)/shard_map/ppermute | solution.py:34
  313.6 59.5 %collective-permute-done.18 = bf16[2,2048,384]{2,1,0:T(8,128)(2,1)S(1)} collective-permute-done((bf16[2,2048,384]{2,1,0:T(8,128)(2,1)}, bf16[2,2048,384]{2,1,0:T(8,128)(2,1)S(1)}, u32[]{:S(2)}, u32[]{:S(2)}) %collective-permute-start.18) | collective-permute-done | bytes 3145760 | tf_op jit(solution)/shard_map/ppermute | solution.py:34
  410.2 19.9 %collective-permute-done.15 = bf16[256,2048]{1,0:T(8,128)(2,1)S(1)} collective-permute-done((bf16[256,2048]{1,0:T(8,128)(2,1)S(1)}, bf16[256,2048]{1,0:T(8,128)(2,1)S(1)}, u32[]{:S(2)}, u32[]{:S(2)}) %collective-permute-start.15) | collective-permute-done | bytes 1048608 | tf_op jit(solution)/shard_map/ppermute | solution.py:90
  434.4 19.3 %collective-permute-done.19 = bf16[2,384,2048]{2,1,0:T(8,128)(2,1)S(1)} collective-permute-done((bf16[2,384,2048]{2,1,0:T(8,128)(2,1)S(1)}, bf16[2,384,2048]{2,1,0:T(8,128)(2,1)S(1)}, u32[]{:S(2)}, u32[]{:S(2)}) %collective-permute-start.19) | collective-permute-done | bytes 3145760 | tf_op jit(solution)/shard_map/ppermute | solution.py:34
  458.7 33.9 %pick.3.cots_ref.right_ref = bf16[2,2560,2048]{2,1,0:T(8,128)(2,1)} custom-call(s32[2]{0:T(128)} %and_select_fusion.1.tiles, s32[20]{0:T(128)} %min.28.first, s32[20]{0:T(128)} %min.30.last, s32[2,16,1,256]{3,2,1,0:T(1,128)} %broadcast_in_dim.134.places_ref, bf16[16,256,2048]{2,1,0:T(8,128)(2,1)} %bitcast_dynamic-update-slice_fusion.refs_0_), custom_call_target="tpu_custom_call" | custom-call | flops 16106127360 | bytes 37748736 | tf_op jit(solution)/shard_map/pick/pallas_call | solution.py:342
  492.6 36.1 %pick.2 = (bf16[2,2560,2048]{2,1,0:T(8,128)(2,1)}, bf16[2,2560,128]{2,1,0:T(8,128)(2,1)}) custom-call(s32[2]{0:T(128)} %and_select_fusion.1.tiles, s32[20]{0:T(128)} %min.28.first, s32[20]{0:T(128)} %min.30.last, s32[2,16,1,256]{3,2,1,0:T(1,128)} %broadcast_in_dim.134.places_ref, bf16[16,256,2176]{2,1,0:T(8,128)(2,1)} %bitcast.264, ...), custom_call_target="tpu_custom_call" | custom-call | flops 16106127360 | bytes 37748736 | tf_op jit(solution)/shard_map/pick/pallas_call | solution.py:342
  528.7 79.4 %run_experts.1 = (bf16[2,2560,768]{2,1,0:T(8,128)(2,1)}, bf16[2,2560,768]{2,1,0:T(8,128)(2,1)}, bf16[2,2560,768]{2,1,0:T(8,128)(2,1)}, bf16[2,2560,2048]{2,1,0:T...) custom-call(s32[2]{0:T(128)} %and_select_fusion.1.tiles, s32[1]{0:T(128)} %bitcast.19.base, ...), custom_call_target="tpu_custom_call" | custom-call | flops 48318382080 | bytes 107479040 | tf_op jit(solution)/shard_map/run_experts/pallas_call | solution.py:487
  608.1 22.4 %spread.2 = bf16[16,256,2048]{2,1,0:T(8,128)(2,1)} custom-call(s32[32]{0:T(128)} %reshape.779.starts, s32[2,16,1,256]{3,2,1,0:T(1,128)} %broadcast_in_dim.134.places_ref, bf16[2,2560,2048]{2,1,0:T(8,128)(2,1)} %get-tuple-element.94.refs_0_), custom_call_target="tpu_custom_call" | custom-call | flops 5905580032 | bytes 41943040 | tf_op jit(solution)/shard_map/spread/pallas_call | solution.py:530
  631.8 24.2 %spread.3 = (bf16[16,256,2048]{2,1,0:T(8,128)(2,1)}, bf16[16,256,128]{2,1,0:T(8,128)(2,1)}) custom-call(s32[32]{0:T(128)} %reshape.779.starts, s32[2,16,1,256]{3,2,1,0:T(1,128)} %broadcast_in_dim.134.places_ref, bf16[2,2560,2048]{2,1,0:T(8,128)(2,1)} %get-tuple-element.96.refs_0_, bf16[2,2560,128]{2,1,0:T(8,128)(2,1)} %get-tuple-element.97.refs_1_), custom_call_target="tpu_custom_call" | custom-call | flops 6274678784 | bytes 44564480 | tf_op jit(solution)/shard_map/spread/pallas_call | solution.py:530
  671.1 45.5 %collective-permute-done.21 = bf16[256,2048]{1,0:T(8,128)(2,1)} collective-permute-done((bf16[256,2048]{1,0:T(8,128)(2,1)}, bf16[256,2048]{1,0:T(8,128)(2,1)}, u32[]{:S(2)}, u32[]{:S(2)}) %collective-permute-start.21) | collective-permute-done | bytes 1048608 | tf_op jit(solution)/shard_map/ppermute | solution.py:120
  757.8 24.9 %collective-permute-done.23 = bf16[256,2048]{1,0:T(8,128)(2,1)} collective-permute-done((bf16[256,2048]{1,0:T(8,128)(2,1)}, bf16[256,2048]{1,0:T(8,128)(2,1)}, u32[]{:S(2)}, u32[]{:S(2)}) %collective-permute-start.23) | collective-permute-done | bytes 1048608 | tf_op jit(solution)/shard_map/ppermute | solution.py:120
  810.7 19.3 %weight_grad.3 = (f32[2,2048,384]{2,1,0:T(8,128)}, bf16[2,2048,384]{2,1,0:T(8,128)(2,1)}) custom-call(s32[2]{0:T(128)} %and_select_fusion.1.tiles, bf16[2,2560,2048]{2,1,0:T(8,128)(2,1)} %get-tuple-element.86.arrived_ref.left_ref, bf16[2,2560,768]{2,1,0:T(8,128)(2,1)} %get-tuple-element.99.right_ref), custom_call_target="tpu_custom_call" | custom-call | flops 8053063680 | bytes 33292288 | tf_op jit(solution)/shard_map/weight_grad/pallas_call | solution.py:401
  856.9 25.6 %collective-permute-done.27 = bf16[256,2048]{1,0:T(8,128)(2,1)} collective-permute-done((bf16[256,2048]{1,0:T(8,128)(2,1)}, bf16[256,2048]{1,0:T(8,128)(2,1)}, u32[]{:S(2)}, u32[]{:S(2)}) %collective-permute-start.27) | collective-permute-done | bytes 1048608 | tf_op jit(solution)/shard_map/ppermute | solution.py:120
  891.0 23.7 %collective-permute-done.35 = bf16[1,256,2048]{2,1,0:T(8,128)(2,1)S(1)} collective-permute-done((bf16[1,256,2048]{2,1,0:T(8,128)(2,1)S(1)}, bf16[1,256,2048]{2,1,0:T(8,128)(2,1)S(1)}, u32[]{:S(2)}, u32[]{:S(2)}) %collective-permute-start.35) | collective-permute-done | bytes 1048608 | tf_op jit(solution)/shard_map/ppermute | solution.py:34
  932.0 41.1 %attend_back.1 = (bf16[512,2560]{1,0:T(8,128)(2,1)}, f32[1,128]{1,0:T(1,128)}, f32[1,128]{1,0:T(1,128)}) custom-call(f32[512,2560]{1,0:T(8,128)} %fusion.68.q_ref.k_ref.v_ref, f32[512,2560]{1,0:T(8,128)} %fusion.68.q_ref.k_ref.v_ref, f32[512,2560]{1,0:T(8,128)} %fusion.68.q_ref.k_ref.v_ref, f32[512,128]{1,0:T(8,128)} %maximum_bitcast_fusion.4.cos_ref, ...), custom_call_target="tpu_custom_call" | custom-call | flops 5368709120 | bytes 13107200 | tf_op jit(solution)/shard_map/attend_back/pallas_call | solution.py:266
  1012.4 19.6 %collective-permute-done.43 = bf16[128,2560]{1,0:T(8,128)(2,1)S(1)} collective-permute-done((bf16[128,2560]{1,0:T(8,128)(2,1)S(1)}, bf16[128,2560]{1,0:T(8,128)(2,1)S(1)}, u32[]{:S(2)}, u32[]{:S(2)}) %collective-permute-start.43) | collective-permute-done | bytes 655392 | tf_op jit(solution)/shard_map/ppermute | solution.py:120
  1049.9 20.9 %collective-permute-done.45 = bf16[128,2560]{1,0:T(8,128)(2,1)} collective-permute-done((bf16[128,2560]{1,0:T(8,128)(2,1)}, bf16[128,2560]{1,0:T(8,128)(2,1)}, u32[]{:S(2)}, u32[]{:S(2)}) %collective-permute-start.45) | collective-permute-done | bytes 655392 | tf_op jit(solution)/shard_map/ppermute | solution.py:120
  1123.0 61.8 %collective-permute-done.37 = bf16[2,2048,384]{2,1,0:T(8,128)(2,1)} collective-permute-done((bf16[2,2048,384]{2,1,0:T(8,128)(2,1)}, bf16[2,2048,384]{2,1,0:T(8,128)(2,1)}, u32[]{:S(2)}, u32[]{:S(2)}) %collective-permute-start.37) | collective-permute-done | bytes 3145760 | tf_op jit(solution)/shard_map/ppermute | solution.py:731
  1184.8 66.9 %collective-permute-done.38 = bf16[2,384,2048]{2,1,0:T(8,128)(2,1)} collective-permute-done((bf16[2,384,2048]{2,1,0:T(8,128)(2,1)}, bf16[2,384,2048]{2,1,0:T(8,128)(2,1)}, u32[]{:S(2)}, u32[]{:S(2)}) %collective-permute-start.38) | collective-permute-done | bytes 3145760 | tf_op jit(solution)/shard_map/ppermute | solution.py:731
  (352 shorter events, 440.3 us)
Async XLA Ops:
  7.2 95.3 %all-gather.5.cloned.1.call-start = ((), (), s32[]{:S(2)}) async-start(), calls=%async_computation.4 | async-start | bytes 11141120 | tf_op jit(solution)/shard_map/all_gather | solution.py:620
  9.4 182.7 %all-gather.7.cloned.1.call-start = ((), (), s32[]{:S(2)}) async-start(), calls=%async_computation.5 | async-start | bytes 8912896 | tf_op jit(solution)/shard_map/all_gather | solution.py:628
  10.1 482.4 %all-gather.9.cloned.1.call-start = ((), (), s32[]{:S(2)}) async-start(), calls=%async_computation.8 | async-start | bytes 18939904 | tf_op jit(solution)/shard_map/all_gather | solution.py:707
  11.1 62.2 %collective-permute-start = (bf16[1,256,2048]{2,1,0:T(8,128)(2,1)S(1)}, bf16[1,256,2048]{2,1,0:T(8,128)(2,1)}, u32[]{:S(2)}, u32[]{:S(2)}) collective-permute-start(bf16[1,256,2048]{2,1,0:T(8,128)(2,1)S(1)} %fusion.4), channel_id=1, source_target_pairs={{0,1},{1,0},{2,3},{3,2},{4,5},{5,4},{6,7},{7,6},{8,9},{9,8},{10,11... | collective-permute-start | bytes 3145736 | tf_op jit(solution)/shard_map/ppermute | solution.py:34
  236.0 696.0 %reduce-scatter.3.cloned.1.call-start = ((), (), s32[]{:S(2)}) async-start(), calls=%async_computation.6 | async-start | bytes 17825792 | tf_op jit(solution)/shard_map/reduce_scatter | solution.py:745
  236.0 71.4 %collective-permute-start.17 = (bf16[2,2048,384]{2,1,0:T(8,128)(2,1)}, bf16[2,2048,384]{2,1,0:T(8,128)(2,1)}, u32[]{:S(2)}, u32[]{:S(2)}) collective-permute-start(bf16[2,2048,384]{2,1,0:T(8,128)(2,1)} %param.122), channel_id=1, source_target_pairs={{0,1},{1,0},{2,3},{3,2},{4,5},{5,4},{6,7},{7,6},{8,9},{9,8},{10,11... | collective-permute-start | bytes 9437192 | tf_op jit(solution)/shard_map/ppermute | solution.py:34
  237.5 135.6 %collective-permute-start.18 = (bf16[2,2048,384]{2,1,0:T(8,128)(2,1)}, bf16[2,2048,384]{2,1,0:T(8,128)(2,1)S(1)}, u32[]{:S(2)}, u32[]{:S(2)}) collective-permute-start(bf16[2,2048,384]{2,1,0:T(8,128)(2,1)} %param.123), channel_id=1, source_target_pairs={{0,1},{1,0},{2,3},{3,2},{4,5},{5,4},{6,7},{7,6},{8,9},{9,8},{10,11... | collective-permute-start | bytes 9437192 | tf_op jit(solution)/shard_map/ppermute | solution.py:34
  242.7 137.7 %collective-permute-start.7 = (bf16[256,2048]{1,0:T(8,128)(2,1)}, bf16[256,2048]{1,0:T(8,128)(2,1)S(1)}, u32[]{:S(2)}, u32[]{:S(2)}) collective-permute-start(bf16[256,2048]{1,0:T(8,128)(2,1)} %collective-permute-done.1), channel_id=1, source_target_pairs={{0,2},{2,0},{4,6},{6,4},{8,10},{10,8},{12,14},{14,12},{16,18},{18,... | collective-permute-start | bytes 3145736 | tf_op jit(solution)/shard_map/ppermute | solution.py:82
  383.6 70.2 %collective-permute-start.19 = (bf16[2,384,2048]{2,1,0:T(8,128)(2,1)S(1)}, bf16[2,384,2048]{2,1,0:T(8,128)(2,1)S(1)}, u32[]{:S(2)}, u32[]{:S(2)}) collective-permute-start(bf16[2,384,2048]{2,1,0:T(8,128)(2,1)S(1)} %copy-done.18), channel_id=1, source_target_pairs={{0,1},{1,0},{2,3},{3,2},{4,5},{5,4},{6,7},{7,6},{8,9},{9,8},{10,11... | collective-permute-start | bytes 9437192 | tf_op jit(solution)/shard_map/ppermute | solution.py:34
  669.3 47.4 %collective-permute-start.21 = (bf16[256,2048]{1,0:T(8,128)(2,1)}, bf16[256,2048]{1,0:T(8,128)(2,1)}, u32[]{:S(2)}, u32[]{:S(2)}) collective-permute-start(bf16[256,2048]{1,0:T(8,128)(2,1)} %fusion.25), channel_id=1, source_target_pairs={{0,8},{2,10},{8,16},{10,18},{16,24},{18,26},{24,28},{26,30},{28,20... | collective-permute-start | bytes 3145736 | tf_op jit(solution)/shard_map/ppermute | solution.py:120
  670.5 87.1 %collective-permute-start.24 = (bf16[256,2048]{1,0:T(8,128)(2,1)}, bf16[256,2048]{1,0:T(8,128)(2,1)}, u32[]{:S(2)}, u32[]{:S(2)}) collective-permute-start(bf16[256,2048]{1,0:T(8,128)(2,1)} %get-tuple-element.230), channel_id=1, source_target_pairs={{0,2},{2,0},{4,6},{6,4},{8,10},{10,8},{12,14},{14,12},{16,18},{18,... | collective-permute-start | bytes 3145736 | tf_op jit(solution)/shard_map/ppermute | solution.py:114
  670.5 87.2 %collective-permute-start.30 = (bf16[256,2048]{1,0:T(8,128)(2,1)}, bf16[256,2048]{1,0:T(8,128)(2,1)}, u32[]{:S(2)}, u32[]{:S(2)}) collective-permute-start(bf16[256,2048]{1,0:T(8,128)(2,1)} %get-tuple-element.227), channel_id=1, source_target_pairs={{0,2},{2,0},{4,6},{6,4},{8,10},{10,8},{12,14},{14,12},{16,18},{18,... | collective-permute-start | bytes 3145736 | tf_op jit(solution)/shard_map/ppermute | solution.py:114
  721.6 61.2 %collective-permute-start.23 = (bf16[256,2048]{1,0:T(8,128)(2,1)}, bf16[256,2048]{1,0:T(8,128)(2,1)}, u32[]{:S(2)}, u32[]{:S(2)}) collective-permute-start(bf16[256,2048]{1,0:T(8,128)(2,1)} %get-tuple-element.222), channel_id=1, source_target_pairs={{0,8},{2,10},{8,16},{10,18},{16,24},{18,26},{24,28},{26,30},{28,20... | collective-permute-start | bytes 3145736 | tf_op jit(solution)/shard_map/ppermute | solution.py:120
  746.4 83.6 %all-to-all-start = ((f32[16,256,2]{1,2,0:T(2,128)}), f32[16,256,2]{1,2,0:T(2,128)S(1)}, u32[]{:S(2)}, u32[]{:S(2)}) async-start(f32[16,256,2]{1,2,0:T(2,128)} %copy.216), calls=%async_computation | async-start | bytes 65536 | tf_op jit(solution)/shard_map/all_to_all | solution.py:719
  757.2 548.6 %reduce-scatter.5.cloned.1.call-start = ((), (), s32[]{:S(2)}) async-start(), calls=%async_computation.7 | async-start | bytes 8912896 | tf_op jit(solution)/shard_map/reduce_scatter | solution.py:764
  757.2 72.9 %collective-permute-start.26 = (bf16[256,2048]{1,0:T(8,128)(2,1)}, bf16[256,2048]{1,0:T(8,128)(2,1)S(1)}, u32[]{:S(2)}, u32[]{:S(2)}) collective-permute-start(bf16[256,2048]{1,0:T(8,128)(2,1)} %get-tuple-element.229), channel_id=1, source_target_pairs={{0,2},{2,0},{4,6},{6,4},{8,10},{10,8},{12,14},{14,12},{16,18},{18,... | collective-permute-start | bytes 3145736 | tf_op jit(solution)/shard_map/ppermute | solution.py:114
  757.7 72.5 %collective-permute-start.32 = (bf16[256,2048]{1,0:T(8,128)(2,1)}, bf16[256,2048]{1,0:T(8,128)(2,1)}, u32[]{:S(2)}, u32[]{:S(2)}) collective-permute-start(bf16[256,2048]{1,0:T(8,128)(2,1)} %get-tuple-element.226), channel_id=1, source_target_pairs={{0,2},{2,0},{4,6},{6,4},{8,10},{10,8},{12,14},{14,12},{16,18},{18,... | collective-permute-start | bytes 3145736 | tf_op jit(solution)/shard_map/ppermute | solution.py:114
  810.7 46.1 %collective-permute-start.34 = (bf16[256,2048]{1,0:T(8,128)(2,1)S(1)}, bf16[256,2048]{1,0:T(8,128)(2,1)}, u32[]{:S(2)}, u32[]{:S(2)}) collective-permute-start(bf16[256,2048]{1,0:T(8,128)(2,1)S(1)} %get-tuple-element.225), channel_id=1, source_target_pairs={{0,2},{2,0},{4,6},{6,4},{8,10},{10,8},{12,14},{14,12},{16,18},{18,... | collective-permute-start | bytes 3145736 | tf_op jit(solution)/shard_map/ppermute | solution.py:114
  835.3 47.1 %collective-permute-start.27 = (bf16[256,2048]{1,0:T(8,128)(2,1)}, bf16[256,2048]{1,0:T(8,128)(2,1)}, u32[]{:S(2)}, u32[]{:S(2)}) collective-permute-start(bf16[256,2048]{1,0:T(8,128)(2,1)} %get-tuple-element.218), channel_id=1, source_target_pairs={{0,8},{2,10},{8,16},{10,18},{16,24},{18,26},{24,28},{26,30},{28,20... | collective-permute-start | bytes 3145736 | tf_op jit(solution)/shard_map/ppermute | solution.py:120
  836.8 47.7 %collective-permute-start.33 = (bf16[256,2048]{1,0:T(8,128)(2,1)}, bf16[256,2048]{1,0:T(8,128)(2,1)}, u32[]{:S(2)}, u32[]{:S(2)}) collective-permute-start(bf16[256,2048]{1,0:T(8,128)(2,1)} %get-tuple-element.219), channel_id=1, source_target_pairs={{8,0},{10,2},{16,8},{18,10},{24,16},{26,18},{28,24},{30,26},{20,28... | collective-permute-start | bytes 3145736 | tf_op jit(solution)/shard_map/ppermute | solution.py:124
  1046.1 76.9 %collective-permute-start.36 = (bf16[2,2048,384]{2,1,0:T(8,128)(2,1)}, bf16[2,2048,384]{2,1,0:T(8,128)(2,1)}, u32[]{:S(2)}, u32[]{:S(2)}) collective-permute-start(bf16[2,2048,384]{2,1,0:T(8,128)(2,1)} %get-tuple-element.100), channel_id=1, source_target_pairs={{0,1},{1,0},{2,3},{3,2},{4,5},{5,4},{6,7},{7,6},{8,9},{9,8},{10,11... | collective-permute-start | bytes 9437192 | tf_op jit(solution)/shard_map/ppermute | solution.py:731
  1047.8 136.9 %collective-permute-start.37 = (bf16[2,2048,384]{2,1,0:T(8,128)(2,1)}, bf16[2,2048,384]{2,1,0:T(8,128)(2,1)}, u32[]{:S(2)}, u32[]{:S(2)}) collective-permute-start(bf16[2,2048,384]{2,1,0:T(8,128)(2,1)} %get-tuple-element.113), channel_id=1, source_target_pairs={{0,1},{1,0},{2,3},{3,2},{4,5},{5,4},{6,7},{7,6},{8,9},{9,8},{10,11... | collective-permute-start | bytes 9437192 | tf_op jit(solution)/shard_map/ppermute | solution.py:731
  1048.1 203.6 %collective-permute-start.38 = (bf16[2,384,2048]{2,1,0:T(8,128)(2,1)}, bf16[2,384,2048]{2,1,0:T(8,128)(2,1)}, u32[]{:S(2)}, u32[]{:S(2)}) collective-permute-start(bf16[2,384,2048]{2,1,0:T(8,128)(2,1)} %get-tuple-element.114), channel_id=1, source_target_pairs={{0,1},{1,0},{2,3},{3,2},{4,5},{5,4},{6,7},{7,6},{8,9},{9,8},{10,11... | collective-permute-start | bytes 9437192 | tf_op jit(solution)/shard_map/ppermute | solution.py:731
  1098.0 164.9 %collective-permute-start.39 = (bf16[1,256,2048]{2,1,0:T(8,128)(2,1)}, bf16[1,256,2048]{2,1,0:T(8,128)(2,1)}, u32[]{:S(2)}, u32[]{:S(2)}) collective-permute-start(bf16[1,256,2048]{2,1,0:T(8,128)(2,1)} %fusion.48), channel_id=1, source_target_pairs={{0,1},{1,0},{2,3},{3,2},{4,5},{5,4},{6,7},{7,6},{8,9},{9,8},{10,11... | collective-permute-start | bytes 3145736 | tf_op jit(solution)/shard_map/ppermute | solution.py:773
  (89 other events, 2315.0 us)
Sparse Core Ops, SparseCore 0:
  10.9 91.6 all-gather.4
  104.7 87.3 all-gather.6
  236.1 92.5 all-gather.8
  630.6 252.7 reduce-scatter.2
  987.4 132.5 reduce-scatter.4
